TPU v7x, 32 devices: a whole 2x2x4 slice. The times are simulated.
32 devices in a mesh: expert: 2 (over x), context: 4 (over y, core), dp: 4 (over z).
Axes of the slice: x: 2, y: 2, z: 4, core: 2. Of those that a mesh axis runs over, the one named last changes fastest.
Arguments:
- hidden: bfloat16 [8, 1024, 1536], P(('expert', 'dp'), 'context'), may hold values from -6 to 6
- cotangent: bfloat16 [8, 1024, 1536], P(('expert', 'dp'), 'context'), may hold values from -6 to 6
- token_order: int32 [8, 1024], P(('expert', 'dp')), may hold values from 0 to 1023, each once within a row
- lengths: int32 [8, 3], P(('expert', 'dp')), may hold values from 1 to 512, 1024 in all within a row
- routes: int32 [8, 1024, 4], P(('expert', 'dp'), 'context'), may hold values from 0 to 7, all different within a row; in each aligned block of 256 rows (0 to 255, 256 to 511, ..., all dimensions but the last counted through in order) at most 144 rows name the same one
- attn_gain: bfloat16 [1536], P(('context', 'dp')), may hold values from 0.5 to 1.5
- w_query: bfloat16 [1536, 1536], P(('context', 'dp')), may hold values from -0.15625 to 0.15625
- key_weight: bfloat16 [1536, 512], P(('context', 'dp')), may hold values from -0.15625 to 0.15625
- value_weight: bfloat16 [1536, 512], P(('context', 'dp')), may hold values from -0.15625 to 0.15625
- w_out: bfloat16 [1536, 1536], P(('context', 'dp')), may hold values from -1.25 to 1.25
- ffn_gain: bfloat16 [1536], P(('context', 'dp')), may hold values from 0.5 to 1.5
- w_router: bfloat16 [1536, 8], P(('context', 'dp')), may hold values from -0.078125 to 0.078125
- w_gate: bfloat16 [8, 1536, 512], P(('expert', 'context')), may hold values from -0.15625 to 0.15625
- w_up: bfloat16 [8, 1536, 512], P(('expert', 'context')), may hold values from -0.15625 to 0.15625
- w_down: bfloat16 [8, 512, 1536], P(('expert', 'context')), may hold values from -1 to 1
Outputs:
- output: bfloat16 [8, 1024, 1536], P(('expert', 'dp'), 'context')
- grad_hidden: bfloat16 [8, 1024, 1536], P(('expert', 'dp'), 'context')
- grad_attn_gain: float32 [1536], P(('context', 'dp'))
- grad_query: float32 [1536, 1536], P(('context', 'dp'))
- grad_key: float32 [1536, 512], P(('context', 'dp'))
- grad_value: float32 [1536, 512], P(('context', 'dp'))
- grad_out: float32 [1536, 1536], P(('context', 'dp'))
- grad_ffn_gain: float32 [1536], P(('context', 'dp'))
- grad_router: float32 [1536, 8], P(('context', 'dp'))
- grad_gate: float32 [8, 1536, 512], P(('expert', 'context'), 'dp')
- grad_up: float32 [8, 1536, 512], P(('expert', 'context'), 'dp')
- grad_down: float32 [8, 512, 1536], P(('expert', 'context'), None, 'dp')
Inputs may be any that keep to these rules, and one draw needn't show every extreme that they name: `token_order`: each row names every place of its group once. `lengths`: each row sums to 1024; its largest length is exactly 512. `routes`: a token names 4 different experts; in the rows of one device no expert is named more than 144 times, a bound that some block reaches.
All inputs are finite; a program needn't handle non-finite values.
Results may differ from a plain program's by a relative error of at most 0.025.
Values may be sent and summed in bfloat16 or wider, within the bound.
No kernel may reach another device: no remote copies, remote signals or barrier semaphores. Data moves between devices by JAX's collectives and lax.ppermute only.
A program may use at most 192 MiB of HBM per device.

v0:
```python
import jax
import jax.numpy as jnp
from jax import lax
from jax.sharding import PartitionSpec as P

MODEL_WIDTH = 1536
QUERY_HEADS = 24
KEY_VALUE_HEADS = 8
HEAD_SIZE = 64
NSEQ = 3


norm_eps = 1e-06
rope_base = 10000.0
masked_score = -1e30


def rms_norm(values, gain_vec):
    inv_rms = lax.rsqrt(jnp.mean(values * values, axis=-1, keepdims=True) + norm_eps)
    return values * inv_rms * gain_vec


def angles(token_positions):
    half_dim = HEAD_SIZE // 2
    frequency = rope_base ** (-(jnp.arange(half_dim, dtype=jnp.float32) * 2.0 / HEAD_SIZE))
    turned = token_positions.astype(jnp.float32)[:, None] * frequency[None, :]
    return (jnp.cos(turned), jnp.sin(turned))


def rotate(values, cosine_table, sine_table):
    half_dim = HEAD_SIZE // 2
    front_half = values[..., :half_dim]
    back_half = values[..., half_dim:]
    cos_rows = cosine_table[:, None, :]
    sin_rows = sine_table[:, None, :]
    return jnp.concatenate(
        [
            front_half * cos_rows - back_half * sin_rows,
            back_half * cos_rows + front_half * sin_rows,
        ],
        axis=-1,
    )


def group_info(token_positions, seq_lengths):
    seq_ends = jnp.cumsum(seq_lengths)
    seq_starts = seq_ends - seq_lengths
    document_rows = jnp.sum(
        (token_positions[:, None] >= seq_ends[None, :]).astype(jnp.int32), axis=1
    )
    picked = document_rows[:, None] == jnp.arange(NSEQ, dtype=jnp.int32)[None, :]
    offset = jnp.sum(jnp.where(picked, seq_starts[None, :], 0), axis=1)
    return (document_rows, token_positions - offset)


def dispatch_index(route_rows, expert_count, capacity):
    flat_ids = route_rows.reshape(-1)
    pair_count = flat_ids.shape[0]
    one_hot = (flat_ids[:, None] == jnp.arange(expert_count, dtype=jnp.int32)[None, :]).astype(
        jnp.int32
    )
    before = jnp.cumsum(one_hot, axis=0) - one_hot
    slot_ids = jnp.sum(before * one_hot, axis=1)
    placed = flat_ids * capacity + slot_ids
    source = (
        jnp.full((expert_count * capacity,), pair_count, jnp.int32)
        .at[placed]
        .set(jnp.arange(pair_count, dtype=jnp.int32))
    )
    return (source, placed)


def body(
    hidden,
    cotangent,
    token_order,
    lengths,
    routes,
    attn_gain,
    w_query,
    key_weight,
    value_weight,
    w_out,
    ffn_gain,
    w_router,
    w_gate,
    w_up,
    w_down,
):
    tokens_per_device = hidden.shape[1]
    top_count = routes.shape[2]
    expert_count = lax.axis_size(("expert", "context"))
    capacity = 9 * tokens_per_device * top_count // (8 * expert_count)
    key_value_width = KEY_VALUE_HEADS * HEAD_SIZE
    q_width = QUERY_HEADS * HEAD_SIZE
    group_width = QUERY_HEADS // KEY_VALUE_HEADS
    gain_one, wq_full, wk_full, wv_full, wo_full, gain_two, wr_full = (
        lax.all_gather(attn_gain, ("context", "dp"), axis=0, tiled=True),
        lax.all_gather(w_query, ("context", "dp"), axis=0, tiled=True),
        lax.all_gather(key_weight, ("context", "dp"), axis=0, tiled=True),
        lax.all_gather(value_weight, ("context", "dp"), axis=0, tiled=True),
        lax.all_gather(w_out, ("context", "dp"), axis=0, tiled=True),
        lax.all_gather(ffn_gain, ("context", "dp"), axis=0, tiled=True),
        lax.all_gather(w_router, ("context", "dp"), axis=0, tiled=True),
    )
    order_row = token_order[0]
    document_rows, rel_places = group_info(order_row, lengths[0])
    cycle_pos = lax.axis_index("context")
    local_doc = lax.dynamic_slice_in_dim(
        document_rows, cycle_pos * tokens_per_device, tokens_per_device
    )
    local_place = lax.dynamic_slice_in_dim(
        order_row, cycle_pos * tokens_per_device, tokens_per_device
    )
    local_rel = lax.dynamic_slice_in_dim(
        rel_places, cycle_pos * tokens_per_device, tokens_per_device
    )
    allowed = (local_doc[:, None] == document_rows[None, :]) & (
        order_row[None, :] <= local_place[:, None]
    )
    inputs = hidden[0].astype(jnp.float32)
    gain_a = gain_one.astype(jnp.float32)
    normed_low = rms_norm(inputs, gain_a).astype(jnp.bfloat16)
    cosine_table, sine_table = angles(local_rel)

    def turn_queries(values):
        return rotate(values, cosine_table, sine_table) * HEAD_SIZE ** (-0.5)

    def turn_keys(values):
        return rotate(values, cosine_table, sine_table)

    q_proj = jnp.dot(normed_low, wq_full, preferred_element_type=jnp.float32).reshape(
        tokens_per_device, QUERY_HEADS, HEAD_SIZE
    )
    key_projected = jnp.dot(normed_low, wk_full, preferred_element_type=jnp.float32).reshape(
        tokens_per_device, KEY_VALUE_HEADS, HEAD_SIZE
    )
    v_proj = jnp.dot(normed_low, wv_full, preferred_element_type=jnp.float32)
    query_rows = turn_queries(q_proj).astype(jnp.bfloat16)
    key_matrix_rows = turn_keys(key_projected).astype(jnp.bfloat16)
    local_kv = jnp.concatenate(
        [key_matrix_rows.reshape(tokens_per_device, key_value_width), v_proj.astype(jnp.bfloat16)],
        axis=1,
    )
    every_key_value = lax.all_gather(local_kv, "context", axis=0, tiled=True)
    key_window = every_key_value.shape[0]
    key_head_rows = (
        every_key_value[:, :key_value_width]
        .reshape(key_window, KEY_VALUE_HEADS, HEAD_SIZE)
        .transpose(1, 0, 2)
    )
    value_head_rows = (
        every_key_value[:, key_value_width:]
        .reshape(key_window, KEY_VALUE_HEADS, HEAD_SIZE)
        .transpose(1, 0, 2)
    )
    query_head_rows = query_rows.reshape(
        tokens_per_device, KEY_VALUE_HEADS, group_width, HEAD_SIZE
    ).transpose(1, 2, 0, 3)

    def head_forward(packed):
        head_q, head_k, head_v = packed
        scores = jnp.einsum("gtd,nd->gtn", head_q, head_k, preferred_element_type=jnp.float32)
        masked = jnp.where(allowed[None], scores, masked_score)
        top_score = jnp.max(masked, axis=-1, keepdims=True)
        weights_exp = jnp.exp(masked - top_score)
        row_total = jnp.sum(weights_exp, axis=-1, keepdims=True)
        prob_low = (weights_exp / row_total).astype(jnp.bfloat16)
        mixed_rows = jnp.einsum("gtn,nd->gtd", prob_low, head_v, preferred_element_type=jnp.float32)
        return (mixed_rows, top_score + jnp.log(row_total))

    mixed_heads, log_total = lax.map(
        head_forward, (query_head_rows, key_head_rows, value_head_rows)
    )
    attn_low = (
        mixed_heads.transpose(2, 0, 1, 3).reshape(tokens_per_device, q_width).astype(jnp.bfloat16)
    )
    branch = jnp.dot(attn_low, wo_full, preferred_element_type=jnp.float32)
    middle = inputs + branch
    gain_b = gain_two.astype(jnp.float32)
    ffn_low = rms_norm(middle, gain_b).astype(jnp.bfloat16)
    logits = jnp.dot(ffn_low, wr_full, preferred_element_type=jnp.float32)
    route_rows = routes[0]
    gate_probs = jax.nn.softmax(jnp.take_along_axis(logits, route_rows, axis=1), axis=-1)
    source, placed = dispatch_index(route_rows, expert_count, capacity)
    padded = jnp.concatenate([ffn_low, jnp.zeros((1, MODEL_WIDTH), jnp.bfloat16)], axis=0)
    send_rows = padded[source // top_count].reshape(expert_count, capacity, MODEL_WIDTH)
    expert_in = lax.all_to_all(
        send_rows, ("expert", "context"), split_axis=0, concat_axis=0, tiled=True
    ).reshape(expert_count * capacity, MODEL_WIDTH)
    gate_w = w_gate[0]
    up_w = w_up[0]
    down_w = w_down[0]
    gate_val = jnp.dot(expert_in, gate_w, preferred_element_type=jnp.float32)
    up_val = jnp.dot(expert_in, up_w, preferred_element_type=jnp.float32)
    sigmoid_gate = jax.nn.sigmoid(gate_val)
    silu_gate = gate_val * sigmoid_gate
    active = (silu_gate * up_val).astype(jnp.bfloat16)
    expert_out = jnp.dot(active, down_w, preferred_element_type=jnp.float32).astype(jnp.bfloat16)
    returned = lax.all_to_all(
        expert_out.reshape(expert_count, capacity, MODEL_WIDTH),
        ("expert", "context"),
        split_axis=0,
        concat_axis=0,
        tiled=True,
    ).reshape(expert_count * capacity, MODEL_WIDTH)
    pair_out = (
        returned[placed].astype(jnp.float32).reshape(tokens_per_device, top_count, MODEL_WIDTH)
    )
    mixture = jnp.sum(gate_probs[:, :, None] * pair_out, axis=1)
    output = (middle + mixture).astype(jnp.bfloat16)
    grad_y = cotangent[0].astype(jnp.float32)
    grad_gp = jnp.sum(grad_y[:, None, :] * pair_out, axis=-1)
    pair_grad = (
        (gate_probs[:, :, None] * grad_y[:, None, :])
        .astype(jnp.bfloat16)
        .reshape(tokens_per_device * top_count, MODEL_WIDTH)
    )
    grad_chosen = gate_probs * (grad_gp - jnp.sum(gate_probs * grad_gp, axis=-1, keepdims=True))
    expert_ids = jnp.arange(expert_count, dtype=jnp.int32)
    grad_logits = jnp.sum(
        jnp.where(
            route_rows[:, :, None] == expert_ids[None, None, :], grad_chosen[:, :, None], 0.0
        ),
        axis=1,
    )
    pair_pad = jnp.concatenate([pair_grad, jnp.zeros((1, MODEL_WIDTH), jnp.bfloat16)], axis=0)
    send_grads = pair_pad[source].reshape(expert_count, capacity, MODEL_WIDTH)
    out_grads = lax.all_to_all(
        send_grads, ("expert", "context"), split_axis=0, concat_axis=0, tiled=True
    ).reshape(expert_count * capacity, MODEL_WIDTH)
    grad_active = jnp.dot(out_grads, down_w.T, preferred_element_type=jnp.float32)
    grad_down_w = jnp.dot(active.T, out_grads, preferred_element_type=jnp.float32)
    grad_gate_val = (
        grad_active * up_val * sigmoid_gate * (1.0 + gate_val * (1.0 - sigmoid_gate))
    ).astype(jnp.bfloat16)
    grad_up_val = (grad_active * silu_gate).astype(jnp.bfloat16)
    grad_gate_w = jnp.dot(expert_in.T, grad_gate_val, preferred_element_type=jnp.float32)
    grad_up_w = jnp.dot(expert_in.T, grad_up_val, preferred_element_type=jnp.float32)
    grad_rows = (
        jnp.dot(grad_gate_val, gate_w.T, preferred_element_type=jnp.float32)
        + jnp.dot(grad_up_val, up_w.T, preferred_element_type=jnp.float32)
    ).astype(jnp.bfloat16)
    back_rows = lax.all_to_all(
        grad_rows.reshape(expert_count, capacity, MODEL_WIDTH),
        ("expert", "context"),
        split_axis=0,
        concat_axis=0,
        tiled=True,
    ).reshape(expert_count * capacity, MODEL_WIDTH)
    grad_ffn = jnp.sum(
        back_rows[placed].astype(jnp.float32).reshape(tokens_per_device, top_count, MODEL_WIDTH),
        axis=1,
    )
    router_f = wr_full.astype(jnp.float32)
    grad_ffn = grad_ffn + jnp.dot(grad_logits, router_f.T, precision=lax.Precision.HIGHEST)
    grad_router_w = jnp.dot(
        ffn_low.astype(jnp.float32).T, grad_logits, precision=lax.Precision.HIGHEST
    )
    _, norm_pull_b = jax.vjp(rms_norm, middle, gain_b)
    grad_middle_norm, grad_gain_two = norm_pull_b(grad_ffn)
    grad_middle = grad_y + grad_middle_norm
    branch_grad = grad_middle.astype(jnp.bfloat16)
    grad_out_w = jnp.dot(attn_low.T, branch_grad, preferred_element_type=jnp.float32)
    attention_gradient = jnp.dot(branch_grad, wo_full.T, preferred_element_type=jnp.float32).astype(
        jnp.bfloat16
    )
    heads_gradient = attention_gradient.reshape(
        tokens_per_device, KEY_VALUE_HEADS, group_width, HEAD_SIZE
    ).transpose(1, 2, 0, 3)

    def head_backward(packed):
        head_q, head_k, head_v, head_do, head_lse = packed
        scores = jnp.einsum("gtd,nd->gtn", head_q, head_k, preferred_element_type=jnp.float32)
        prob_full = jnp.where(allowed[None], jnp.exp(scores - head_lse), 0.0)
        prob_low = prob_full.astype(jnp.bfloat16)
        grad_probs = jnp.einsum("gtd,nd->gtn", head_do, head_v, preferred_element_type=jnp.float32)
        row_delta = jnp.sum(prob_full * grad_probs, axis=-1, keepdims=True)
        grad_scores = (prob_full * (grad_probs - row_delta)).astype(jnp.bfloat16)
        grad_q = jnp.einsum("gtn,nd->gtd", grad_scores, head_k, preferred_element_type=jnp.float32)
        grad_k = jnp.einsum("gtn,gtd->nd", grad_scores, head_q, preferred_element_type=jnp.float32)
        grad_v = jnp.einsum("gtn,gtd->nd", prob_low, head_do, preferred_element_type=jnp.float32)
        return (grad_q, grad_k, grad_v)

    grad_qh, grad_kh, grad_vh = lax.map(
        head_backward, (query_head_rows, key_head_rows, value_head_rows, heads_gradient, log_total)
    )
    grad_queries = grad_qh.transpose(2, 0, 1, 3).reshape(tokens_per_device, QUERY_HEADS, HEAD_SIZE)
    key_terms = jnp.concatenate(
        [
            grad_kh.transpose(1, 0, 2).reshape(key_window, key_value_width),
            grad_vh.transpose(1, 0, 2).reshape(key_window, key_value_width),
        ],
        axis=1,
    )
    key_gradient_rows = lax.psum_scatter(
        key_terms.astype(jnp.bfloat16), "context", scatter_dimension=0, tiled=True
    ).astype(jnp.float32)
    _, query_pull = jax.vjp(turn_queries, q_proj)
    grad_qp = query_pull(grad_queries)[0].reshape(tokens_per_device, q_width).astype(jnp.bfloat16)
    _, key_pullback = jax.vjp(turn_keys, key_projected)
    grad_kp = (
        key_pullback(
            key_gradient_rows[:, :key_value_width].reshape(
                tokens_per_device, KEY_VALUE_HEADS, HEAD_SIZE
            )
        )[0]
        .reshape(tokens_per_device, key_value_width)
        .astype(jnp.bfloat16)
    )
    grad_vp = key_gradient_rows[:, key_value_width:].astype(jnp.bfloat16)
    grad_normed = (
        jnp.dot(grad_qp, wq_full.T, preferred_element_type=jnp.float32)
        + jnp.dot(grad_kp, wk_full.T, preferred_element_type=jnp.float32)
        + jnp.dot(grad_vp, wv_full.T, preferred_element_type=jnp.float32)
    )
    grad_wq = jnp.dot(normed_low.T, grad_qp, preferred_element_type=jnp.float32)
    grad_wk = jnp.dot(normed_low.T, grad_kp, preferred_element_type=jnp.float32)
    grad_wv = jnp.dot(normed_low.T, grad_vp, preferred_element_type=jnp.float32)
    _, norm_pull_a = jax.vjp(rms_norm, inputs, gain_a)
    grad_norm_in, grad_gain_one = norm_pull_a(grad_normed)
    grad_input = (grad_middle + grad_norm_in).astype(jnp.bfloat16)
    piece_a, piece_q, piece_k, piece_v, piece_o, piece_b, piece_r = (
        lax.psum_scatter(
            grad_gain_one.astype(jnp.bfloat16), ("context", "dp"), scatter_dimension=0, tiled=True
        ).astype(jnp.float32),
        lax.psum_scatter(
            grad_wq.astype(jnp.bfloat16), ("context", "dp"), scatter_dimension=0, tiled=True
        ).astype(jnp.float32),
        lax.psum_scatter(
            grad_wk.astype(jnp.bfloat16), ("context", "dp"), scatter_dimension=0, tiled=True
        ).astype(jnp.float32),
        lax.psum_scatter(
            grad_wv.astype(jnp.bfloat16), ("context", "dp"), scatter_dimension=0, tiled=True
        ).astype(jnp.float32),
        lax.psum_scatter(
            grad_out_w.astype(jnp.bfloat16), ("context", "dp"), scatter_dimension=0, tiled=True
        ).astype(jnp.float32),
        lax.psum_scatter(
            grad_gain_two.astype(jnp.bfloat16), ("context", "dp"), scatter_dimension=0, tiled=True
        ).astype(jnp.float32),
        lax.psum_scatter(
            grad_router_w.astype(jnp.bfloat16), ("context", "dp"), scatter_dimension=0, tiled=True
        ).astype(jnp.float32),
    )
    sum_a, sum_q, sum_k, sum_v, sum_o, sum_b, sum_r = (
        lax.psum(piece_a.astype(jnp.bfloat16), "expert").astype(jnp.float32),
        lax.psum(piece_q.astype(jnp.bfloat16), "expert").astype(jnp.float32),
        lax.psum(piece_k.astype(jnp.bfloat16), "expert").astype(jnp.float32),
        lax.psum(piece_v.astype(jnp.bfloat16), "expert").astype(jnp.float32),
        lax.psum(piece_o.astype(jnp.bfloat16), "expert").astype(jnp.float32),
        lax.psum(piece_b.astype(jnp.bfloat16), "expert").astype(jnp.float32),
        lax.psum(piece_r.astype(jnp.bfloat16), "expert").astype(jnp.float32),
    )
    sum_gate, sum_up, sum_down = (
        lax.psum_scatter(
            grad_gate_w.astype(jnp.bfloat16), "dp", scatter_dimension=0, tiled=True
        ).astype(jnp.float32),
        lax.psum_scatter(
            grad_up_w.astype(jnp.bfloat16), "dp", scatter_dimension=0, tiled=True
        ).astype(jnp.float32),
        lax.psum_scatter(
            grad_down_w.astype(jnp.bfloat16), "dp", scatter_dimension=1, tiled=True
        ).astype(jnp.float32),
    )
    return (
        output[None],
        grad_input[None],
        sum_a,
        sum_q,
        sum_k,
        sum_v,
        sum_o,
        sum_b,
        sum_r,
        sum_gate[None],
        sum_up[None],
        sum_down[None],
    )


def solution(mesh):
    placed = (
        P(("expert", "dp"), "context", None),
        P(("expert", "dp"), "context", None),
        P(("expert", "dp"), None),
        P(("expert", "dp"), None),
        P(("expert", "dp"), "context", None),
        P(("context", "dp")),
        P(("context", "dp"), None),
        P(("context", "dp"), None),
        P(("context", "dp"), None),
        P(("context", "dp"), None),
        P(("context", "dp")),
        P(("context", "dp"), None),
        P(("expert", "context"), None, None),
        P(("expert", "context"), None, None),
        P(("expert", "context"), None, None),
    )
    return jax.shard_map(
        body,
        mesh=mesh,
        in_specs=placed,
        out_specs=(
            P(("expert", "dp"), "context", None),
            P(("expert", "dp"), "context", None),
            P(("context", "dp")),
            P(("context", "dp"), None),
            P(("context", "dp"), None),
            P(("context", "dp"), None),
            P(("context", "dp"), None),
            P(("context", "dp")),
            P(("context", "dp"), None),
            P(("expert", "context"), "dp", None),
            P(("expert", "context"), "dp", None),
            P(("expert", "context"), None, "dp"),
        ),
        check_vma=False,
    )
```

profile of v0, /device:TPU:0, one launch (start us, length us, event | category | flops | bytes accessed | tf_op | source)
XLA Modules:
  0.0 1111.7 jit_solution(13946006384287516629)
XLA Ops:
  15.5 36.6 %all-reduce.11 = (bf16[1536]{0:T(1024)(128)(2,1)S(1)}, bf16[1536]{0:T(1024)(128)(2,1)S(1)}) all-reduce(bf16[1536]{0:T(1024)(128)(2,1)S(1)} %dynamic-update-slice, bf16[1536]{0:T(1024)(128)(2,1)S(1)} %dynamic-update-slice.1), channel_id=1, replica_groups=mesh['expert'=2,'context'=4,'dp'=4] {'context','dp'}, use_global_device_ids=true, to_apply=%add.6 | all-reduce | flops 3072 | bytes 12288
  53.9 2.7 copy.61
  59.0 35.2 %all-gather.11.cloned.1.call-done = bf16[1536,512]{1,0:T(8,128)(2,1)} async-done(((bf16[96,512]{1,0:T(8,128)(2,1)}), bf16[1536,512]{1,0:T(8,128)(2,1)}) %all-gather.11.cloned.1.call-update) | async-done | bytes 1572880 | tf_op jit(solution)/shard_map/all_gather | solution.py:101
  98.9 2.3 reduce-window.11
  104.2 4.3 scatter_custom_fusion
  108.5 10.3 all-gather.13.cloned.1.call-done
  118.8 3.0 fusion.116
  121.8 2.3 copy.63
  126.3 48.1 %all-gather.7.cloned.1.call-done = bf16[1536,1536]{1,0:T(8,128)(2,1)} async-done(((bf16[96,1536]{1,0:T(8,128)(2,1)}), bf16[1536,1536]{1,0:T(8,128)(2,1)}) %all-gather.7.cloned.1.call-update) | async-done | bytes 4718608 | tf_op jit(solution)/shard_map/all_gather | solution.py:99
  174.4 6.6 copy.60
  181.0 4.0 fusion.85
  186.4 37.9 %while.30 = (s32[]{:T(128)}, bf16[8,3,256,64]{2,3,1,0:T(8,128)(2,1)S(1)}, f32[8,3,256,1]{2,1,3,0:T(4,128)S(1)}, bf16[8,3,256,64]{2,3,1,0:T(8,128)(2,1)}, bf16[8,...) while((s32[]{:T(128)}, ...), condition=%wide.region_7.8_spmd.clone.clone, body=%wide.region_4.7_spmd.clone.sunk.clone | while | flops 209190144 | bytes 11084905 | solution.py:172
  224.3 4.2 all-gather.15.cloned.1.call-done
  228.5 3.8 multiply_reduce_fusion.5
  233.8 5.4 gather_fusion
  239.2 4.9 all-to-all-start
  244.0 31.9 %all-gather = bf16[16,96,8]{1,2,0:T(8,128)(2,1)S(1)} all-gather(bf16[1,96,8]{1,2,0:T(8,128)(2,1)S(1)} %bitcast.357), channel_id=1, replica_groups=mesh['expert'=2,'context'=4,'dp'=4] {'context','dp'}, dimensions={0}, use_global_device_ids=true | all-gather | bytes 26112 | tf_op jit(solution)/shard_map/all_gather | solution.py:104
  277.6 3.7 mul.407
  281.3 7.7 mul.408
  290.5 6.5 gather_fusion.4
  301.1 3.2 multiply_convert_fusion.1
  306.2 11.1 gather_fusion.2
  317.2 4.5 all-to-all-start.2
  321.8 6.0 fusion.74
  327.7 5.4 fusion.78
  333.2 29.7 %all-to-all-done.2 = bf16[8,144,1536]{2,1,0:T(8,128)(2,1)} async-done(((bf16[8,144,1536]{2,1,0:T(8,128)(2,1)}), bf16[8,144,1536]{2,1,0:T(8,128)(2,1)}, u32[]{:S(2)}, u32[]{:S(2)}) %all-to-all-start.2) | async-done | bytes 3538976 | tf_op jit(solution)/shard_map/all_to_all | solution.py:229
  362.9 7.8 multiply_convert_fusion.2
  370.7 3.8 convolution_convert_fusion.2
  374.5 5.0 all-to-all-start.1
  379.5 3.4 fusion.76
  383.0 3.8 fusion.52
  386.8 33.8 %all-to-all-done.1 = bf16[8,144,1536]{2,1,0:T(8,128)(2,1)} async-done(((bf16[8,144,1536]{2,1,0:T(8,128)(2,1)}), bf16[8,144,1536]{2,1,0:T(8,128)(2,1)}, u32[]{:S(2)}, u32[]{:S(2)}) %all-to-all-start.1) | async-done | bytes 3538976 | tf_op jit(solution)/shard_map/all_to_all | solution.py:200
  420.6 4.7 all-to-all-start.3
  425.6 9.8 gather_fusion.1
  435.4 6.6 reshape.521
  442.0 9.7 multiply_reduce_fusion.1
  452.0 14.4 %all-to-all-done.3 = bf16[8,144,1536]{2,1,0:T(8,128)(2,1)} async-done(((bf16[8,144,1536]{2,1,0:T(8,128)(2,1)}), bf16[8,144,1536]{2,1,0:T(8,128)(2,1)}, u32[]{:S(2)}, u32[]{:S(2)}) %all-to-all-start.3) | async-done | bytes 3538976 | tf_op jit(solution)/shard_map/all_to_all | solution.py:244
  466.4 9.7 gather_fusion.3
  476.2 6.8 reshape.523
  483.0 7.8 reduce_sum.187
  490.9 2.8 multiply_reduce_fusion.3
  493.7 2.8 fusion.66
  497.6 2.3 convolution_convert_fusion.8
  501.5 77.6 %while.31 = (s32[]{:T(128)}, f32[8,3,256,64]{2,3,1,0:T(8,128)S(1)}, bf16[8,1024,64]{1,2,0:T(8,128)(2,1)}, bf16[8,1024,64]{1,2,0:T(8,128)(2,1)}, bf16[8,3,256,64]...) while((s32[]{:T(128)}, f32[8,3,256,64]{2,3,1,0:T(8,128)S(1)}, ...), condition=%wide.region_23.24_spmd.clone.clone, body=%wide.region_21.23_spmd.clone.sunk.clone | while | flops 513539328 | bytes 26187904 | solution.py:285
  579.2 3.6 pad_maximum_fusion
  585.5 4.3 convolution_convert_fusion.3
  592.7 5.4 convolution_convert_fusion.4
  599.4 5.4 convolution_convert_fusion.5
  604.9 6.7 reduce-scatter.14.cloned.1.call-done
  616.8 4.9 convolution_convert_fusion
  623.7 3.7 convolution_convert_fusion.1
  628.4 5.0 fusion.119
  633.4 38.3 %reduce-scatter.28.cloned.1.call-done = bf16[96,8]{1,0:T(8,128)(2,1)} async-done(((bf16[1536,8]{1,0:T(8,128)(2,1)}), bf16[96,8]{1,0:T(8,128)(2,1)}) %reduce-scatter.28.cloned.1.call-update) | async-done | bytes 1552
  673.1 35.2 %reduce-scatter.30.cloned.1.call-done = bf16[384,512]{1,0:T(8,128)(2,1)} async-done(((bf16[1536,512]{1,0:T(8,128)(2,1)}), bf16[384,512]{1,0:T(8,128)(2,1)}) %reduce-scatter.30.cloned.1.call-update) | async-done | bytes 393232
  710.5 34.4 %reduce-scatter.26.cloned.1.call-done = bf16[384,512]{1,0:T(8,128)(2,1)} async-done(((bf16[1536,512]{1,0:T(8,128)(2,1)}), bf16[384,512]{1,0:T(8,128)(2,1)}) %reduce-scatter.26.cloned.1.call-update) | async-done | bytes 393232 | tf_op jit(solution)/shard_map/reduce_scatter | solution.py:359
  746.9 34.5 %reduce-scatter.24.cloned.1.call-done = bf16[384,512]{1,0:T(8,128)(2,1)} async-done(((bf16[1536,512]{1,0:T(8,128)(2,1)}), bf16[384,512]{1,0:T(8,128)(2,1)}) %reduce-scatter.24.cloned.1.call-update) | async-done | bytes 393232 | tf_op jit(solution)/shard_map/reduce_scatter | solution.py:356
  787.6 32.4 %all-reduce.10 = (bf16[1536]{0:T(1024)(128)(2,1)S(1)}, bf16[1536]{0:T(1024)(128)(2,1)S(1)}) all-reduce(bf16[1536]{0:T(1024)(128)(2,1)S(1)} %get-tuple-element.171, bf16[1536]{0:T(1024)(128)(2,1)S(1)} %get-tuple-element.169), channel_id=3, replica_groups=mesh['expert'=2,'context'=4,'dp'=4] {'context','dp'}, use_global_device_ids=true, to_apply=%region_27.28.clone | all-reduce | flops 3072 | bytes 12288
  820.2 4.9 all-reduce.12
  826.8 16.8 %reduce-scatter.18.cloned.1.call-done = bf16[96,512]{1,0:T(8,128)(2,1)} async-done(((bf16[1536,512]{1,0:T(8,128)(2,1)}), bf16[96,512]{1,0:T(8,128)(2,1)}) %reduce-scatter.18.cloned.1.call-update) | async-done | bytes 98320 | tf_op jit(solution)/shard_map/reduce_scatter | solution.py:330
  843.6 62.5 %reduce-scatter.20.cloned.1.call-done = bf16[96,512]{1,0:T(8,128)(2,1)} async-done(((bf16[1536,512]{1,0:T(8,128)(2,1)}), bf16[96,512]{1,0:T(8,128)(2,1)}) %reduce-scatter.20.cloned.1.call-update) | async-done | bytes 98320 | tf_op jit(solution)/shard_map/reduce_scatter | solution.py:333
  906.1 78.4 %reduce-scatter.22.cloned.1.call-done = bf16[96,1536]{1,0:T(8,128)(2,1)} async-done(((bf16[1536,1536]{1,0:T(8,128)(2,1)}), bf16[96,1536]{1,0:T(8,128)(2,1)}) %reduce-scatter.22.cloned.1.call-update) | async-done | bytes 294928 | tf_op jit(solution)/shard_map/reduce_scatter | solution.py:336
  984.5 78.8 %reduce-scatter.16.cloned.1.call-done = bf16[96,1536]{1,0:T(8,128)(2,1)} async-done(((bf16[1536,1536]{1,0:T(8,128)(2,1)}), bf16[96,1536]{1,0:T(8,128)(2,1)}) %reduce-scatter.16.cloned.1.call-update) | async-done | bytes 294928 | tf_op jit(solution)/shard_map/reduce_scatter | solution.py:327
  1063.4 3.3 fusion.82
  1066.7 32.9 %all-reduce.16.cloned.1.call-done = (bf16[96,1536]{1,0:T(8,128)(2,1)}, bf16[96,512]{1,0:T(8,128)(2,1)}, bf16[96,512]{1,0:T(8,128)(2,1)}, bf16[96,1536]{1,0:T(8,128)(2,1)}) async-done(((bf16[96,1536]{1,0:T(8,128)(2,1)}, bf16[96,512]{1,0:T(8,128)(2,1)}, bf16[96,512]{1,0:T(8,128)(2,1)}, bf16[96,1536]{1,0:T(8,128)(2,1)}), (bf16[96,1536]{1,0:T(8,128)(2,1)}, bf16[96,512]{1,0:T(8,128)(2,1)}, ...) | async-done | bytes 786448 | tf_op jit(solution)/shard_map/psum | solution.py:348
  (332 shorter events, 184.6 us)
Async XLA Ops:
  7.2 355.7 %copy-start = (bf16[1,512,1536]{2,1,0:T(8,128)(2,1)S(1)}, bf16[1,512,1536]{2,1,0:T(8,128)(2,1)}, u32[]{:S(2)}) copy-start(bf16[1,512,1536]{2,1,0:T(8,128)(2,1)} %param.33) | copy-start | bytes 4718596
  7.2 46.7 %all-gather.9.cloned.1.call-start = ((), (), s32[]{:S(2)}) async-start(), calls=%async_computation.14 | async-start | bytes 1671168 | tf_op jit(solution)/shard_map/all_gather | solution.py:100
  7.9 86.3 %all-gather.11.cloned.1.call-start = ((), (), s32[]{:S(2)}) async-start(), calls=%async_computation.15 | async-start | bytes 1671168 | tf_op jit(solution)/shard_map/all_gather | solution.py:101
  8.7 110.1 %all-gather.13.cloned.1.call-start = ((), (), s32[]{:S(2)}) async-start(), calls=%async_computation.16 | async-start | bytes 2621440 | tf_op jit(solution)/shard_map/all_gather | solution.py:145
  52.2 128.8 %copy-start.22 = (f32[1536]{0:T(1024)}, f32[1536]{0:T(1024)S(1)}, u32[]{:S(2)}) copy-start(f32[1536]{0:T(1024)S(1)} %convert_element_type.225) | copy-start | bytes 18436
  53.6 3.0 copy-start.31
  53.6 127.4 %copy-start.26 = (f32[256]{0:T(256)}, f32[256]{0:T(256)S(1)}, u32[]{:S(2)}) copy-start(f32[256]{0:T(256)S(1)} %fusion.108) | copy-start | bytes 3076
  53.9 131.2 %copy-start.16 = (f32[256,32]{0,1:T(8,128)}, f32[256,32]{0,1:T(8,128)S(1)}, u32[]{:S(2)}) copy-start(f32[256,32]{0,1:T(8,128)S(1)} %get-tuple-element.251) | copy-start | bytes 98308
  53.9 131.2 %copy-start.18 = (f32[256,32]{0,1:T(8,128)}, f32[256,32]{0,1:T(8,128)S(1)}, u32[]{:S(2)}) copy-start(f32[256,32]{0,1:T(8,128)S(1)} %get-tuple-element.252) | copy-start | bytes 98308
  53.9 2.7 copy-start.2
  96.2 2.2 copy-start.20
  96.2 2.2 copy-start.28
  97.1 77.2 %all-gather.7.cloned.1.call-start = ((), (), s32[]{:S(2)}) async-start(), calls=%async_computation.13 | async-start | bytes 5013504 | tf_op jit(solution)/shard_map/all_gather | solution.py:99
  97.7 130.8 %all-gather.15.cloned.1.call-start = ((), (), s32[]{:S(2)}) async-start(), calls=%async_computation.17 | async-start | bytes 5013504 | tf_op jit(solution)/shard_map/all_gather | solution.py:102
  103.6 0.6 copy-start.29
  224.3 8.1 copy-start.6
  232.4 1.4 copy-start.4
  232.6 1.1 copy-start.9
  239.1 4.9 copy-start.34
  239.2 78.1 %all-to-all-start = ((bf16[8,144,1536]{2,1,0:T(8,128)(2,1)}), bf16[8,144,1536]{2,1,0:T(8,128)(2,1)}, u32[]{:S(2)}, u32[]{:S(2)}) async-start(bf16[8,144,1536]{2,1,0:T(8,128)(2,1)} %bitcast.325), calls=%async_computation | async-start | bytes 7077888 | tf_op jit(solution)/shard_map/all_to_all | solution.py:188
  317.2 45.7 %all-to-all-start.2 = ((bf16[8,144,1536]{2,1,0:T(8,128)(2,1)}), bf16[8,144,1536]{2,1,0:T(8,128)(2,1)}, u32[]{:S(2)}, u32[]{:S(2)}) async-start(bf16[8,144,1536]{2,1,0:T(8,128)(2,1)} %bitcast.326), calls=%async_computation.2 | async-start | bytes 7077888 | tf_op jit(solution)/shard_map/all_to_all | solution.py:229
  321.7 6.0 copy-start.35
  370.7 3.8 copy-start.41
  374.5 5.0 copy-start.36
  374.5 46.2 %all-to-all-start.1 = ((bf16[8,144,1536]{2,1,0:T(8,128)(2,1)}), bf16[8,144,1536]{2,1,0:T(8,128)(2,1)}, u32[]{:S(2)}, u32[]{:S(2)}) async-start(bf16[8,144,1536]{2,1,0:T(8,128)(2,1)} %bitcast.335), calls=%async_computation.1 | async-start | bytes 7077888 | tf_op jit(solution)/shard_map/all_to_all | solution.py:200
  379.5 3.5 copy-start.37
  379.5 3.5 copy-start.38
  420.6 4.8 copy-start.30
  420.6 45.8 %all-to-all-start.3 = ((bf16[8,144,1536]{2,1,0:T(8,128)(2,1)}), bf16[8,144,1536]{2,1,0:T(8,128)(2,1)}, u32[]{:S(2)}, u32[]{:S(2)}) async-start(bf16[8,144,1536]{2,1,0:T(8,128)(2,1)} %bitcast.334), calls=%async_computation.3 | async-start | bytes 7077888 | tf_op jit(solution)/shard_map/all_to_all | solution.py:244
  425.3 186.3 %reduce-scatter.14.cloned.1.call-start = ((), (), s32[]{:S(2)}) async-start(), calls=%async_computation.18 | async-start | bytes 2621440 | tf_op jit(solution)/shard_map/reduce_scatter | solution.py:296
  483.0 7.9 copy-start.5
  483.0 10.6 copy-start.12
  483.0 14.6 %slice-start = ((s8[4718592]{0:T(1024)(128)(4,1)}), s8[524288]{0:T(1024)(128)(4,1)S(1)}, s32[]{:S(2)}) async-start(s8[4718592]{0:T(1024)(128)(4,1)} %bitcast.323), calls=%async_computation.28 | async-start | bytes 1048576
  490.8 6.8 slice-start.1
  496.4 1.2 copy-start.8
  499.9 1.6 copy-start.13
  579.2 3.6 copy-start.14
  582.8 1.1 copy-start.10
  582.8 2.8 copy-start.42
  582.8 88.9 %reduce-scatter.28.cloned.1.call-start = ((), (), s32[]{:S(2)}) async-start(), calls=%async_computation.25 | async-start | bytes 417792
  585.3 123.1 %reduce-scatter.30.cloned.1.call-start = ((), (), s32[]{:S(2)}) async-start(), calls=%async_computation.26 | async-start | bytes 1966080
  591.4 1.3 copy-start.39
  591.4 153.5 %reduce-scatter.26.cloned.1.call-start = ((), (), s32[]{:S(2)}) async-start(), calls=%async_computation.24 | async-start | bytes 1966080 | tf_op jit(solution)/shard_map/reduce_scatter | solution.py:359
  598.1 1.3 copy-start.40
  598.1 183.3 %reduce-scatter.24.cloned.1.call-start = ((), (), s32[]{:S(2)}) async-start(), calls=%async_computation.23 | async-start | bytes 1966080 | tf_op jit(solution)/shard_map/reduce_scatter | solution.py:356
  604.8 7.9 copy-start.17
  604.8 7.9 copy-start.19
  604.8 8.0 copy-start.3
  604.8 8.0 copy-start.23
  604.8 8.0 copy-start.27
  604.8 238.8 %reduce-scatter.18.cloned.1.call-start = ((), (), s32[]{:S(2)}) async-start(), calls=%async_computation.20 | async-start | bytes 1671168 | tf_op jit(solution)/shard_map/reduce_scatter | solution.py:330
  612.8 2.0 copy-start.21
  614.7 2.0 copy-start.7
  614.7 291.3 %reduce-scatter.20.cloned.1.call-start = ((), (), s32[]{:S(2)}) async-start(), calls=%async_computation.21 | async-start | bytes 1671168 | tf_op jit(solution)/shard_map/reduce_scatter | solution.py:333
  616.7 367.8 %reduce-scatter.22.cloned.1.call-start = ((), (), s32[]{:S(2)}) async-start(), calls=%async_computation.22 | async-start | bytes 5013504 | tf_op jit(solution)/shard_map/reduce_scatter | solution.py:336
  621.7 441.6 %reduce-scatter.16.cloned.1.call-start = ((), (), s32[]{:S(2)}) async-start(), calls=%async_computation.19 | async-start | bytes 5013504 | tf_op jit(solution)/shard_map/reduce_scatter | solution.py:327
  627.4 472.1 %all-reduce.16.cloned.1.call-start = ((), (), s32[]{:S(2)}) async-start(), calls=%async_computation.27 | async-start | bytes 1572864 | tf_op jit(solution)/shard_map/psum | solution.py:348
  709.6 73.8 %copy-start.11 = (bf16[1536,512]{1,0:T(8,128)(2,1)S(1)}, bf16[1536,512]{1,0:T(8,128)(2,1)}, u32[]{:S(2)}) copy-start(bf16[1536,512]{1,0:T(8,128)(2,1)} %all-gather.9.cloned.1.call-done) | copy-start | bytes 4718596
  783.3 2.2 copy-start.15
  785.5 34.7 %copy-start.33 = (bf16[96,8]{0,1:T(8,128)(2,1)S(1)}, bf16[96,8]{0,1:T(8,128)(2,1)}, u32[]{:S(2)}) copy-start(bf16[96,8]{0,1:T(8,128)(2,1)} %copy.75) | copy-start | bytes 4612
  785.5 277.8 %copy-start.32 = (f32[256]{0:T(256)S(1)}, f32[256]{0:T(256)}, u32[]{:S(2)}) copy-start(f32[256]{0:T(256)} %copy-done.31) | copy-start | bytes 3076
  1063.4 41.3 %copy-start.1 = (bf16[1,512,1536]{2,1,0:T(8,128)(2,1)S(1)}, bf16[1,512,1536]{2,1,0:T(8,128)(2,1)}, u32[]{:S(2)}) copy-start(bf16[1,512,1536]{2,1,0:T(8,128)(2,1)} %param.33) | copy-start | bytes 4718596
  1099.6 3.7 copy-start.25
  1099.6 4.4 copy-start.24
Sparse Core Ops, SparseCore 0:
  10.3 42.8 all-gather.8
  55.6 38.5 all-gather.10
  97.3 21.5 all-gather.12
  121.0 53.3 all-gather.6
  176.5 51.9 all-gather.14
  582.9 28.6 reduce-scatter.13
  616.1 55.5 reduce-scatter.27
  674.0 34.2 reduce-scatter.29
  710.7 34.2 reduce-scatter.25
  747.1 34.2 reduce-scatter.23
  785.0 58.4 reduce-scatter.17
  847.6 58.4 reduce-scatter.19
  909.9 74.5 reduce-scatter.21
  988.7 74.5 reduce-scatter.15
  1065.6 33.9 all-reduce.15
where the time goes:
time: 1120 us; the launch traced here: 1110 us
  waiting for transfers between devices  597 us (53%)
  matrix products  183 us (16%)
  local copies, waits for them, and re-layouts  115 us (10%)
  blocking collectives  106 us (9%)
  other arithmetic  73.8 us (7%)
  starting transfers between devices  20.1 us (2%)
  between operations  16.6 us (1%)
    reduce_scatter x1, waiting for transfers between devices, body(): lax.psum_scatter(grad_wq.astype(jnp.bfloat16), ('context', 'dp'), scatter...  78.8 us
    reduce_scatter x1, waiting for transfers between devices, body(): lax.psum_scatter(grad_out_w.astype(jnp.bfloat16), ('context', 'dp'), scat...  78.4 us
    unnamed x17, waiting for transfers between devices  76.1 us
    unnamed x2, blocking collectives  69.1 us
    reduce_scatter x1, waiting for transfers between devices, body(): lax.psum_scatter(grad_wv.astype(jnp.bfloat16), ('context', 'dp'), scatter...  62.5 us
    all_gather x1, waiting for transfers between devices, body(): lax.all_gather(w_query, ('context', 'dp'), axis=0, tiled=True)  48.1 us
    all_gather x1, waiting for transfers between devices, body(): lax.all_gather(value_weight, ('context', 'dp'), axis=0, tiled=True)  35.2 us
    reduce_scatter x1, waiting for transfers between devices, body(): lax.psum_scatter(grad_gate_w.astype(jnp.bfloat16), 'dp', scatter_dimensio...  34.5 us
  transfers between devices with their start and end apart: 19, of which 17 were waited for; matrix products, arithmetic and copies ran while one was open for 20% of the time, Pallas kernels for 0%

commit v1 on v0

v1 whole, which is shorter than its diff:
```python
import functools

import jax
import jax.numpy as jnp
from jax import lax
from jax.experimental import pallas as pl
from jax.experimental.pallas import tpu as pltpu
from jax.sharding import PartitionSpec as P

MODEL_WIDTH = 1536
QUERY_HEADS = 24
KEY_VALUE_HEADS = 8
HEAD_SIZE = 64
MOST_LEN = 512
NORM_EPS = 1e-06
ROPE_BASE = 10000.0
MASKED = -1e30
QROWS = 128
LANES = 128
bf16 = jnp.bfloat16
f32 = jnp.float32
ANY = pl.BlockSpec(memory_space=pl.ANY)
VMEM = pl.BlockSpec(memory_space=pltpu.VMEM)
SMEM = pl.BlockSpec(memory_space=pltpu.SMEM)
NT = (((1,), (1,)), ((), ()))
TN = (((0,), (0,)), ((), ()))


def params(limit=56):
    return pltpu.CompilerParams(vmem_limit_bytes=limit * 1024 * 1024)


def cost(flops, nbytes):
    return pl.CostEstimate(flops=int(flops), bytes_accessed=int(nbytes), transcendentals=0)


def dot(a, b, dims=(((1,), (0,)), ((), ()))):
    return lax.dot_general(a, b, dims, preferred_element_type=f32)


def lane_iota(rows):
    return lax.broadcasted_iota(jnp.int32, (rows, LANES), 1)


def half_swap(v):
    lane = lane_iota(v.shape[0])
    low = lax.rem(lane, HEAD_SIZE) < HEAD_SIZE // 2
    up = pltpu.roll(v, LANES - HEAD_SIZE // 2, 1)
    down = pltpu.roll(v, HEAD_SIZE // 2, 1)
    return jnp.where(low, up, down)


def three_parts(v):
    hi = v.astype(bf16).astype(f32)
    mid = (v - hi).astype(bf16).astype(f32)
    return hi, mid, v - hi - mid


def with_parts(base, v):
    lane = lane_iota(base.shape[0])
    hi, mid, lo = three_parts(v)
    out = jnp.where(lane == HEAD_SIZE, hi, base)
    out = jnp.where(lane == HEAD_SIZE + 1, mid, out)
    return jnp.where(lane == HEAD_SIZE + 2, lo, out)


def attn_fwd_kernel(
    n_ctx, n_dp, qh, kvh, place_ref, *refs
):
    x_refs, refs = refs[:n_ctx], refs[n_ctx:]
    w_refs, refs = refs[:n_dp], refs[n_dp:]
    (gain_ref, row_ref, col_ref, start_ref, cos_ref, sin_ref), refs = refs[:6], refs[6:]
    (h1_ref, attn_ref, q_ref, k_ref, v_ref, w_ref), refs = refs[:6], refs[6:]
    x_buf, qkv_buf, sorted_buf, sem_x, sem_w = refs
    tok = x_buf.shape[1]
    total = n_ctx * tok
    group = qh // kvh
    copies = [pltpu.make_async_copy(x_refs[m], x_buf.at[m], sem_x.at[m]) for m in range(n_ctx)]
    w_copies = [
        pltpu.make_async_copy(
            w_refs[k].at[m], w_ref.at[place_ref[k * n_ctx + m]], sem_w.at[k * n_ctx + m]
        )
        for k in range(n_dp)
        for m in range(n_ctx)
    ]
    for c in copies + w_copies:
        c.start()
    for c in copies + w_copies:
        c.wait()
    q_chunks = qh * HEAD_SIZE // LANES
    k_chunks = kvh * HEAD_SIZE // LANES

    def project(m, carry):
        x = x_buf[m].astype(f32)
        r = lax.rsqrt(jnp.mean(x * x, axis=-1, keepdims=True) + NORM_EPS)
        h = (x * r * gain_ref[...]).astype(bf16)
        h1_ref[m] = h
        w = w_ref[...].reshape(MODEL_WIDTH, w_ref.shape[2])
        qkv = dot(h, w)
        rows = pl.ds(m * tok, tok)
        cos, sin = cos_ref[rows, :], sin_ref[rows, :]
        out = []
        for j in range(q_chunks + 2 * k_chunks):
            piece = qkv[:, j * LANES : (j + 1) * LANES]
            if j < q_chunks + k_chunks:
                piece = piece * cos + half_swap(piece) * sin
                if j < q_chunks:
                    piece = piece * HEAD_SIZE**-0.5
            out.append(piece)
        qkv_buf[rows, :] = jnp.concatenate(out, axis=1).astype(bf16)
        return carry

    lax.fori_loop(0, n_ctx, project, 0)

    def arrange(b, carry):
        rows = pl.ds(b * tok, tok)
        place = lax.broadcasted_iota(jnp.int32, (tok, total), 0) + b * tok
        pick = (place == row_ref[...]).astype(f32).astype(bf16)
        s = dot(pick, qkv_buf[...])
        lane = lane_iota(tok)
        ones = jnp.where(lane < HEAD_SIZE + 3, 1.0, 0.0)
        for h in range(qh + 2 * kvh):
            piece = s[:, (h // 2) * LANES : (h // 2 + 1) * LANES]
            if h % 2:
                piece = pltpu.roll(piece, HEAD_SIZE, 1)
            fill = jnp.zeros_like(ones) if h < qh else ones
            piece = jnp.where(lane < HEAD_SIZE, piece, fill).astype(bf16)
            if h < qh:
                q_ref[h, rows, :] = piece
            elif h < qh + kvh:
                k_ref[h - qh, rows, :] = piece
            else:
                v_ref[h - qh - kvh, rows, :] = piece
        return carry

    lax.fori_loop(0, n_ctx, arrange, 0)
    window = min(MOST_LEN + QROWS, total)

    def attend(b, carry):
        q0 = pl.multiple_of(b * QROWS, QROWS)
        k0 = pl.multiple_of(jnp.maximum(q0 + QROWS - window, 0), QROWS)
        rows, keys = pl.ds(q0, QROWS), pl.ds(k0, window)
        kidx = lax.broadcasted_iota(jnp.int32, (QROWS, window), 1) + k0
        qidx = lax.broadcasted_iota(jnp.int32, (QROWS, window), 0) + q0
        allowed = (kidx <= qidx) & (kidx >= start_ref[rows, :])
        outs = []
        for g in range(kvh):
            q = q_ref[g * group : (g + 1) * group, rows, :].reshape(group * QROWS, LANES)
            s = dot(q, k_ref[g, keys, :], NT).reshape(group, QROWS, window)
            s = jnp.where(allowed[None], s, MASKED)
            top = jnp.max(s, axis=-1, keepdims=True)
            e = jnp.exp(s - top)
            o = dot(e.astype(bf16).reshape(group * QROWS, window), v_ref[g, keys, :])
            o = o.reshape(group, QROWS, LANES)
            total_e = o[:, :, HEAD_SIZE : HEAD_SIZE + 1]
            lse = top + jnp.log(total_e)
            o = o / total_e
            for i in range(group):
                h = g * group + i
                base = q_ref[h, rows, :].astype(f32)
                q_ref[h, rows, :] = with_parts(base, -lse[i]).astype(bf16)
                outs.append(o[i])
        lane = lane_iota(QROWS)
        for j in range(q_chunks):
            pair = jnp.where(lane < HEAD_SIZE, outs[2 * j], pltpu.roll(outs[2 * j + 1], HEAD_SIZE, 1))
            sorted_buf[rows, j * LANES : (j + 1) * LANES] = pair.astype(bf16)
        return carry

    lax.fori_loop(0, total // QROWS, attend, 0)

    def scatter(m, carry):
        place = lax.broadcasted_iota(jnp.int32, (tok, total), 1)
        pick = (place == col_ref[pl.ds(m * tok, tok), :]).astype(f32).astype(bf16)
        attn_ref[m] = dot(pick, sorted_buf[...]).astype(bf16)
        return carry

    lax.fori_loop(0, n_ctx, scatter, 0)


def attn_fwd(places, x_pieces, w_pieces, gain, row, col, start_col, cos, sin, qh, kvh):
    n_ctx, n_dp = len(x_pieces), len(w_pieces)
    tok = x_pieces[0].shape[0]
    total = n_ctx * tok
    rows, width = w_pieces[0].shape[1:]
    shape = jax.ShapeDtypeStruct
    return pl.pallas_call(
        functools.partial(attn_fwd_kernel, n_ctx, n_dp, qh, kvh),
        out_shape=(
            shape((n_ctx, tok, MODEL_WIDTH), bf16),
            shape((n_ctx, tok, qh * HEAD_SIZE), bf16),
            shape((qh, total, LANES), bf16),
            shape((kvh, total, LANES), bf16),
            shape((kvh, total, LANES), bf16),
            shape((n_ctx * n_dp, rows, width), bf16),
        ),
        in_specs=[SMEM] + [ANY] * (n_ctx + n_dp) + [VMEM] * 6,
        out_specs=(VMEM,) * 6,
        scratch_shapes=[
            pltpu.VMEM((n_ctx, tok, MODEL_WIDTH), bf16),
            pltpu.VMEM((total, width), bf16),
            pltpu.VMEM((total, qh * HEAD_SIZE), bf16),
            pltpu.SemaphoreType.DMA((n_ctx,)),
            pltpu.SemaphoreType.DMA((n_ctx * n_dp,)),
        ],
        compiler_params=params(),
        cost_estimate=cost(20e9, 20e6),
        name="attn_fwd",
    )(places, *x_pieces, *w_pieces, gain, row, col, start_col, cos, sin)


def attn_bwd_kernel(n_ctx, qh, kvh, *refs):
    db_refs, refs = refs[:n_ctx], refs[n_ctx:]
    (wo_ref, attn_ref, q_ref, k_ref, v_ref), refs = refs[:5], refs[5:]
    (row_ref, col_ref, start_ref, cos_ref, sin_ref), refs = refs[:5], refs[5:]
    out_ref, db_buf, dat_buf, do_buf, dq_buf, dk_buf, dv_buf, dqkv_buf, sem = refs
    tok = db_buf.shape[1]
    total = n_ctx * tok
    group = qh // kvh
    q_chunks = qh * HEAD_SIZE // LANES
    k_chunks = kvh * HEAD_SIZE // LANES
    copies = [pltpu.make_async_copy(db_refs[m], db_buf.at[m], sem.at[m]) for m in range(n_ctx)]
    for c in copies:
        c.start()
    dk_buf[...] = jnp.zeros_like(dk_buf)
    dv_buf[...] = jnp.zeros_like(dv_buf)
    for c in copies:
        c.wait()
    q_width = qh * HEAD_SIZE

    def lift(m, carry):
        rows = pl.ds(m * tok, tok)
        low = dot(db_buf[m], wo_ref[...], NT).astype(bf16)
        dat_buf[rows, :q_width] = low
        prod = low.astype(f32) * attn_ref[m].astype(f32)
        lane = lane_iota(tok)
        parts = jnp.zeros((tok, LANES), f32)
        for h in range(qh):
            delta = -jnp.sum(prod[:, h * HEAD_SIZE : (h + 1) * HEAD_SIZE], axis=1, keepdims=True)
            for i, v in enumerate(three_parts(delta)):
                parts = jnp.where(lane == 3 * h + i, v, parts)
        dat_buf[rows, q_width:] = parts.astype(bf16)
        return carry

    lax.fori_loop(0, n_ctx, lift, 0)

    def arrange(b, carry):
        rows = pl.ds(b * tok, tok)
        place = lax.broadcasted_iota(jnp.int32, (tok, total), 0) + b * tok
        pick = (place == row_ref[...]).astype(f32).astype(bf16)
        s = dot(pick, dat_buf[...])
        lane = lane_iota(tok)
        extra = s[:, q_width:]
        for h in range(qh):
            piece = s[:, (h // 2) * LANES : (h // 2 + 1) * LANES]
            if h % 2:
                piece = pltpu.roll(piece, HEAD_SIZE, 1)
            tail = pltpu.roll(extra, HEAD_SIZE - 3 * h, 1)
            tail = jnp.where(lane < HEAD_SIZE + 3, tail, 0.0)
            do_buf[h, rows, :] = jnp.where(lane < HEAD_SIZE, piece, tail).astype(bf16)
        return carry

    lax.fori_loop(0, n_ctx, arrange, 0)
    window = min(MOST_LEN + QROWS, total)

    def attend(b, carry):
        q0 = pl.multiple_of(b * QROWS, QROWS)
        k0 = pl.multiple_of(jnp.maximum(q0 + QROWS - window, 0), QROWS)
        rows, keys = pl.ds(q0, QROWS), pl.ds(k0, window)
        kidx = lax.broadcasted_iota(jnp.int32, (window, QROWS), 0) + k0
        qidx = lax.broadcasted_iota(jnp.int32, (window, QROWS), 1) + q0
        allowed = (kidx <= qidx) & (kidx >= start_ref[:, rows])
        allowed = jnp.concatenate([allowed.astype(f32)] * group, axis=1) > 0.5
        for g in range(kvh):
            heads = slice(g * group, (g + 1) * group)
            q = q_ref[heads, rows, :].reshape(group * QROWS, LANES)
            do = do_buf[heads, rows, :].reshape(group * QROWS, LANES)
            k, v = k_ref[g, keys, :], v_ref[g, keys, :]
            p = jnp.where(allowed, jnp.exp(dot(k, q, NT)), 0.0)
            ds = (p * dot(v, do, NT)).astype(bf16)
            dv_buf[g, keys, :] += dot(p.astype(bf16), do)
            dk_buf[g, keys, :] += dot(ds, q)
            dq = dot(ds, k, TN)
            dq_buf[heads, rows, :] = dq.reshape(group, QROWS, LANES)
        return carry

    lax.fori_loop(0, total // QROWS, attend, 0)

    def turn_back(b, carry):
        rows = pl.ds(b * tok, tok)
        cos, sin = cos_ref[rows, :], sin_ref[rows, :]
        lane = lane_iota(tok)
        heads = [dq_buf[h, rows, :] for h in range(qh)]
        heads += [dk_buf[h, rows, :] for h in range(kvh)]
        heads += [dv_buf[h, rows, :] for h in range(kvh)]
        for j in range(q_chunks + 2 * k_chunks):
            pair = jnp.where(lane < HEAD_SIZE, heads[2 * j], pltpu.roll(heads[2 * j + 1], HEAD_SIZE, 1))
            if j < q_chunks:
                pair = pair * HEAD_SIZE**-0.5
            if j < q_chunks + k_chunks:
                pair = pair * cos - half_swap(pair) * sin
            dqkv_buf[rows, j * LANES : (j + 1) * LANES] = pair.astype(bf16)
        return carry

    lax.fori_loop(0, n_ctx, turn_back, 0)

    def scatter(m, carry):
        place = lax.broadcasted_iota(jnp.int32, (tok, total), 1)
        pick = (place == col_ref[pl.ds(m * tok, tok), :]).astype(f32).astype(bf16)
        out_ref[m] = dot(pick, dqkv_buf[...]).astype(bf16)
        return carry

    lax.fori_loop(0, n_ctx, scatter, 0)


def attn_bwd(db_pieces, wo, attn, q, k, v, row, col, start_row, cos, sin, qh, kvh):
    n_ctx = len(db_pieces)
    tok = db_pieces[0].shape[0]
    total = n_ctx * tok
    width = (qh + 2 * kvh) * HEAD_SIZE
    return pl.pallas_call(
        functools.partial(attn_bwd_kernel, n_ctx, qh, kvh),
        out_shape=jax.ShapeDtypeStruct((n_ctx, tok, width), bf16),
        in_specs=[ANY] * n_ctx + [VMEM] * 10,
        out_specs=VMEM,
        scratch_shapes=[
            pltpu.VMEM((n_ctx, tok, MODEL_WIDTH), bf16),
            pltpu.VMEM((total, qh * HEAD_SIZE + LANES), bf16),
            pltpu.VMEM((qh, total, LANES), bf16),
            pltpu.VMEM((qh, total, LANES), f32),
            pltpu.VMEM((kvh, total, LANES), f32),
            pltpu.VMEM((kvh, total, LANES), f32),
            pltpu.VMEM((total, width), bf16),
            pltpu.SemaphoreType.DMA((n_ctx,)),
        ],
        compiler_params=params(),
        cost_estimate=cost(25e9, 20e6),
        name="attn_bwd",
    )(*db_pieces, wo, attn, q, k, v, row, col, start_row, cos, sin)


def expert_math(e, cap, experts, h_blocks, dy_blocks, route_blocks, wg, wu, wd, wr):
    tok = h_blocks[0].shape[0]
    before = lax.broadcasted_iota(jnp.int32, (tok, tok), 0) < lax.broadcasted_iota(
        jnp.int32, (tok, tok), 1
    )
    before = before.astype(f32).astype(bf16)
    names = lax.broadcasted_iota(jnp.int32, (LANES, tok), 0)
    slots = lax.broadcasted_iota(jnp.int32, (cap, tok), 0).astype(f32)
    picks, xs, dys, masks = [], [], [], []
    for h, dy, routes in zip(h_blocks, dy_blocks, route_blocks):
        hit = jnp.zeros((1, tok), f32)
        named = jnp.zeros((LANES, tok), f32)
        for j in range(routes.shape[0]):
            hit = hit + jnp.where(routes[j : j + 1] == e, 1.0, 0.0)
            named = named + jnp.where(names == routes[j : j + 1], 1.0, 0.0)
        hits = jnp.broadcast_to(hit, (8, tok)).astype(bf16)
        slot = dot(hits, before)[0:1]
        pick = jnp.where((slots == slot) & (hit > 0.5), 1.0, 0.0).astype(bf16)
        picks.append(pick)
        xs.append(dot(pick, h))
        dys.append(dot(pick, dy))
        masks.append(dot(pick, named.astype(bf16), NT))
    xs = jnp.concatenate(xs, axis=0).astype(bf16)
    dys = jnp.concatenate(dys, axis=0)
    mask = jnp.concatenate(masks, axis=0) > 0.5
    gate = dot(xs, wg)
    up = dot(xs, wu)
    sig = jax.nn.sigmoid(gate)
    silu = gate * sig
    act = (silu * up).astype(bf16)
    eout = dot(act, wd).astype(bf16).astype(f32)
    logits = jnp.where(mask, dot(xs, wr), MASKED)
    ex = jnp.where(mask, jnp.exp(logits - jnp.max(logits, axis=1, keepdims=True)), 0.0)
    lane = lax.broadcasted_iota(jnp.int32, ex.shape, 1)
    own = lane == e
    denom = jnp.sum(ex, axis=1, keepdims=True)
    probs = ex / jnp.where(denom > 0.0, denom, 1.0)
    gp = jnp.sum(jnp.where(own, probs, 0.0), axis=1, keepdims=True)
    dgp = jnp.sum(dys * eout, axis=1, keepdims=True)
    coef = gp * dgp * (jnp.where(own, 1.0, 0.0) - probs)
    hi = coef.astype(bf16).astype(f32)
    low = pltpu.roll(coef - hi, LANES // 2, 1)
    coef = jnp.where(lane < LANES // 2, hi, low).astype(bf16)
    deout = (gp * dys).astype(bf16)
    yrow = (gp * eout).astype(bf16)
    dact = dot(deout, wd, NT)
    dgate = (dact * up * sig * (1.0 + gate * (1.0 - sig))).astype(bf16)
    dup = (dact * silu).astype(bf16)
    lane_w = lax.broadcasted_iota(jnp.int32, wr.shape, 1)
    both = jnp.where(lane_w < LANES // 2, wr.astype(f32), pltpu.roll(wr.astype(f32), LANES // 2, 1))
    drow = dot(dgate, wg, NT) + dot(dup, wu, NT) + dot(coef, both.astype(bf16), NT)
    drow = drow.astype(bf16)
    d_out, y_out = [], []
    for i, pick in enumerate(picks):
        rows = slice(i * cap, (i + 1) * cap)
        d_out.append(dot(pick, drow[rows], TN).astype(bf16))
        y_out.append(dot(pick, yrow[rows], TN).astype(bf16))
    return d_out, y_out, xs, deout, act, dgate, dup, coef


def expert_kernel(pieces, cap, experts, e_ref, *refs):
    n_in = len(pieces)
    h_refs, refs = refs[:n_in], refs[n_in:]
    dy_refs, refs = refs[:n_in], refs[n_in:]
    (routes_ref, wg_ref, wu_ref, wd_ref, wr_ref), refs = refs[:5], refs[5:]
    outs, refs = refs[:10], refs[10:]
    step = pl.program_id(0)
    if len(refs):
        h_buf, dy_buf, sem = refs

        def copies(which):
            got = []
            for i, (block, col, width) in enumerate(pieces):
                if block // 2 == which:
                    spot = (block, slice(None), slice(col, col + width))
                    got.append(pltpu.make_async_copy(h_refs[i], h_buf.at[spot], sem.at[0, i]))
                    got.append(pltpu.make_async_copy(dy_refs[i], dy_buf.at[spot], sem.at[1, i]))
            return got

        n_steps = h_buf.shape[0] // 2

        @pl.when(step == 0)
        def _():
            for s in range(n_steps):
                for c in copies(s):
                    c.start()

        for s in range(n_steps):

            @pl.when(step == s)
            def _():
                for c in copies(s):
                    c.wait()

        h_blocks = [h_buf[2 * step + i] for i in range(2)]
        dy_blocks = [dy_buf[2 * step + i] for i in range(2)]
    else:
        h_blocks = [h_refs[0][i] for i in range(2)]
        dy_blocks = [dy_refs[0][i] for i in range(2)]
    routes = [routes_ref[2 * step + i] for i in range(2)]
    d_out, y_out, xs, deout, act, dgate, dup, coef = expert_math(
        e_ref[0], cap, experts, h_blocks, dy_blocks, routes,
        wg_ref[...], wu_ref[...], wd_ref[...], wr_ref[...],
    )
    outs[0][0] = d_out[0]
    outs[1][0] = d_out[1]
    outs[2][0] = y_out[0]
    outs[3][0] = y_out[1]
    for ref, v in zip(outs[4:], (xs, deout, act, dgate, dup, coef)):
        ref[...] = v


def run_experts(e, pieces, h_list, dy_list, routes_t, wg, wu, wd, wr, cap, experts, tok):
    n_blocks = routes_t.shape[0]
    steps = n_blocks // 2
    ff = wg.shape[1]
    rows = 2 * cap
    shape = jax.ShapeDtypeStruct
    block = pl.BlockSpec((1, tok, MODEL_WIDTH), lambda i, *_: (i, 0, 0))
    wide = pl.BlockSpec((rows, MODEL_WIDTH), lambda i, *_: (i, 0))
    thin = pl.BlockSpec((rows, ff), lambda i, *_: (i, 0))
    edge = pl.BlockSpec((rows, LANES), lambda i, *_: (i, 0))
    whole = pl.BlockSpec((2, tok, MODEL_WIDTH), lambda i, *_: (i, 0, 0))
    by_hand = pieces is not None
    n_in = len(h_list)
    scratch = []
    if by_hand:
        scratch = [
            pltpu.VMEM((n_blocks, tok, MODEL_WIDTH), bf16),
            pltpu.VMEM((n_blocks, tok, MODEL_WIDTH), bf16),
            pltpu.SemaphoreType.DMA((2, n_in)),
        ]
    grid_spec = pltpu.PrefetchScalarGridSpec(
        num_scalar_prefetch=1,
        grid=(steps,),
        in_specs=[ANY if by_hand else whole] * (2 * n_in) + [VMEM] * 5,
        out_specs=[block] * 4 + [wide] * 2 + [thin] * 3 + [edge],
        scratch_shapes=scratch,
    )
    half = shape((steps, tok, MODEL_WIDTH), bf16)
    return pl.pallas_call(
        functools.partial(
            expert_kernel, pieces if by_hand else [None] * n_in, cap, experts
        ),
        out_shape=[half] * 4
        + [shape((steps * rows, MODEL_WIDTH), bf16)] * 2
        + [shape((steps * rows, ff), bf16)] * 3
        + [shape((steps * rows, LANES), bf16)],
        grid_spec=grid_spec,
        compiler_params=params(60),
        cost_estimate=cost(30e9, 30e6),
        name="experts",
    )(e, *h_list, *dy_list, routes_t, wg, wu, wd, wr)


def flip(v, axis, bit):
    n = lax.axis_size(axis)
    return lax.ppermute(v, axis, [(i, i ^ bit) for i in range(n)])


def step_up(v, axis):
    n = lax.axis_size(axis)
    return lax.ppermute(v, axis, [(i, (i + 1) % n) for i in range(n)])


def ctx_gather(v):
    n = lax.axis_size("context")
    pieces = {0: v}
    bit = n // 2
    while bit:
        for m in list(pieces):
            pieces[m | bit] = flip(pieces[m], "context", bit)
        bit //= 2
    return [pieces[m] for m in range(n)]


def add_low(a, b):
    return (a.astype(f32) + b.astype(f32)).astype(bf16)


def ring(v, axis):
    pieces = [v]
    for _ in range(lax.axis_size(axis) - 1):
        pieces.append(step_up(pieces[-1], axis))
    return pieces


def ring_sum(chunk, axis):
    n = lax.axis_size(axis)
    d = lax.axis_index(axis)
    part = chunk(lax.rem(d + n - 1, n)).astype(bf16)
    for s in range(n - 1):
        got = step_up(part, axis)
        part = got.astype(f32) + chunk(lax.rem(d + 2 * n - 2 - s, n)).astype(f32)
        if s < n - 2:
            part = part.astype(bf16)
    return part


def after(v, *deps):
    return lax.optimization_barrier((v, *deps))[0]


HALF = MODEL_WIDTH // 2


def plane_gather(v, wide=True):
    if lax.axis_size("expert") != 2 or lax.axis_size("context") != 4:
        return None, [lax.all_gather(v, ("expert", "context"), axis=0, tiled=False)]
    a, b = v[:, :HALF], v[:, HALF:]
    ay, bx = flip(a, "context", 2), flip(b, "expert", 1)
    ax, by = flip(a, "expert", 1), flip(b, "context", 2)
    axy, bxy = flip(ay, "expert", 1), flip(bx, "context", 2)
    spec, out = [(0, 0, MODEL_WIDTH), (1, 0, MODEL_WIDTH)], [v, flip(v, "context", 1)]
    for block, col, p in (
        (2, 0, ay), (4, HALF, bx), (4, 0, ax), (2, HALF, by), (6, 0, axy), (6, HALF, bxy),
    ):
        spec += [(block, col, HALF), (block + 1, col, HALF)]
        out += [p, flip(p, "context", 1)]
    return spec, out


def plane_sum(even, odd):
    if lax.axis_size("expert") != 2 or lax.axis_size("context") != 4:
        both = jnp.stack([even, odd], axis=1)
        tok, width = even.shape[1:]
        return lax.psum_scatter(
            both.reshape(-1, width), ("expert", "context"), scatter_dimension=0, tiled=True
        ).astype(f32)
    got = flip(odd, "context", 1)
    d3 = add_low(even[3], got[3])
    ga, gb = flip(d3[:, :HALF], "expert", 1), flip(d3[:, HALF:], "context", 2)
    y = add_low(even[1], got[1])
    x = add_low(even[2], got[2])
    yb, xa = flip(y[:, HALF:], "context", 2), flip(x[:, :HALF], "expert", 1)
    ya = flip(add_low(y[:, :HALF], ga), "context", 2)
    xb = flip(add_low(x[:, HALF:], gb), "expert", 1)
    own = even[0].astype(f32) + got[0].astype(f32)
    left = own[:, :HALF] + ya.astype(f32) + xa.astype(f32)
    right = own[:, HALF:] + yb.astype(f32) + xb.astype(f32)
    return jnp.concatenate([left, right], axis=1)


def ctx_sum(p):
    own = p[0].astype(f32) + flip(p[1], "context", 1).astype(f32)
    far = add_low(p[2], flip(p[3], "context", 1))
    return own + flip(far, "context", 2).astype(f32)


def put_in_order(places, pieces, name):
    n = len(pieces)
    rows, width = pieces[0].shape

    def kernel(place_ref, *refs):
        out_ref, sem = refs[n:]
        copies = [
            pltpu.make_async_copy(refs[k], out_ref.at[place_ref[k]], sem.at[k]) for k in range(n)
        ]
        for c in copies:
            c.start()
        for c in copies:
            c.wait()

    return pl.pallas_call(
        kernel,
        out_shape=jax.ShapeDtypeStruct((n, rows, width), pieces[0].dtype),
        in_specs=[SMEM] + [ANY] * n,
        out_specs=ANY,
        scratch_shapes=[pltpu.SemaphoreType.DMA((n,))],
        cost_estimate=cost(0, 2 * n * rows * width * 2),
        name=name,
    )(places, *pieces)


def rms_back(dh, v, r, gain):
    inner = jnp.sum(gain * dh * v, axis=-1, keepdims=True)
    dv = r * gain * dh - v * (r * r * r) * (inner / MODEL_WIDTH)
    return dv, jnp.sum(dh * v * r, axis=0)


def body(
    hidden, cotangent, token_order, lengths, routes, attn_gain, w_query, key_weight,
    value_weight, w_out, ffn_gain, w_router, w_gate, w_up, w_down,
):
    tok, top = hidden.shape[1], routes.shape[2]
    n_exp, n_ctx, n_dp = (lax.axis_size(a) for a in ("expert", "context", "dp"))
    experts = n_exp * n_ctx
    cap = -(-(9 * tok * top // (8 * experts)) // 16) * 16
    qh, kvh = QUERY_HEADS // n_ctx, KEY_VALUE_HEADS // n_ctx
    qw, kw = qh * HEAD_SIZE, kvh * HEAD_SIZE
    rows = w_query.shape[0]
    ex, cx, dx = (lax.axis_index(a) for a in ("expert", "context", "dp"))
    my_expert = ex * n_ctx + cx
    total = n_ctx * tok

    def for_context(c):
        return jnp.concatenate(
            [
                lax.dynamic_slice_in_dim(w_query, c * qw, qw, 1),
                lax.dynamic_slice_in_dim(key_weight, c * kw, kw, 1),
                lax.dynamic_slice_in_dim(value_weight, c * kw, kw, 1),
            ],
            axis=1,
        )

    got = [for_context(cx)]
    for m in range(1, n_ctx):
        got.append(flip(for_context(cx ^ m), "context", m))
    w_pieces = ring(jnp.stack(got), "dp")
    small = jnp.concatenate([attn_gain[None], ffn_gain[None], w_router.T], axis=0)
    small_rows = small.shape[0]
    small = jnp.pad(small, ((0, -small_rows % 8), (0, LANES - rows)))
    small_got = [small] + [flip(small, "context", m) for m in range(1, n_ctx)]
    small_pieces = ring(jnp.stack(small_got), "dp")
    k_of = jnp.arange(n_dp, dtype=jnp.int32)
    d_of = lax.rem(dx - k_of + n_dp, n_dp)
    c_of = cx ^ jnp.arange(n_ctx, dtype=jnp.int32)
    places = (c_of[None, :] * n_dp + d_of[:, None]).reshape(-1).astype(jnp.int32)
    small_all = jnp.stack(small_pieces)[:, :, :small_rows, :rows]
    where_is = (lax.rem(dx - jnp.arange(n_dp) + n_dp, n_dp)[None, :] * n_ctx) + (
        cx ^ jnp.arange(n_ctx)
    )[:, None]
    small_all = small_all.reshape(n_dp * n_ctx, small_rows, rows)[where_is.reshape(-1)]
    small_all = small_all.transpose(1, 0, 2).reshape(small_rows, MODEL_WIDTH)
    gain_a = small_all[0:1].astype(f32)
    gain_b = small_all[1:2].astype(f32)
    wr = jnp.pad(small_all[2:].T, ((0, 0), (0, LANES - experts)))

    x_pieces = ctx_gather(hidden[0])
    order_rel = token_order[0].reshape(n_ctx, tok)[c_of].reshape(-1)
    place_ids = jnp.arange(total, dtype=jnp.int32)
    both = jnp.concatenate([order_rel, place_ids])
    end = jnp.zeros((), jnp.int32)
    start = jnp.zeros_like(both)
    for j in range(lengths.shape[1]):
        end = end + lengths[0, j]
        start = start + jnp.where(both >= end, lengths[0, j], 0)
    half = HEAD_SIZE // 2
    freq = ROPE_BASE ** (-(jnp.arange(half, dtype=f32) * 2.0 / HEAD_SIZE))
    angle = (both - start).astype(f32)[:, None] * freq[None, :]
    cos, sin = jnp.cos(angle), jnp.sin(angle)
    cos = jnp.concatenate([cos] * 4, axis=1)
    sin = jnp.concatenate([-sin, sin] * 2, axis=1)
    row, col = order_rel[None, :], order_rel[:, None]
    start_place = start[total:]

    h1, attn, q, k, v, wqkv = attn_fwd(
        places, x_pieces, w_pieces, gain_a, row, col, start_place[:, None],
        cos[:total], sin[:total], qh, kvh,
    )
    wo_pieces = ring(after(w_out, w_pieces[-1]), "dp")
    wo = put_in_order(d_of.astype(jnp.int32), wo_pieces, "wo").reshape(qw, MODEL_WIDTH)

    dy_own = after(cotangent[0], x_pieces[-1])
    pieces, dy_list = plane_gather(dy_own)
    routes_t = routes[0].T
    if pieces is None:
        routes_all = lax.all_gather(routes_t, ("expert", "context"), axis=0, tiled=False)
    else:
        pr = {0: routes_t}
        for axis, bit, off in (("expert", 1, 4), ("context", 2, 2), ("context", 1, 1)):
            for m in list(pr):
                pr[m | off] = flip(pr[m], axis, bit)
        routes_all = jnp.stack([pr[m] for m in range(8)])

    partial_far = dot(attn[2:].reshape(-1, qw), wo).astype(bf16).reshape(2, tok, MODEL_WIDTH)
    partial_near = dot(attn[:2].reshape(-1, qw), wo).astype(bf16).reshape(2, tok, MODEL_WIDTH)
    x_own = hidden[0].astype(f32)
    middle = x_own + ctx_sum([partial_near[0], partial_near[1], partial_far[0], partial_far[1]])
    r_b = lax.rsqrt(jnp.mean(middle * middle, axis=-1, keepdims=True) + NORM_EPS)
    h2 = (middle * r_b * gain_b).astype(bf16)
    _, h_list = plane_gather(h2)

    wg, wu, wd = w_gate[0], w_up[0], w_down[0]
    d_even, d_odd, y_even, y_odd, xs, deout, act, dgate, dup, coef = run_experts(
        my_expert.reshape(1).astype(jnp.int32), pieces, h_list, dy_list, routes_all,
        wg, wu, wd, wr, cap, experts, tok,
    )
    dh2 = plane_sum(d_even, d_odd)
    g_gate = dot(xs, dgate, TN).astype(bf16)
    g_up = dot(xs, dup, TN).astype(bf16)
    g_down = dot(act, deout, TN).astype(bf16)
    g_router = dot(xs, coef, TN)
    g_router = g_router[:, :experts] + g_router[:, LANES // 2 : LANES // 2 + experts]

    dy = cotangent[0].astype(f32)
    d_norm, g_gain_b = rms_back(dh2, middle, r_b, gain_b)
    d_middle = dy + d_norm
    db_pieces = ctx_gather(d_middle.astype(bf16))
    mixture = plane_sum(after(y_even, db_pieces[2]), after(y_odd, db_pieces[2]))
    output = (middle + mixture).astype(bf16)

    slab = MODEL_WIDTH // n_dp

    def rows_of(g):
        return lambda d: lax.dynamic_slice_in_dim(g, d * slab, slab, 0)

    sum_gate = ring_sum(rows_of(g_gate), "dp")
    sum_up = ring_sum(rows_of(g_up), "dp")
    sum_down = ring_sum(lambda d: lax.dynamic_slice_in_dim(g_down, d * slab, slab, 1), "dp")

    dqkv = attn_bwd(
        db_pieces, wo, attn, q, k, v, row, col, start_place[None, :],
        cos[total:], sin[total:], qh, kvh,
    )
    db_all = jnp.concatenate(db_pieces, axis=0)
    g_out = dot(attn.reshape(total, qw), db_all, TN).astype(bf16)
    dqkv_flat = dqkv.reshape(total, -1)
    g_qkv = dot(h1.reshape(total, MODEL_WIDTH), dqkv_flat, TN).astype(bf16)
    w_flat = wqkv.reshape(MODEL_WIDTH, -1)
    dh1_part = dot(dqkv_flat, w_flat, NT).astype(bf16).reshape(n_ctx, tok, MODEL_WIDTH)
    dh1 = ctx_sum([dh1_part[m] for m in range(n_ctx)])
    r_a = lax.rsqrt(jnp.mean(x_own * x_own, axis=-1, keepdims=True) + NORM_EPS)
    d_in, g_gain_a = rms_back(dh1, x_own, r_a, gain_a)
    grad_input = (d_middle + d_in).astype(bf16)

    def over_experts(part):
        if n_exp == 2:
            low = part.astype(bf16)
            return low.astype(f32) + flip(low, "expert", 1).astype(f32)
        return lax.psum(part.astype(bf16), "expert").astype(f32)

    width = qw + 2 * kw
    g4 = g_qkv.reshape(n_ctx, n_dp, rows, width)
    s_qkv = ring_sum(lambda d: lax.dynamic_index_in_dim(g4, d, 1, keepdims=False), "dp")
    s_qkv = over_experts(s_qkv).astype(bf16)
    s_out = over_experts(
        ring_sum(lambda d: lax.dynamic_slice_in_dim(g_out, d * rows, rows, 0), "dp")
    )
    back = [lax.dynamic_index_in_dim(s_qkv, cx, 0, keepdims=False)]
    for m in range(1, n_ctx):
        back.append(flip(lax.dynamic_index_in_dim(s_qkv, cx ^ m, 0, keepdims=False), "context", m))
    back = jnp.stack(back)[c_of]

    def columns(lo, hi):
        return back[:, :, lo:hi].transpose(1, 0, 2).reshape(rows, -1).astype(f32)

    sum_q, sum_k, sum_v = columns(0, qw), columns(qw, qw + kw), columns(qw + kw, width)
    tiny = jnp.concatenate([g_gain_a[None], g_gain_b[None], g_router.T], axis=0)
    tiny_rows = tiny.shape[0]
    if n_exp == 2:
        tiny = tiny + flip(tiny, "expert", 1)
    else:
        tiny = lax.psum(tiny, "expert")
    tiny = tiny.reshape(tiny_rows, n_ctx * n_dp, rows).transpose(1, 0, 2)
    tiny = lax.all_to_all(tiny, ("context", "dp"), split_axis=0, concat_axis=0, tiled=True)
    tiny = jnp.sum(tiny, axis=0)
    return (
        output[None], grad_input[None], tiny[0], sum_q, sum_k, sum_v, s_out,
        tiny[1], tiny[2:].T, sum_gate[None], sum_up[None], sum_down[None],
    )


def solution(mesh):
    tokens = P(("expert", "dp"), "context", None)
    group = P(("expert", "dp"), None)
    vec, mat = P(("context", "dp")), P(("context", "dp"), None)
    expert = P(("expert", "context"), None, None)
    by_rows = P(("expert", "context"), "dp", None)
    by_cols = P(("expert", "context"), None, "dp")
    return jax.shard_map(
        body,
        mesh=mesh,
        in_specs=(
            tokens, tokens, group, group, tokens, vec, mat, mat, mat, mat, vec, mat,
            expert, expert, expert,
        ),
        out_specs=(
            tokens, tokens, vec, mat, mat, mat, mat, vec, mat, by_rows, by_rows, by_cols,
        ),
        check_vma=False,
    )
```

time: 1120 us -> 538 us (0.48)
  waiting for transfers between devices: 597 us -> 223 us
  matrix products: 183 us -> 22.8 us
  Pallas kernels: 0 us -> 131 us
  blocking collectives: 106 us -> 0 us
  local copies, waits for them, and re-layouts: 115 us -> 35.4 us
  starting transfers between devices: 20.1 us -> 67 us
  other arithmetic: 73.8 us -> 49 us
  between operations: 16.6 us -> 4.25 us
    reduce_scatter x7 -> x0, waiting for transfers between devices: 312 us -> none  [the longest x1 78.8 us: body(): lax.psum_scatter(grad_wq.astype(jnp.bfloat16), ('context', 'dp'), scatter...]
    ppermute x0 -> x95, waiting for transfers between devices: none -> 220 us  [the longest x24 115 us: step_up(): return lax.ppermute(v, axis, [(i, (i + 1) % n) for i in range(n)])]
    dot_general x80 -> x9, matrix products: 183 us -> 22.8 us  [dot(): return lax.dot_general(a, b, dims, preferred_element_type=f32)]
    pallas_call x0 -> x4, Pallas kernels: none -> 131 us  [the longest x1 37.5 us: put_in_order(): pl.pallas_call(kernel, out_shape=jax.ShapeDtypeStruct((n, rows, width), p...]
    all_gather x5 -> x0, waiting for transfers between devices: 97.8 us -> none  [the longest x1 48.1 us: body(): lax.all_gather(w_query, ('context', 'dp'), axis=0, tiled=True)]
    unnamed x17 -> x0, waiting for transfers between devices: 76.1 us -> none
    all_to_all x4 -> x1, waiting for transfers between devices: 77.9 us -> 3.14 us  [body(): lax.all_to_all(tiny, ('context', 'dp'), split_axis=0, concat_axis=0, tile...]
    unnamed x2 -> x0, blocking collectives: 69.1 us -> none
  transfers between devices with their start and end apart: 19 -> 96, of which waited for: 17 -> 41; matrix products, arithmetic and copies ran while one was open for 20% -> 17% of each run, Pallas kernels for 0% -> 11%
where the time goes in v1:
time: 538 us; the launch traced here: 532 us
  waiting for transfers between devices  223 us (41%)
  Pallas kernels  131 us (24%)
  starting transfers between devices  67 us (12%)
  other arithmetic  49 us (9%)
  local copies, waits for them, and re-layouts  35.4 us (7%)
  matrix products  22.8 us (4%)
    ppermute x24, waiting for transfers between devices, step_up(): return lax.ppermute(v, axis, [(i, (i + 1) % n) for i in range(n)])  115 us
    ppermute x71, waiting for transfers between devices, flip(): return lax.ppermute(v, axis, [(i, i ^ bit) for i in range(n)])  105 us
    ppermute x71, starting transfers between devices, flip(): return lax.ppermute(v, axis, [(i, i ^ bit) for i in range(n)])  48.6 us
    pallas_call x1, Pallas kernels, put_in_order(): pl.pallas_call(kernel, out_shape=jax.ShapeDtypeStruct((n, rows, width), p...  37.5 us
    pallas_call x1, Pallas kernels, run_experts(): pl.pallas_call(functools.partial(expert_kernel, pieces if by_hand else [N...  32.8 us
    pallas_call x1, Pallas kernels, attn_bwd(): pl.pallas_call(functools.partial(attn_bwd_kernel, n_ctx, qh, kvh), out_sh...  32.7 us
    pallas_call x1, Pallas kernels, attn_fwd(): pl.pallas_call(functools.partial(attn_fwd_kernel, n_ctx, n_dp, qh, kvh),...  27.9 us
    dot_general x9, matrix products, dot(): return lax.dot_general(a, b, dims, preferred_element_type=f32)  22.8 us
  transfers between devices with their start and end apart: 96, of which 41 were waited for; matrix products, arithmetic and copies ran while one was open for 17% of the time, Pallas kernels for 11%

profile of v1, /device:TPU:0, one launch (start us, length us, event | category | flops | bytes accessed | tf_op | source)
XLA Modules:
  0.0 532.5 jit_solution(4455456975666470108)
XLA Ops:
  2.5 2.5 collective-permute-start.10
  13.7 1.9 subtract_convert_fusion
  15.8 1.6 collective-permute-start.1
  17.5 1.6 collective-permute-start.6
  19.1 5.3 %fusion.35 = (f32[2048,32]{1,0:T(8,128)S(1)}, f32[2048,32]{1,0:T(8,128)S(1)}, f32[2048,32]{1,0:T(8,128)}) fusion(f32[32]{0:T(128)S(1)} %negate_power_fusion, f32[2048]{0:T(1024)S(1)} %get-tuple-element.116), kind=kLoop, calls=%fused_computation.99 | loop fusion | flops 131072 | bytes 794752 | tf_op jit(solution)/shard_map/neg | solution.py:683
  24.5 4.2 pad_maximum_fusion.1
  28.8 4.1 collective-permute-done.6.refs_5_
  34.0 13.5 %collective-permute-done.7.refs_6_ = bf16[4,96,640]{2,1,0:T(8,128)(2,1)S(1)} collective-permute-done((bf16[4,96,640]{2,1,0:T(8,128)(2,1)}, bf16[4,96,640]{2,1,0:T(8,128)(2,1)S(1)}, u32[]{:S(2)}, u32[]{:S(2)}) %collective-permute-start.7) | collective-permute-done | bytes 491552 | tf_op jit(solution)/shard_map/ppermute | solution.py:503
  49.3 11.9 %collective-permute-done.8.refs_7_ = bf16[4,96,640]{2,1,0:T(8,128)(2,1)} collective-permute-done((bf16[4,96,640]{2,1,0:T(8,128)(2,1)S(1)}, bf16[4,96,640]{2,1,0:T(8,128)(2,1)}, u32[]{:S(2)}, u32[]{:S(2)}) %collective-permute-start.8) | collective-permute-done | bytes 491552 | tf_op jit(solution)/shard_map/ppermute | solution.py:503
  61.4 8.5 %collective-permute-done.13 = bf16[4,16,128]{2,1,0:T(8,128)(2,1)S(1)} collective-permute-done((bf16[4,16,128]{2,1,0:T(8,128)(2,1)S(1)}, bf16[4,16,128]{2,1,0:T(8,128)(2,1)S(1)}, u32[]{:S(2)}, u32[]{:S(2)}) %collective-permute-start.13) | collective-permute-done | bytes 16416 | tf_op jit(solution)/shard_map/ppermute | solution.py:503
  72.6 2.8 collective-permute-done.14
  76.7 2.1 collective-permute-done.16.refs_2_
  79.9 27.9 %attn_fwd.1 = (bf16[4,256,1536]{2,1,0:T(8,128)(2,1)}, bf16[4,256,384]{2,1,0:T(8,128)(2,1)}, bf16[6,1024,128]{2,1,0:T(8,128)(2,1)}, bf16[2,1024,128]{2,1,0:T(8,12...) custom-call(s32[16]{0:T(128)} %add.404.place_ref, bf16[256,1536]{1,0:T(8,128)(2,1)} %bitcast.182, ...), custom_call_target="tpu_custom_call" | custom-call | flops 20000000000 | bytes 20000000 | tf_op jit(solution)/shard_map/attn_fwd/pallas_call | solution.py:186
  109.8 37.5 %wo.1 = bf16[4,96,1536]{2,1,0:T(8,128)(2,1)} custom-call(s32[4]{0:T(128)} %copy-done.49, bf16[96,1536]{1,0:T(8,128)(2,1)} %refs_0_, bf16[96,1536]{1,0:T(8,128)(2,1)} %copy-done.18, bf16[96,1536]{1,0:T(8,128)(2,1)} %copy-done.19, bf16[96,1536]{1,0:T(8,128)(2,1)} %copy-done.20), custom_call_target="tpu_custom_call" | custom-call | bytes 2359296 | tf_op jit(solution)/shard_map/wo/pallas_call | solution.py:604
  147.4 2.2 convolution_convert_fusion.4
  158.7 13.8 %collective-permute-done.48 = s32[4,256]{1,0:T(4,128)S(1)} collective-permute-done((s32[4,256]{1,0:T(4,128)S(1)}, s32[4,256]{1,0:T(4,128)S(1)}, u32[]{:S(2)}, u32[]{:S(2)}) %collective-permute-start.48) | collective-permute-done | bytes 4128 | tf_op jit(solution)/shard_map/ppermute | solution.py:498
  179.7 6.6 %collective-permute-done.41.refs_22_ = bf16[256,768]{1,0:T(8,128)(2,1)} collective-permute-done((bf16[256,768]{1,0:T(8,128)(2,1)}, bf16[256,768]{1,0:T(8,128)(2,1)}, u32[]{:S(2)}, u32[]{:S(2)}) %collective-permute-start.41) | collective-permute-done | bytes 393248 | tf_op jit(solution)/shard_map/ppermute | solution.py:498
  190.0 2.8 multiply_reduce_fusion.2
  192.7 2.9 collective-permute-done.39.refs_20_
  196.2 2.1 collective-permute-done.35.refs_16_
  199.9 5.5 %collective-permute-done.45.refs_26_ = bf16[256,768]{1,0:T(8,128)(2,1)S(1)} collective-permute-done((bf16[256,768]{1,0:T(8,128)(2,1)}, bf16[256,768]{1,0:T(8,128)(2,1)S(1)}, u32[]{:S(2)}, u32[]{:S(2)}) %collective-permute-start.45) | collective-permute-done | bytes 393248 | tf_op jit(solution)/shard_map/ppermute | solution.py:498
  213.3 6.5 %collective-permute-done.28.refs_8_ = bf16[256,768]{1,0:T(8,128)(2,1)S(1)} collective-permute-done((bf16[256,768]{1,0:T(8,128)(2,1)S(1)}, bf16[256,768]{1,0:T(8,128)(2,1)S(1)}, u32[]{:S(2)}, u32[]{:S(2)}) %collective-permute-start.28) | collective-permute-done | bytes 393248 | tf_op jit(solution)/shard_map/ppermute | solution.py:498
  221.9 6.3 %collective-permute-done.22.refs_2_ = bf16[256,768]{1,0:T(8,128)(2,1)} collective-permute-done((bf16[256,768]{1,0:T(8,128)(2,1)S(1)}, bf16[256,768]{1,0:T(8,128)(2,1)}, u32[]{:S(2)}, u32[]{:S(2)}) %collective-permute-start.22) | collective-permute-done | bytes 393248 | tf_op jit(solution)/shard_map/ppermute | solution.py:498
  231.5 4.7 collective-permute-done.32.refs_12_
  236.3 2.6 collective-permute-done.30.refs_10_
  241.9 32.8 %experts.1 = (bf16[4,256,1536]{2,1,0:T(8,128)(2,1)}, bf16[4,256,1536]{2,1,0:T(8,128)(2,1)}, bf16[4,256,1536]{2,1,0:T(8,128)(2,1)}, bf16[4,256,1536]{2,1,0:T(8,12...) custom-call(s32[1]{0:T(128)} %bitcast.27.e_ref, ...), custom_call_target="tpu_custom_call" | custom-call | flops 30000001024 | bytes 30000000 | tf_op jit(solution)/shard_map/experts/pallas_call | solution.py:481
  276.0 4.7 convolution_convert_fusion.3
  280.7 3.0 collective-permute-start.86
  283.7 2.3 convolution_convert_fusion.2
  286.0 2.2 convolution_convert_fusion.1
  288.3 2.7 fusion.23
  296.1 7.0 %collective-permute-done.55 = bf16[256,768]{1,0:T(8,128)(2,1)S(1)} collective-permute-done((bf16[256,768]{1,0:T(8,128)(2,1)S(1)}, bf16[256,768]{1,0:T(8,128)(2,1)S(1)}, u32[]{:S(2)}, u32[]{:S(2)}) %collective-permute-start.55) | collective-permute-done | bytes 393248 | tf_op jit(solution)/shard_map/ppermute | solution.py:498
  306.5 5.1 collective-permute-done.57
  311.6 2.5 collective-permute-start.89
  314.0 6.0 %collective-permute-done.56 = bf16[256,768]{1,0:T(8,128)(2,1)S(1)} collective-permute-done((bf16[256,768]{1,0:T(8,128)(2,1)S(1)}, bf16[256,768]{1,0:T(8,128)(2,1)S(1)}, u32[]{:S(2)}, u32[]{:S(2)}) %collective-permute-start.56) | collective-permute-done | bytes 393248 | tf_op jit(solution)/shard_map/ppermute | solution.py:498
  321.8 1.7 fusion.54
  325.1 2.5 collective-permute-start.92
  328.3 10.6 %collective-permute-done.92 = bf16[512,384]{1,0:T(8,128)(2,1)S(1)} collective-permute-done((bf16[512,384]{1,0:T(8,128)(2,1)S(1)}, bf16[512,384]{1,0:T(8,128)(2,1)S(1)}, u32[]{:S(2)}, u32[]{:S(2)}) %collective-permute-start.92) | collective-permute-done | bytes 393248 | tf_op jit(solution)/shard_map/ppermute | solution.py:503
  339.8 1.8 collective-permute-done.61.refs_2_
  341.6 5.8 %collective-permute-done.87 = bf16[384,512]{1,0:T(8,128)(2,1)S(1)} collective-permute-done((bf16[384,512]{1,0:T(8,128)(2,1)S(1)}, bf16[384,512]{1,0:T(8,128)(2,1)S(1)}, u32[]{:S(2)}, u32[]{:S(2)}) %collective-permute-start.87) | collective-permute-done | bytes 393248 | tf_op jit(solution)/shard_map/ppermute | solution.py:503
  348.2 7.6 %collective-permute-done.90 = bf16[384,512]{1,0:T(8,128)(2,1)S(1)} collective-permute-done((bf16[384,512]{1,0:T(8,128)(2,1)S(1)}, bf16[384,512]{1,0:T(8,128)(2,1)S(1)}, u32[]{:S(2)}, u32[]{:S(2)}) %collective-permute-start.90) | collective-permute-done | bytes 393248 | tf_op jit(solution)/shard_map/ppermute | solution.py:503
  357.3 6.9 %collective-permute-done.93 = bf16[512,384]{1,0:T(8,128)(2,1)S(1)} collective-permute-done((bf16[512,384]{1,0:T(8,128)(2,1)S(1)}, bf16[512,384]{1,0:T(8,128)(2,1)S(1)}, u32[]{:S(2)}, u32[]{:S(2)}) %collective-permute-start.93) | collective-permute-done | bytes 393248 | tf_op jit(solution)/shard_map/ppermute | solution.py:503
  365.8 6.9 %collective-permute-done.88 = bf16[384,512]{1,0:T(8,128)(2,1)S(1)} collective-permute-done((bf16[384,512]{1,0:T(8,128)(2,1)S(1)}, bf16[384,512]{1,0:T(8,128)(2,1)S(1)}, u32[]{:S(2)}, u32[]{:S(2)}) %collective-permute-start.88) | collective-permute-done | bytes 393248 | tf_op jit(solution)/shard_map/ppermute | solution.py:503
  373.7 1.7 fusion.8
  376.4 32.7 %attn_bwd.1 = bf16[4,256,640]{2,1,0:T(8,128)(2,1)} custom-call(bf16[256,1536]{1,0:T(8,128)(2,1)} %copy-done.14, bf16[256,1536]{1,0:T(8,128)(2,1)} %copy-done.56, bf16[256,1536]{1,0:T(8,128)(2,1)} %copy-done.55, bf16[256,1536]{1,0:T(8,128)(2,1)} %copy-done.57, bf16[384,1536]{1,0:T(8,128)(2,1)} %bitcast.180, bf16[4,256,384]{2,1,0:T(8,128)(2,1)} %get-tuple-element.32.refs_5_, ...), custom_call_target="tpu_custom_call" | custom-call | flops 24999999488 | bytes 20000000 | tf_op jit(solution)/shard_map/attn_bwd/pallas_call | solution.py:320
  409.1 5.1 bitcast_convert_fusion
  414.6 2.9 convolution_convert_fusion
  417.9 2.3 add_bitcast_fusion.3
  420.3 6.7 %collective-permute-done.75 = bf16[4,96,640]{2,1,0:T(8,128)(2,1)S(1)} collective-permute-done((bf16[4,96,640]{2,1,0:T(8,128)(2,1)S(1)}, bf16[4,96,640]{2,1,0:T(8,128)(2,1)S(1)}, u32[]{:S(2)}, u32[]{:S(2)}) %collective-permute-start.75) | collective-permute-done | bytes 491552 | tf_op jit(solution)/shard_map/ppermute | solution.py:503
  427.2 4.1 collective-permute-done.83
  431.6 18.9 %collective-permute-done.84 = bf16[96,1536]{1,0:T(8,128)(2,1)S(1)} collective-permute-done((bf16[96,1536]{1,0:T(8,128)(2,1)S(1)}, bf16[96,1536]{1,0:T(8,128)(2,1)S(1)}, u32[]{:S(2)}, u32[]{:S(2)}) %collective-permute-start.84) | collective-permute-done | bytes 294944 | tf_op jit(solution)/shard_map/ppermute | solution.py:503
  452.9 5.0 collective-permute-done.85
  458.7 4.6 collective-permute-done.77
  468.5 6.7 %collective-permute-done.74 = f32[10,1536]{1,0:T(8,128)S(1)} collective-permute-done((f32[10,1536]{1,0:T(8,128)S(1)}, f32[10,1536]{1,0:T(8,128)S(1)}, u32[]{:S(2)}, u32[]{:S(2)}) %collective-permute-start.74) | collective-permute-done | bytes 61472 | tf_op jit(solution)/shard_map/ppermute | solution.py:498
  476.2 3.7 all-to-all-start
  479.9 3.4 fusion.30
  483.3 3.1 all-to-all-done
  489.8 4.8 fusion.26
  500.1 2.5 collective-permute-done.81
  502.6 2.7 collective-permute-done.80
  506.1 2.5 gather_fusion.2
  513.0 1.7 collective-permute-start.64
  519.7 3.2 collective-permute-done.65
  523.5 7.4 %collective-permute-done.64 = bf16[256,768]{1,0:T(8,128)(2,1)S(1)} collective-permute-done((bf16[256,768]{1,0:T(8,128)(2,1)S(1)}, bf16[256,768]{1,0:T(8,128)(2,1)S(1)}, u32[]{:S(2)}, u32[]{:S(2)}) %collective-permute-start.64) | collective-permute-done | bytes 393248 | tf_op jit(solution)/shard_map/ppermute | solution.py:498
  (424 shorter events, 109.1 us)
Async XLA Ops:
  2.1 46.5 %collective-permute-start.9 = (bf16[16,128]{1,0:T(8,128)(2,1)}, bf16[16,128]{1,0:T(8,128)(2,1)S(1)}, u32[]{:S(2)}, u32[]{:S(2)}) collective-permute-start(bf16[16,128]{1,0:T(8,128)(2,1)} %fusion.46), channel_id=1, source_target_pairs={{0,4},{4,0},{8,12},{12,8},{1,5},{5,1},{9,13},{13,9},{2,6},{6,2},{1... | collective-permute-start | bytes 12296 | tf_op jit(solution)/shard_map/ppermute | solution.py:498
  2.5 46.2 %collective-permute-start.10 = (bf16[16,128]{1,0:T(8,128)(2,1)}, bf16[16,128]{1,0:T(8,128)(2,1)S(1)}, u32[]{:S(2)}, u32[]{:S(2)}) collective-permute-start(bf16[16,128]{1,0:T(8,128)(2,1)} %fusion.46), channel_id=1, source_target_pairs={{0,8},{4,12},{8,0},{12,4},{1,9},{5,13},{9,1},{13,5},{2,10},{6,14},... | collective-permute-start | bytes 12296 | tf_op jit(solution)/shard_map/ppermute | solution.py:498
  15.7 33.0 %collective-permute-start.11 = (bf16[16,128]{1,0:T(8,128)(2,1)}, bf16[16,128]{1,0:T(8,128)(2,1)S(1)}, u32[]{:S(2)}, u32[]{:S(2)}) collective-permute-start(bf16[16,128]{1,0:T(8,128)(2,1)} %fusion.46), channel_id=1, source_target_pairs={{0,12},{4,8},{8,4},{12,0},{1,13},{5,9},{9,5},{13,1},{2,14},{6,10},... | collective-permute-start | bytes 12296 | tf_op jit(solution)/shard_map/ppermute | solution.py:498
  15.8 33.0 %collective-permute-start.1 = (bf16[256,1536]{1,0:T(8,128)(2,1)S(1)}, bf16[256,1536]{1,0:T(8,128)(2,1)}, u32[]{:S(2)}, u32[]{:S(2)}) collective-permute-start(bf16[256,1536]{1,0:T(8,128)(2,1)S(1)} %bitcast.183), channel_id=1, source_target_pairs={{0,8},{4,12},{8,0},{12,4},{1,9},{5,13},{9,1},{13,5},{2,10},{6,14},... | collective-permute-start | bytes 2359304 | tf_op jit(solution)/shard_map/ppermute | solution.py:498
  17.5 15.3 %collective-permute-start.6 = (bf16[4,96,640]{2,1,0:T(8,128)(2,1)S(1)}, bf16[4,96,640]{2,1,0:T(8,128)(2,1)}, u32[]{:S(2)}, u32[]{:S(2)}) collective-permute-start(bf16[4,96,640]{2,1,0:T(8,128)(2,1)S(1)} %pad_maximum_fusion.3.refs_4_), channel_id=1, source_target_pairs={{0,1},{1,2},{2,3},{3,0},{4,5},{5,6},{6,7},{7,4},{8,9},{9,10},{10,1... | collective-permute-start | bytes 1474568 | tf_op jit(solution)/shard_map/ppermute | solution.py:503
  32.9 14.6 %collective-permute-start.7 = (bf16[4,96,640]{2,1,0:T(8,128)(2,1)}, bf16[4,96,640]{2,1,0:T(8,128)(2,1)S(1)}, u32[]{:S(2)}, u32[]{:S(2)}) collective-permute-start(bf16[4,96,640]{2,1,0:T(8,128)(2,1)} %collective-permute-done.6.refs_5_), channel_id=1, source_target_pairs={{0,1},{1,2},{2,3},{3,0},{4,5},{5,6},{6,7},{7,4},{8,9},{9,10},{10,1... | collective-permute-start | bytes 1474568 | tf_op jit(solution)/shard_map/ppermute | solution.py:503
  47.5 13.7 %collective-permute-start.8 = (bf16[4,96,640]{2,1,0:T(8,128)(2,1)S(1)}, bf16[4,96,640]{2,1,0:T(8,128)(2,1)}, u32[]{:S(2)}, u32[]{:S(2)}) collective-permute-start(bf16[4,96,640]{2,1,0:T(8,128)(2,1)S(1)} %collective-permute-done.7.refs_6_), channel_id=1, source_target_pairs={{0,1},{1,2},{2,3},{3,0},{4,5},{5,6},{6,7},{7,4},{8,9},{9,10},{10,1... | collective-permute-start | bytes 1474568 | tf_op jit(solution)/shard_map/ppermute | solution.py:503
  48.6 30.4 %collective-permute-start = (bf16[256,1536]{1,0:T(8,128)(2,1)S(1)}, bf16[256,1536]{1,0:T(8,128)(2,1)S(1)}, u32[]{:S(2)}, u32[]{:S(2)}) collective-permute-start(bf16[256,1536]{1,0:T(8,128)(2,1)S(1)} %bitcast.184), channel_id=1, source_target_pairs={{0,4},{4,0},{8,12},{12,8},{1,5},{5,1},{9,13},{13,9},{2,6},{6,2},{1... | collective-permute-start | bytes 2359304 | tf_op jit(solution)/shard_map/ppermute | solution.py:498
  48.7 12.6 %collective-permute-start.12 = (bf16[4,16,128]{2,1,0:T(8,128)(2,1)S(1)}, bf16[4,16,128]{2,1,0:T(8,128)(2,1)S(1)}, u32[]{:S(2)}, u32[]{:S(2)}) collective-permute-start(bf16[4,16,128]{2,1,0:T(8,128)(2,1)S(1)} %get-tuple-element.110), channel_id=1, source_target_pairs={{0,1},{1,2},{2,3},{3,0},{4,5},{5,6},{6,7},{7,4},{8,9},{9,10},{10,1... | collective-permute-start | bytes 49160 | tf_op jit(solution)/shard_map/ppermute | solution.py:503
  48.8 30.2 %collective-permute-start.2 = (bf16[256,1536]{1,0:T(8,128)(2,1)}, bf16[256,1536]{1,0:T(8,128)(2,1)}, u32[]{:S(2)}, u32[]{:S(2)}) collective-permute-start(bf16[256,1536]{1,0:T(8,128)(2,1)} %collective-permute-done.1.refs_2_), channel_id=1, source_target_pairs={{0,4},{4,0},{8,12},{12,8},{1,5},{5,1},{9,13},{13,9},{2,6},{6,2},{1... | collective-permute-start | bytes 2359304 | tf_op jit(solution)/shard_map/ppermute | solution.py:498
  78.8 30.3 %collective-permute-start.17 = (bf16[96,1536]{1,0:T(8,128)(2,1)S(1)}, bf16[96,1536]{1,0:T(8,128)(2,1)S(1)}, u32[]{:S(2)}, u32[]{:S(2)}) collective-permute-start(bf16[96,1536]{1,0:T(8,128)(2,1)S(1)} %collective-permute-done.16.refs_2_), channel_id=1, source_target_pairs={{0,1},{1,2},{2,3},{3,0},{4,5},{5,6},{6,7},{7,4},{8,9},{9,10},{10,1... | collective-permute-start | bytes 884744 | tf_op jit(solution)/shard_map/ppermute | solution.py:503
  152.0 37.5 %collective-permute-start.18 = (bf16[256,1536]{1,0:T(8,128)(2,1)S(1)}, bf16[256,1536]{1,0:T(8,128)(2,1)}, u32[]{:S(2)}, u32[]{:S(2)}) collective-permute-start(bf16[256,1536]{1,0:T(8,128)(2,1)S(1)} %slice.292), channel_id=1, source_target_pairs={{0,4},{4,0},{8,12},{12,8},{1,5},{5,1},{9,13},{13,9},{2,6},{6,2},{1... | collective-permute-start | bytes 2359304 | tf_op jit(solution)/shard_map/ppermute | solution.py:498
  153.0 36.4 %collective-permute-start.20 = (bf16[256,1536]{1,0:T(8,128)(2,1)S(1)}, bf16[256,1536]{1,0:T(8,128)(2,1)}, u32[]{:S(2)}, u32[]{:S(2)}) collective-permute-start(bf16[256,1536]{1,0:T(8,128)(2,1)S(1)} %add_convert_fusion.7), channel_id=1, source_target_pairs={{0,8},{4,12},{8,0},{12,4},{1,9},{5,13},{9,1},{13,5},{2,10},{6,14},... | collective-permute-start | bytes 2359304 | tf_op jit(solution)/shard_map/ppermute | solution.py:498
  155.0 17.4 %collective-permute-start.48 = (s32[4,256]{1,0:T(4,128)S(1)}, s32[4,256]{1,0:T(4,128)S(1)}, u32[]{:S(2)}, u32[]{:S(2)}) collective-permute-start(s32[4,256]{1,0:T(4,128)S(1)} %bitcast.230), channel_id=1, source_target_pairs={{0,8},{4,12},{8,0},{12,4},{1,9},{5,13},{9,1},{13,5},{2,10},{6,14},... | collective-permute-start | bytes 12296 | tf_op jit(solution)/shard_map/ppermute | solution.py:498
  156.6 15.9 %collective-permute-start.47 = (s32[4,256]{1,0:T(4,128)S(1)}, s32[4,256]{1,0:T(4,128)S(1)}, u32[]{:S(2)}, u32[]{:S(2)}) collective-permute-start(s32[4,256]{1,0:T(4,128)S(1)} %bitcast.231), channel_id=1, source_target_pairs={{0,4},{4,0},{8,12},{12,8},{1,5},{5,1},{9,13},{13,9},{2,6},{6,2},{1... | collective-permute-start | bytes 12296 | tf_op jit(solution)/shard_map/ppermute | solution.py:498
  157.2 17.2 %collective-permute-start.52 = (s32[4,256]{1,0:T(4,128)S(1)}, s32[4,256]{1,0:T(4,128)S(1)}, u32[]{:S(2)}, u32[]{:S(2)}) collective-permute-start(s32[4,256]{1,0:T(4,128)S(1)} %collective-permute-done.50), channel_id=1, source_target_pairs={{0,8},{4,12},{8,0},{12,4},{1,9},{5,13},{9,1},{13,5},{2,10},{6,14},... | collective-permute-start | bytes 12296 | tf_op jit(solution)/shard_map/ppermute | solution.py:498
  174.5 11.8 %collective-permute-start.41 = (bf16[256,768]{1,0:T(8,128)(2,1)}, bf16[256,768]{1,0:T(8,128)(2,1)}, u32[]{:S(2)}, u32[]{:S(2)}) collective-permute-start(bf16[256,768]{1,0:T(8,128)(2,1)} %get-tuple-element.85), channel_id=1, source_target_pairs={{0,8},{4,12},{8,0},{12,4},{1,9},{5,13},{9,1},{13,5},{2,10},{6,14},... | collective-permute-start | bytes 1179656 | tf_op jit(solution)/shard_map/ppermute | solution.py:498
  175.7 12.3 %collective-permute-start.37 = (bf16[256,768]{1,0:T(8,128)(2,1)}, bf16[256,768]{1,0:T(8,128)(2,1)}, u32[]{:S(2)}, u32[]{:S(2)}) collective-permute-start(bf16[256,768]{1,0:T(8,128)(2,1)} %get-tuple-element.85), channel_id=1, source_target_pairs={{0,16},{16,0},{1,17},{17,1},{2,18},{18,2},{3,19},{19,3},{4,20},{20... | collective-permute-start | bytes 1179656 | tf_op jit(solution)/shard_map/ppermute | solution.py:498
  177.7 17.9 %collective-permute-start.39 = (bf16[256,768]{1,0:T(8,128)(2,1)S(1)}, bf16[256,768]{1,0:T(8,128)(2,1)}, u32[]{:S(2)}, u32[]{:S(2)}) collective-permute-start(bf16[256,768]{1,0:T(8,128)(2,1)S(1)} %get-tuple-element.86), channel_id=1, source_target_pairs={{0,16},{16,0},{1,17},{17,1},{2,18},{18,2},{3,19},{19,3},{4,20},{20... | collective-permute-start | bytes 1179656 | tf_op jit(solution)/shard_map/ppermute | solution.py:498
  186.3 12.0 %collective-permute-start.35 = (bf16[256,768]{1,0:T(8,128)(2,1)S(1)}, bf16[256,768]{1,0:T(8,128)(2,1)S(1)}, u32[]{:S(2)}, u32[]{:S(2)}) collective-permute-start(bf16[256,768]{1,0:T(8,128)(2,1)S(1)} %get-tuple-element.86), channel_id=1, source_target_pairs={{0,8},{4,12},{8,0},{12,4},{1,9},{5,13},{9,1},{13,5},{2,10},{6,14},... | collective-permute-start | bytes 1179656 | tf_op jit(solution)/shard_map/ppermute | solution.py:498
  188.0 17.4 %collective-permute-start.45 = (bf16[256,768]{1,0:T(8,128)(2,1)}, bf16[256,768]{1,0:T(8,128)(2,1)S(1)}, u32[]{:S(2)}, u32[]{:S(2)}) collective-permute-start(bf16[256,768]{1,0:T(8,128)(2,1)} %collective-permute-done.37.refs_18_), channel_id=1, source_target_pairs={{0,8},{4,12},{8,0},{12,4},{1,9},{5,13},{9,1},{13,5},{2,10},{6,14},... | collective-permute-start | bytes 1179656 | tf_op jit(solution)/shard_map/ppermute | solution.py:498
  189.5 16.0 %collective-permute-start.38 = (bf16[256,768]{1,0:T(8,128)(2,1)}, bf16[256,768]{1,0:T(8,128)(2,1)S(1)}, u32[]{:S(2)}, u32[]{:S(2)}) collective-permute-start(bf16[256,768]{1,0:T(8,128)(2,1)} %collective-permute-done.37.refs_18_), channel_id=1, source_target_pairs={{0,4},{4,0},{8,12},{12,8},{1,5},{5,1},{9,13},{13,9},{2,6},{6,2},{1... | collective-permute-start | bytes 1179656 | tf_op jit(solution)/shard_map/ppermute | solution.py:498
  195.6 15.2 %collective-permute-start.34 = (bf16[256,1536]{1,0:T(8,128)(2,1)S(1)}, bf16[256,1536]{1,0:T(8,128)(2,1)S(1)}, u32[]{:S(2)}, u32[]{:S(2)}) collective-permute-start(bf16[256,1536]{1,0:T(8,128)(2,1)S(1)} %bitcast.187), channel_id=1, source_target_pairs={{0,4},{4,0},{8,12},{12,8},{1,5},{5,1},{9,13},{13,9},{2,6},{6,2},{1... | collective-permute-start | bytes 2359304 | tf_op jit(solution)/shard_map/ppermute | solution.py:498
  207.8 12.0 %collective-permute-start.28 = (bf16[256,768]{1,0:T(8,128)(2,1)S(1)}, bf16[256,768]{1,0:T(8,128)(2,1)S(1)}, u32[]{:S(2)}, u32[]{:S(2)}) collective-permute-start(bf16[256,768]{1,0:T(8,128)(2,1)S(1)} %get-tuple-element.87), channel_id=1, source_target_pairs={{0,8},{4,12},{8,0},{12,4},{1,9},{5,13},{9,1},{13,5},{2,10},{6,14},... | collective-permute-start | bytes 1179656 | tf_op jit(solution)/shard_map/ppermute | solution.py:498
  209.3 12.1 %collective-permute-start.24 = (bf16[256,768]{1,0:T(8,128)(2,1)S(1)}, bf16[256,768]{1,0:T(8,128)(2,1)}, u32[]{:S(2)}, u32[]{:S(2)}) collective-permute-start(bf16[256,768]{1,0:T(8,128)(2,1)S(1)} %get-tuple-element.87), channel_id=1, source_target_pairs={{0,16},{16,0},{1,17},{17,1},{2,18},{18,2},{3,19},{19,3},{4,20},{20... | collective-permute-start | bytes 1179656 | tf_op jit(solution)/shard_map/ppermute | solution.py:498
  210.8 20.1 %collective-permute-start.21 = (bf16[256,1536]{1,0:T(8,128)(2,1)S(1)}, bf16[256,1536]{1,0:T(8,128)(2,1)S(1)}, u32[]{:S(2)}, u32[]{:S(2)}) collective-permute-start(bf16[256,1536]{1,0:T(8,128)(2,1)S(1)} %multiply_convert_fusion.refs_0_), channel_id=1, source_target_pairs={{0,4},{4,0},{8,12},{12,8},{1,5},{5,1},{9,13},{13,9},{2,6},{6,2},{1... | collective-permute-start | bytes 2359304 | tf_op jit(solution)/shard_map/ppermute | solution.py:498
  210.9 17.4 %collective-permute-start.22 = (bf16[256,768]{1,0:T(8,128)(2,1)S(1)}, bf16[256,768]{1,0:T(8,128)(2,1)}, u32[]{:S(2)}, u32[]{:S(2)}) collective-permute-start(bf16[256,768]{1,0:T(8,128)(2,1)S(1)} %get-tuple-element.88), channel_id=1, source_target_pairs={{0,8},{4,12},{8,0},{12,4},{1,9},{5,13},{9,1},{13,5},{2,10},{6,14},... | collective-permute-start | bytes 1179656 | tf_op jit(solution)/shard_map/ppermute | solution.py:498
  212.7 18.2 %collective-permute-start.26 = (bf16[256,768]{1,0:T(8,128)(2,1)S(1)}, bf16[256,768]{1,0:T(8,128)(2,1)}, u32[]{:S(2)}, u32[]{:S(2)}) collective-permute-start(bf16[256,768]{1,0:T(8,128)(2,1)S(1)} %get-tuple-element.88), channel_id=1, source_target_pairs={{0,16},{16,0},{1,17},{17,1},{2,18},{18,2},{3,19},{19,3},{4,20},{20... | collective-permute-start | bytes 1179656 | tf_op jit(solution)/shard_map/ppermute | solution.py:498
  221.4 14.9 %collective-permute-start.32 = (bf16[256,768]{1,0:T(8,128)(2,1)}, bf16[256,768]{1,0:T(8,128)(2,1)}, u32[]{:S(2)}, u32[]{:S(2)}) collective-permute-start(bf16[256,768]{1,0:T(8,128)(2,1)} %collective-permute-done.24.refs_4_), channel_id=1, source_target_pairs={{0,8},{4,12},{8,0},{12,4},{1,9},{5,13},{9,1},{13,5},{2,10},{6,14},... | collective-permute-start | bytes 1179656 | tf_op jit(solution)/shard_map/ppermute | solution.py:498
  274.7 13.6 %collective-permute-start.54 = (bf16[4,256,1536]{2,1,0:T(8,128)(2,1)}, bf16[4,256,1536]{2,1,0:T(8,128)(2,1)}, u32[]{:S(2)}, u32[]{:S(2)}) collective-permute-start(bf16[4,256,1536]{2,1,0:T(8,128)(2,1)} %get-tuple-element.37), channel_id=1, source_target_pairs={{0,4},{4,0},{8,12},{12,8},{1,5},{5,1},{9,13},{13,9},{2,6},{6,2},{1... | collective-permute-start | bytes 9437192 | tf_op jit(solution)/shard_map/ppermute | solution.py:498
  280.7 46.9 %collective-permute-start.86 = (bf16[384,512]{1,0:T(8,128)(2,1)S(1)}, bf16[384,512]{1,0:T(8,128)(2,1)S(1)}, u32[]{:S(2)}, u32[]{:S(2)}) collective-permute-start(bf16[384,512]{1,0:T(8,128)(2,1)S(1)} %constant_dynamic-slice_fusion.2), channel_id=1, source_target_pairs={{0,1},{1,2},{2,3},{3,0},{4,5},{5,6},{6,7},{7,4},{8,9},{9,10},{10,1... | collective-permute-start | bytes 1179656 | tf_op jit(solution)/shard_map/ppermute | solution.py:503
  291.1 12.1 %collective-permute-start.55 = (bf16[256,768]{1,0:T(8,128)(2,1)S(1)}, bf16[256,768]{1,0:T(8,128)(2,1)S(1)}, u32[]{:S(2)}, u32[]{:S(2)}) collective-permute-start(bf16[256,768]{1,0:T(8,128)(2,1)S(1)} %get-tuple-element.83), channel_id=1, source_target_pairs={{0,16},{16,0},{1,17},{17,1},{2,18},{18,2},{3,19},{19,3},{4,20},{20... | collective-permute-start | bytes 1179656 | tf_op jit(solution)/shard_map/ppermute | solution.py:498
  292.6 12.2 %collective-permute-start.59 = (bf16[256,768]{1,0:T(8,128)(2,1)S(1)}, bf16[256,768]{1,0:T(8,128)(2,1)S(1)}, u32[]{:S(2)}, u32[]{:S(2)}) collective-permute-start(bf16[256,768]{1,0:T(8,128)(2,1)S(1)} %get-tuple-element.84), channel_id=1, source_target_pairs={{0,8},{4,12},{8,0},{12,4},{1,9},{5,13},{9,1},{13,5},{2,10},{6,14},... | collective-permute-start | bytes 1179656 | tf_op jit(solution)/shard_map/ppermute | solution.py:498
  294.9 16.6 %collective-permute-start.57 = (bf16[256,768]{1,0:T(8,128)(2,1)S(1)}, bf16[256,768]{1,0:T(8,128)(2,1)S(1)}, u32[]{:S(2)}, u32[]{:S(2)}) collective-permute-start(bf16[256,768]{1,0:T(8,128)(2,1)S(1)} %slice.306), channel_id=1, source_target_pairs={{0,16},{16,0},{1,17},{17,1},{2,18},{18,2},{3,19},{19,3},{4,20},{20... | collective-permute-start | bytes 1179656 | tf_op jit(solution)/shard_map/ppermute | solution.py:498
  295.6 18.5 %collective-permute-start.58 = (bf16[256,768]{1,0:T(8,128)(2,1)S(1)}, bf16[256,768]{1,0:T(8,128)(2,1)S(1)}, u32[]{:S(2)}, u32[]{:S(2)}) collective-permute-start(bf16[256,768]{1,0:T(8,128)(2,1)S(1)} %slice.308), channel_id=1, source_target_pairs={{0,8},{4,12},{8,0},{12,4},{1,9},{5,13},{9,1},{13,5},{2,10},{6,14},... | collective-permute-start | bytes 1179656 | tf_op jit(solution)/shard_map/ppermute | solution.py:498
  303.2 16.8 %collective-permute-start.56 = (bf16[256,768]{1,0:T(8,128)(2,1)S(1)}, bf16[256,768]{1,0:T(8,128)(2,1)S(1)}, u32[]{:S(2)}, u32[]{:S(2)}) collective-permute-start(bf16[256,768]{1,0:T(8,128)(2,1)S(1)} %add_convert_fusion.18), channel_id=1, source_target_pairs={{0,8},{4,12},{8,0},{12,4},{1,9},{5,13},{9,1},{13,5},{2,10},{6,14},... | collective-permute-start | bytes 1179656 | tf_op jit(solution)/shard_map/ppermute | solution.py:498
  304.9 15.1 %collective-permute-start.60 = (bf16[256,768]{1,0:T(8,128)(2,1)S(1)}, bf16[256,768]{1,0:T(8,128)(2,1)S(1)}, u32[]{:S(2)}, u32[]{:S(2)}) collective-permute-start(bf16[256,768]{1,0:T(8,128)(2,1)S(1)} %add_convert_fusion.17), channel_id=1, source_target_pairs={{0,16},{16,0},{1,17},{17,1},{2,18},{18,2},{3,19},{19,3},{4,20},{20... | collective-permute-start | bytes 1179656 | tf_op jit(solution)/shard_map/ppermute | solution.py:498
  311.6 16.5 %collective-permute-start.89 = (bf16[384,512]{1,0:T(8,128)(2,1)S(1)}, bf16[384,512]{1,0:T(8,128)(2,1)S(1)}, u32[]{:S(2)}, u32[]{:S(2)}) collective-permute-start(bf16[384,512]{1,0:T(8,128)(2,1)S(1)} %constant_dynamic-slice_fusion.1), channel_id=1, source_target_pairs={{0,1},{1,2},{2,3},{3,0},{4,5},{5,6},{6,7},{7,4},{8,9},{9,10},{10,1... | collective-permute-start | bytes 1179656 | tf_op jit(solution)/shard_map/ppermute | solution.py:503
  323.5 18.1 %collective-permute-start.61 = (bf16[256,1536]{1,0:T(8,128)(2,1)S(1)}, bf16[256,1536]{1,0:T(8,128)(2,1)S(1)}, u32[]{:S(2)}, u32[]{:S(2)}) collective-permute-start(bf16[256,1536]{1,0:T(8,128)(2,1)S(1)} %get-tuple-element.58.refs_0_), channel_id=1, source_target_pairs={{0,8},{4,12},{8,0},{12,4},{1,9},{5,13},{9,1},{13,5},{2,10},{6,14},... | collective-permute-start | bytes 2359304 | tf_op jit(solution)/shard_map/ppermute | solution.py:498
  325.1 13.9 %collective-permute-start.92 = (bf16[512,384]{1,0:T(8,128)(2,1)S(1)}, bf16[512,384]{1,0:T(8,128)(2,1)S(1)}, u32[]{:S(2)}, u32[]{:S(2)}) collective-permute-start(bf16[512,384]{1,0:T(8,128)(2,1)S(1)} %constant_dynamic-slice_fusion), channel_id=1, source_target_pairs={{0,1},{1,2},{2,3},{3,0},{4,5},{5,6},{6,7},{7,4},{8,9},{9,10},{10,1... | collective-permute-start | bytes 1179656 | tf_op jit(solution)/shard_map/ppermute | solution.py:503
  327.7 19.7 %collective-permute-start.87 = (bf16[384,512]{1,0:T(8,128)(2,1)S(1)}, bf16[384,512]{1,0:T(8,128)(2,1)S(1)}, u32[]{:S(2)}, u32[]{:S(2)}) collective-permute-start(bf16[384,512]{1,0:T(8,128)(2,1)S(1)} %add_convert_fusion.14), channel_id=1, source_target_pairs={{0,1},{1,2},{2,3},{3,0},{4,5},{5,6},{6,7},{7,4},{8,9},{9,10},{10,1... | collective-permute-start | bytes 1179656 | tf_op jit(solution)/shard_map/ppermute | solution.py:503
  328.2 27.6 %collective-permute-start.90 = (bf16[384,512]{1,0:T(8,128)(2,1)S(1)}, bf16[384,512]{1,0:T(8,128)(2,1)S(1)}, u32[]{:S(2)}, u32[]{:S(2)}) collective-permute-start(bf16[384,512]{1,0:T(8,128)(2,1)S(1)} %add_convert_fusion.12), channel_id=1, source_target_pairs={{0,1},{1,2},{2,3},{3,0},{4,5},{5,6},{6,7},{7,4},{8,9},{9,10},{10,1... | collective-permute-start | bytes 1179656 | tf_op jit(solution)/shard_map/ppermute | solution.py:503
  339.1 25.2 %collective-permute-start.93 = (bf16[512,384]{1,0:T(8,128)(2,1)S(1)}, bf16[512,384]{1,0:T(8,128)(2,1)S(1)}, u32[]{:S(2)}, u32[]{:S(2)}) collective-permute-start(bf16[512,384]{1,0:T(8,128)(2,1)S(1)} %add_convert_fusion.10), channel_id=1, source_target_pairs={{0,1},{1,2},{2,3},{3,0},{4,5},{5,6},{6,7},{7,4},{8,9},{9,10},{10,1... | collective-permute-start | bytes 1179656 | tf_op jit(solution)/shard_map/ppermute | solution.py:503
  339.8 33.9 %collective-permute-start.69 = (bf16[256,1536]{1,0:T(8,128)(2,1)S(1)}, bf16[256,1536]{1,0:T(8,128)(2,1)S(1)}, u32[]{:S(2)}, u32[]{:S(2)}) collective-permute-start(bf16[256,1536]{1,0:T(8,128)(2,1)S(1)} %get-tuple-element.58.refs_0_), channel_id=1, source_target_pairs={{0,4},{4,0},{8,12},{12,8},{1,5},{5,1},{9,13},{13,9},{2,6},{6,2},{1... | collective-permute-start | bytes 2359304 | tf_op jit(solution)/shard_map/ppermute | solution.py:498
  341.6 32.1 %collective-permute-start.70 = (bf16[256,1536]{1,0:T(8,128)(2,1)S(1)}, bf16[256,1536]{1,0:T(8,128)(2,1)S(1)}, u32[]{:S(2)}, u32[]{:S(2)}) collective-permute-start(bf16[256,1536]{1,0:T(8,128)(2,1)S(1)} %collective-permute-done.61.refs_2_), channel_id=1, source_target_pairs={{0,4},{4,0},{8,12},{12,8},{1,5},{5,1},{9,13},{13,9},{2,6},{6,2},{1... | collective-permute-start | bytes 2359304 | tf_op jit(solution)/shard_map/ppermute | solution.py:498
  347.5 25.2 %collective-permute-start.88 = (bf16[384,512]{1,0:T(8,128)(2,1)S(1)}, bf16[384,512]{1,0:T(8,128)(2,1)S(1)}, u32[]{:S(2)}, u32[]{:S(2)}) collective-permute-start(bf16[384,512]{1,0:T(8,128)(2,1)S(1)} %add_convert_fusion.13), channel_id=1, source_target_pairs={{0,1},{1,2},{2,3},{3,0},{4,5},{5,6},{6,7},{7,4},{8,9},{9,10},{10,1... | collective-permute-start | bytes 1179656 | tf_op jit(solution)/shard_map/ppermute | solution.py:503
  356.7 61.2 %collective-permute-start.91 = (bf16[384,512]{1,0:T(8,128)(2,1)}, bf16[384,512]{1,0:T(8,128)(2,1)}, u32[]{:S(2)}, u32[]{:S(2)}) collective-permute-start(bf16[384,512]{1,0:T(8,128)(2,1)} %add_convert_fusion.11), channel_id=1, source_target_pairs={{0,1},{1,2},{2,3},{3,0},{4,5},{5,6},{6,7},{7,4},{8,9},{9,10},{10,1... | collective-permute-start | bytes 1179656 | tf_op jit(solution)/shard_map/ppermute | solution.py:503
  365.1 86.7 %collective-permute-start.94 = (bf16[512,384]{1,0:T(8,128)(2,1)}, bf16[512,384]{1,0:T(8,128)(2,1)S(1)}, u32[]{:S(2)}, u32[]{:S(2)}) collective-permute-start(bf16[512,384]{1,0:T(8,128)(2,1)} %add_convert_fusion.9), channel_id=1, source_target_pairs={{0,1},{1,2},{2,3},{3,0},{4,5},{5,6},{6,7},{7,4},{8,9},{9,10},{10,1... | collective-permute-start | bytes 1179656 | tf_op jit(solution)/shard_map/ppermute | solution.py:503
  375.5 42.2 %collective-permute-start.82 = (bf16[96,1536]{1,0:T(8,128)(2,1)S(1)}, bf16[96,1536]{1,0:T(8,128)(2,1)S(1)}, u32[]{:S(2)}, u32[]{:S(2)}) collective-permute-start(bf16[96,1536]{1,0:T(8,128)(2,1)S(1)} %constant_dynamic-slice_fusion.3), channel_id=1, source_target_pairs={{0,1},{1,2},{2,3},{3,0},{4,5},{5,6},{6,7},{7,4},{8,9},{9,10},{10,1... | collective-permute-start | bytes 884744 | tf_op jit(solution)/shard_map/ppermute | solution.py:503
  414.2 12.8 %collective-permute-start.75 = (bf16[4,96,640]{2,1,0:T(8,128)(2,1)S(1)}, bf16[4,96,640]{2,1,0:T(8,128)(2,1)S(1)}, u32[]{:S(2)}, u32[]{:S(2)}) collective-permute-start(bf16[4,96,640]{2,1,0:T(8,128)(2,1)S(1)} %dynamic-slice_bitcast_fusion), channel_id=1, source_target_pairs={{0,1},{1,2},{2,3},{3,0},{4,5},{5,6},{6,7},{7,4},{8,9},{9,10},{10,1... | collective-permute-start | bytes 1474568 | tf_op jit(solution)/shard_map/ppermute | solution.py:503
  417.6 13.7 %collective-permute-start.72 = (bf16[256,1536]{1,0:T(8,128)(2,1)S(1)}, bf16[256,1536]{1,0:T(8,128)(2,1)S(1)}, u32[]{:S(2)}, u32[]{:S(2)}) collective-permute-start(bf16[256,1536]{1,0:T(8,128)(2,1)S(1)} %get-tuple-element.71), channel_id=1, source_target_pairs={{0,4},{4,0},{8,12},{12,8},{1,5},{5,1},{9,13},{13,9},{2,6},{6,2},{1... | collective-permute-start | bytes 2359304 | tf_op jit(solution)/shard_map/ppermute | solution.py:498
  417.8 13.4 %collective-permute-start.83 = (bf16[96,1536]{1,0:T(8,128)(2,1)S(1)}, bf16[96,1536]{1,0:T(8,128)(2,1)S(1)}, u32[]{:S(2)}, u32[]{:S(2)}) collective-permute-start(bf16[96,1536]{1,0:T(8,128)(2,1)S(1)} %add_convert_fusion.21), channel_id=1, source_target_pairs={{0,1},{1,2},{2,3},{3,0},{4,5},{5,6},{6,7},{7,4},{8,9},{9,10},{10,1... | collective-permute-start | bytes 884744 | tf_op jit(solution)/shard_map/ppermute | solution.py:503
  420.2 69.6 %collective-permute-start.62 = (bf16[4,256,1536]{2,1,0:T(8,128)(2,1)}, bf16[4,256,1536]{2,1,0:T(8,128)(2,1)}, u32[]{:S(2)}, u32[]{:S(2)}) collective-permute-start(bf16[4,256,1536]{2,1,0:T(8,128)(2,1)} %get-tuple-element.40), channel_id=1, source_target_pairs={{0,4},{4,0},{8,12},{12,8},{1,5},{5,1},{9,13},{13,9},{2,6},{6,2},{1... | collective-permute-start | bytes 9437192 | tf_op jit(solution)/shard_map/ppermute | solution.py:498
  427.1 38.6 %collective-permute-start.71 = (bf16[256,1536]{1,0:T(8,128)(2,1)S(1)}, bf16[256,1536]{1,0:T(8,128)(2,1)S(1)}, u32[]{:S(2)}, u32[]{:S(2)}) collective-permute-start(bf16[256,1536]{1,0:T(8,128)(2,1)S(1)} %get-tuple-element.70), channel_id=1, source_target_pairs={{0,4},{4,0},{8,12},{12,8},{1,5},{5,1},{9,13},{13,9},{2,6},{6,2},{1... | collective-permute-start | bytes 2359304 | tf_op jit(solution)/shard_map/ppermute | solution.py:498
  431.2 19.8 %collective-permute-start.76 = (bf16[4,96,640]{2,1,0:T(8,128)(2,1)S(1)}, bf16[4,96,640]{2,1,0:T(8,128)(2,1)S(1)}, u32[]{:S(2)}, u32[]{:S(2)}) collective-permute-start(bf16[4,96,640]{2,1,0:T(8,128)(2,1)S(1)} %fusion.22), channel_id=1, source_target_pairs={{0,1},{1,2},{2,3},{3,0},{4,5},{5,6},{6,7},{7,4},{8,9},{9,10},{10,1... | collective-permute-start | bytes 1474568 | tf_op jit(solution)/shard_map/ppermute | solution.py:503
  431.3 19.1 %collective-permute-start.84 = (bf16[96,1536]{1,0:T(8,128)(2,1)S(1)}, bf16[96,1536]{1,0:T(8,128)(2,1)S(1)}, u32[]{:S(2)}, u32[]{:S(2)}) collective-permute-start(bf16[96,1536]{1,0:T(8,128)(2,1)S(1)} %add_convert_fusion.20), channel_id=1, source_target_pairs={{0,1},{1,2},{2,3},{3,0},{4,5},{5,6},{6,7},{7,4},{8,9},{9,10},{10,1... | collective-permute-start | bytes 884744 | tf_op jit(solution)/shard_map/ppermute | solution.py:503
  450.5 16.5 %collective-permute-start.73 = (bf16[256,1536]{1,0:T(8,128)(2,1)S(1)}, bf16[256,1536]{1,0:T(8,128)(2,1)S(1)}, u32[]{:S(2)}, u32[]{:S(2)}) collective-permute-start(bf16[256,1536]{1,0:T(8,128)(2,1)S(1)} %add_convert_fusion), channel_id=1, source_target_pairs={{0,8},{4,12},{8,0},{12,4},{1,9},{5,13},{9,1},{13,5},{2,10},{6,14},... | collective-permute-start | bytes 2359304 | tf_op jit(solution)/shard_map/ppermute | solution.py:498
  464.2 24.3 %collective-permute-start.78 = (bf16[4,96,640]{2,1,0:T(8,128)(2,1)}, bf16[4,96,640]{2,1,0:T(8,128)(2,1)}, u32[]{:S(2)}, u32[]{:S(2)}) collective-permute-start(bf16[4,96,640]{2,1,0:T(8,128)(2,1)} %fusion.20), channel_id=1, source_target_pairs={{0,16},{16,0},{1,17},{17,1},{2,18},{18,2},{3,19},{19,3},{4,20},{20... | collective-permute-start | bytes 1474568 | tf_op jit(solution)/shard_map/ppermute | solution.py:498
  495.4 16.5 %collective-permute-start.63 = (bf16[256,768]{1,0:T(8,128)(2,1)}, bf16[256,768]{1,0:T(8,128)(2,1)}, u32[]{:S(2)}, u32[]{:S(2)}) collective-permute-start(bf16[256,768]{1,0:T(8,128)(2,1)} %get-tuple-element.81), channel_id=1, source_target_pairs={{0,16},{16,0},{1,17},{17,1},{2,18},{18,2},{3,19},{19,3},{4,20},{20... | collective-permute-start | bytes 1179656 | tf_op jit(solution)/shard_map/ppermute | solution.py:498
  498.8 15.9 %collective-permute-start.67 = (bf16[256,768]{1,0:T(8,128)(2,1)S(1)}, bf16[256,768]{1,0:T(8,128)(2,1)}, u32[]{:S(2)}, u32[]{:S(2)}) collective-permute-start(bf16[256,768]{1,0:T(8,128)(2,1)S(1)} %get-tuple-element.82), channel_id=1, source_target_pairs={{0,8},{4,12},{8,0},{12,4},{1,9},{5,13},{9,1},{13,5},{2,10},{6,14},... | collective-permute-start | bytes 1179656 | tf_op jit(solution)/shard_map/ppermute | solution.py:498
  510.9 12.0 %collective-permute-start.65 = (bf16[256,768]{1,0:T(8,128)(2,1)S(1)}, bf16[256,768]{1,0:T(8,128)(2,1)S(1)}, u32[]{:S(2)}, u32[]{:S(2)}) collective-permute-start(bf16[256,768]{1,0:T(8,128)(2,1)S(1)} %slice.318), channel_id=1, source_target_pairs={{0,16},{16,0},{1,17},{17,1},{2,18},{18,2},{3,19},{19,3},{4,20},{20... | collective-permute-start | bytes 1179656 | tf_op jit(solution)/shard_map/ppermute | solution.py:498
  511.5 12.0 %collective-permute-start.66 = (bf16[256,768]{1,0:T(8,128)(2,1)S(1)}, bf16[256,768]{1,0:T(8,128)(2,1)S(1)}, u32[]{:S(2)}, u32[]{:S(2)}) collective-permute-start(bf16[256,768]{1,0:T(8,128)(2,1)S(1)} %slice.320), channel_id=1, source_target_pairs={{0,8},{4,12},{8,0},{12,4},{1,9},{5,13},{9,1},{13,5},{2,10},{6,14},... | collective-permute-start | bytes 1179656 | tf_op jit(solution)/shard_map/ppermute | solution.py:498
  513.0 17.8 %collective-permute-start.64 = (bf16[256,768]{1,0:T(8,128)(2,1)S(1)}, bf16[256,768]{1,0:T(8,128)(2,1)S(1)}, u32[]{:S(2)}, u32[]{:S(2)}) collective-permute-start(bf16[256,768]{1,0:T(8,128)(2,1)S(1)} %add_convert_fusion.16), channel_id=1, source_target_pairs={{0,8},{4,12},{8,0},{12,4},{1,9},{5,13},{9,1},{13,5},{2,10},{6,14},... | collective-permute-start | bytes 1179656 | tf_op jit(solution)/shard_map/ppermute | solution.py:498
  515.8 15.0 %collective-permute-start.68 = (bf16[256,768]{1,0:T(8,128)(2,1)S(1)}, bf16[256,768]{1,0:T(8,128)(2,1)S(1)}, u32[]{:S(2)}, u32[]{:S(2)}) collective-permute-start(bf16[256,768]{1,0:T(8,128)(2,1)S(1)} %add_convert_fusion.15), channel_id=1, source_target_pairs={{0,16},{16,0},{1,17},{17,1},{2,18},{18,2},{3,19},{19,3},{4,20},{20... | collective-permute-start | bytes 1179656 | tf_op jit(solution)/shard_map/ppermute | solution.py:498
  (107 other events, 1341.8 us)

commit v2 on v1

v2 whole, which is shorter than its diff:
```python
import functools

import jax
import jax.numpy as jnp
from jax import lax
from jax.experimental import pallas as pl
from jax.experimental.pallas import tpu as pltpu
from jax.sharding import PartitionSpec as P

MODEL_WIDTH = 1536
QUERY_HEADS = 24
KEY_VALUE_HEADS = 8
HEAD_SIZE = 64
MOST_LEN = 512
NORM_EPS = 1e-06
ROPE_BASE = 10000.0
MASKED = -1e30
QROWS = 128
LANES = 128
bf16 = jnp.bfloat16
f32 = jnp.float32
ANY = pl.BlockSpec(memory_space=pl.ANY)
VMEM = pl.BlockSpec(memory_space=pltpu.VMEM)
SMEM = pl.BlockSpec(memory_space=pltpu.SMEM)
NT = (((1,), (1,)), ((), ()))
TN = (((0,), (0,)), ((), ()))


def params(limit=56):
    return pltpu.CompilerParams(vmem_limit_bytes=limit * 1024 * 1024)


def cost(flops, nbytes):
    return pl.CostEstimate(flops=int(flops), bytes_accessed=int(nbytes), transcendentals=0)


def dot(a, b, dims=(((1,), (0,)), ((), ()))):
    return lax.dot_general(a, b, dims, preferred_element_type=f32)


def lane_iota(rows):
    return lax.broadcasted_iota(jnp.int32, (rows, LANES), 1)


def half_swap(v):
    lane = lane_iota(v.shape[0])
    low = lax.rem(lane, HEAD_SIZE) < HEAD_SIZE // 2
    up = pltpu.roll(v, LANES - HEAD_SIZE // 2, 1)
    down = pltpu.roll(v, HEAD_SIZE // 2, 1)
    return jnp.where(low, up, down)


def three_parts(v):
    hi = v.astype(bf16).astype(f32)
    mid = (v - hi).astype(bf16).astype(f32)
    return hi, mid, v - hi - mid


def norm_kernel(n_ctx, *refs):
    x_refs, (gain_ref, h1_ref, x_buf, sem) = refs[:n_ctx], refs[n_ctx:]
    tok = x_buf.shape[1]
    copies = [pltpu.make_async_copy(x_refs[m], x_buf.at[m], sem.at[m]) for m in range(n_ctx)]
    for c in copies:
        c.start()
    for c in copies:
        c.wait()
    step = 64

    def norm(i, carry):
        rows = pl.ds(pl.multiple_of(i % (tok // step) * step, step), step)
        x = x_buf[i // (tok // step), rows, :].astype(f32)
        r = lax.rsqrt(jnp.mean(x * x, axis=-1, keepdims=True) + NORM_EPS)
        h1_ref[i // (tok // step), rows, :] = (x * r * gain_ref[...]).astype(bf16)
        return carry

    lax.fori_loop(0, n_ctx * tok // step, norm, 0)


def norm_rows(x_pieces, gain):
    n_ctx, tok = len(x_pieces), x_pieces[0].shape[0]
    return pl.pallas_call(
        functools.partial(norm_kernel, n_ctx),
        out_shape=jax.ShapeDtypeStruct((n_ctx, tok, MODEL_WIDTH), bf16),
        in_specs=[ANY] * n_ctx + [VMEM],
        out_specs=VMEM,
        scratch_shapes=[
            pltpu.VMEM((n_ctx, tok, MODEL_WIDTH), bf16),
            pltpu.SemaphoreType.DMA((n_ctx,)),
        ],
        compiler_params=params(),
        cost_estimate=cost(3e9, 6e6),
        name="norm_rows",
    )(*x_pieces, gain)


def attn_fwd_kernel(n_ctx, n_w, qh, kvh, place_ref, *refs):
    w_refs, refs = refs[:n_w], refs[n_w:]
    (h1_ref, row_ref, col_ref, start_ref, cos_ref, sin_ref), refs = refs[:6], refs[6:]
    (near_ref, far_ref, q_ref, k_ref, v_ref, lse_ref, w_out), refs = refs[:7], refs[7:]
    w_ref, h1_buf, qkv_buf, sorted_buf, sem_w, sem_h, sem_out = refs
    tok = h1_buf.shape[1]
    total = n_ctx * tok
    group = qh // kvh
    part = w_refs[0].shape[1]
    w_copies = []
    for k in range(n_w):
        for m in range(n_ctx):
            i = k * n_ctx + m
            row0 = pl.multiple_of(place_ref[n_w * n_ctx + k] * part, 16)
            spot = w_ref.at[place_ref[i], pl.ds(row0, part), :]
            w_copies.append(pltpu.make_async_copy(w_refs[k].at[m], spot, sem_w.at[i]))
    h_copies = [pltpu.make_async_copy(h1_ref.at[m], h1_buf.at[m], sem_h.at[m]) for m in range(n_ctx)]
    for c in w_copies + h_copies:
        c.start()
    for c in w_copies + h_copies:
        c.wait()
    keep_w = pltpu.make_async_copy(w_ref, w_out, sem_out)
    keep_w.start()
    q_chunks = qh * HEAD_SIZE // LANES
    k_chunks = kvh * HEAD_SIZE // LANES

    def project(m, carry):
        w = w_ref[...].reshape(MODEL_WIDTH, w_ref.shape[2])
        qkv = dot(h1_buf[m], w)
        rows = pl.ds(m * tok, tok)
        cos, sin = cos_ref[rows, :], sin_ref[rows, :]
        out = []
        for j in range(q_chunks + 2 * k_chunks):
            piece = qkv[:, j * LANES : (j + 1) * LANES]
            if j < q_chunks + k_chunks:
                piece = piece * cos + half_swap(piece) * sin
                if j < q_chunks:
                    piece = piece * HEAD_SIZE**-0.5
            out.append(piece)
        qkv_buf[rows, :] = jnp.concatenate(out, axis=1).astype(bf16)
        return carry

    lax.fori_loop(0, n_ctx, project, 0)

    def arrange(b, carry):
        rows = pl.ds(b * tok, tok)
        place = lax.broadcasted_iota(jnp.int32, (tok, total), 0) + b * tok
        pick = (place == row_ref[...]).astype(f32).astype(bf16)
        s = dot(pick, qkv_buf[...])
        lane = lane_iota(tok)
        one = jnp.where(lane == HEAD_SIZE, 1.0, 0.0)
        for h in range(qh + 2 * kvh):
            piece = s[:, (h // 2) * LANES : (h // 2 + 1) * LANES]
            if h % 2:
                piece = pltpu.roll(piece, HEAD_SIZE, 1)
            fill = jnp.zeros_like(one) if h < qh + kvh else one
            piece = jnp.where(lane < HEAD_SIZE, piece, fill).astype(bf16)
            if h < qh:
                q_ref[h, rows, :] = piece
            elif h < qh + kvh:
                k_ref[h - qh, rows, :] = piece
            else:
                v_ref[h - qh - kvh, rows, :] = piece
        return carry

    lax.fori_loop(0, n_ctx, arrange, 0)
    window = min(MOST_LEN + QROWS, total)
    lse_ref[...] = jnp.zeros_like(lse_ref)

    def attend(b, carry):
        q0 = pl.multiple_of(b * QROWS, QROWS)
        k0 = pl.multiple_of(jnp.maximum(q0 + QROWS - window, 0), QROWS)
        rows, keys = pl.ds(q0, QROWS), pl.ds(k0, window)
        kidx = lax.broadcasted_iota(jnp.int32, (window, QROWS), 0) + k0
        qidx = lax.broadcasted_iota(jnp.int32, (window, QROWS), 1) + q0
        allowed = (kidx <= qidx) & (kidx >= start_ref[:, rows])
        for g in range(kvh):
            q = q_ref[g * group : (g + 1) * group, rows, :].reshape(group * QROWS, LANES)
            s = dot(k_ref[g, keys, :], q, NT)
            tops, exps = [], []
            for i in range(group):
                one = jnp.where(allowed, s[:, i * QROWS : (i + 1) * QROWS], MASKED)
                top = jnp.max(one, axis=0, keepdims=True)
                tops.append(top)
                exps.append(jnp.exp(one - top).astype(bf16))
            o = dot(v_ref[g, keys, :], jnp.concatenate(exps, axis=1), TN)
            total_e = o[HEAD_SIZE : HEAD_SIZE + 1, :]
            o = (o[:HEAD_SIZE, :] / total_e).astype(bf16)
            lse = jnp.log(total_e)
            for i in range(group):
                h = g * group + i
                cols = slice(i * QROWS, (i + 1) * QROWS)
                lse_ref[h : h + 1, rows] = tops[i] + lse[:, cols]
                sorted_buf[h * HEAD_SIZE : (h + 1) * HEAD_SIZE, rows] = o[:, cols]
        return carry

    lax.fori_loop(0, total // QROWS, attend, 0)

    def scatter(m, carry):
        place = lax.broadcasted_iota(jnp.int32, (tok, total), 1)
        pick = (place == col_ref[pl.ds(m * tok, tok), :]).astype(f32).astype(bf16)
        out = dot(pick, sorted_buf[...], NT).astype(bf16)

        @pl.when(m < n_ctx // 2)
        def _():
            near_ref[m] = out

        @pl.when(m >= n_ctx // 2)
        def _():
            far_ref[m - n_ctx // 2] = out

        return carry

    lax.fori_loop(0, n_ctx, scatter, 0)
    keep_w.wait()


def attn_fwd(places, w_pieces, n_dp, h1, row, col, start_row, cos, sin, qh, kvh):
    n_w = len(w_pieces)
    n_ctx, tok = h1.shape[:2]
    total = n_ctx * tok
    width = w_pieces[0].shape[2]
    rows = w_pieces[0].shape[1] * (n_w // n_dp)
    shape = jax.ShapeDtypeStruct
    return pl.pallas_call(
        functools.partial(attn_fwd_kernel, n_ctx, n_w, qh, kvh),
        out_shape=(
            shape((n_ctx // 2, tok, qh * HEAD_SIZE), bf16),
            shape((n_ctx // 2, tok, qh * HEAD_SIZE), bf16),
            shape((qh, total, LANES), bf16),
            shape((kvh, total, LANES), bf16),
            shape((kvh, total, LANES), bf16),
            shape((-(-qh // 8) * 8, total), f32),
            shape((n_ctx * n_dp, rows, width), bf16),
        ),
        in_specs=[SMEM] + [ANY] * (n_w + 1) + [VMEM] * 5,
        out_specs=(VMEM,) * 6 + (ANY,),
        scratch_shapes=[
            pltpu.VMEM((n_ctx * n_dp, rows, width), bf16),
            pltpu.VMEM((n_ctx, tok, MODEL_WIDTH), bf16),
            pltpu.VMEM((total, width), bf16),
            pltpu.VMEM((qh * HEAD_SIZE, total), bf16),
            pltpu.SemaphoreType.DMA((n_ctx * n_w,)),
            pltpu.SemaphoreType.DMA((n_ctx,)),
            pltpu.SemaphoreType.DMA,
        ],
        compiler_params=params(),
        cost_estimate=cost(20e9, 20e6),
        name="attn_fwd",
    )(places, *w_pieces, h1, row, col, start_row, cos, sin)


def attn_bwd_kernel(n_ctx, qh, kvh, *refs):
    db_refs, refs = refs[:n_ctx], refs[n_ctx:]
    (wo_ref, near_ref, far_ref, q_ref, k_ref, v_ref, lse_ref), refs = refs[:7], refs[7:]
    (row_ref, col_ref, start_ref, cos_ref, sin_ref, cos_t, sin_t), refs = refs[:7], refs[7:]
    out_ref, db_buf, dat_buf, del_buf, do_buf, dq_buf, dk_buf, dv_buf, kv_buf, sem = refs
    tok = db_buf.shape[1]
    total = n_ctx * tok
    group = qh // kvh
    k_chunks = kvh * HEAD_SIZE // LANES
    n_rows = lse_ref.shape[0]
    copies = [pltpu.make_async_copy(db_refs[m], db_buf.at[m], sem.at[m]) for m in range(n_ctx)]
    for c in copies:
        c.start()
    dk_buf[...] = jnp.zeros_like(dk_buf)
    dv_buf[...] = jnp.zeros_like(dv_buf)
    for c in copies:
        c.wait()
    q_width = qh * HEAD_SIZE
    head_of = lax.broadcasted_iota(jnp.int32, (n_rows, q_width), 1) // HEAD_SIZE
    ones = (head_of == lax.broadcasted_iota(jnp.int32, (n_rows, q_width), 0)).astype(f32).astype(bf16)

    def lift(m, carry):
        rows = pl.ds(pl.multiple_of(m * tok, tok), tok)
        low = dot(db_buf[m], wo_ref[...], NT).astype(bf16)
        dat_buf[rows, :] = low
        attn = jnp.where(m < n_ctx // 2, near_ref[m % (n_ctx // 2)], far_ref[m % (n_ctx // 2)])
        prod = low.astype(f32) * attn.astype(f32)
        hi = prod.astype(bf16)
        rest = (prod - hi.astype(f32)).astype(bf16)
        delta = dot(ones, hi, NT) + dot(ones, rest, NT)
        for i, v in enumerate(three_parts(delta)):
            del_buf[i * n_rows : (i + 1) * n_rows, rows] = v
        return carry

    lax.fori_loop(0, n_ctx, lift, 0)
    delta_parts = del_buf[...].astype(bf16)

    def arrange(b, carry):
        rows = pl.ds(pl.multiple_of(b * tok, tok), tok)
        place = lax.broadcasted_iota(jnp.int32, (tok, total), 0) + b * tok
        pick = (place == row_ref[...]).astype(f32).astype(bf16)
        s = dot(pick, dat_buf[...])
        lane = lane_iota(tok)
        for h in range(qh):
            piece = s[:, (h // 2) * LANES : (h // 2 + 1) * LANES]
            if h % 2:
                piece = pltpu.roll(piece, HEAD_SIZE, 1)
            do_buf[h, rows, :] = jnp.where(lane < HEAD_SIZE, piece, 0.0).astype(bf16)
        d = dot(delta_parts, pick, NT)
        del_buf[:n_rows, rows] = d[:n_rows] + d[n_rows : 2 * n_rows] + d[2 * n_rows :]
        return carry

    lax.fori_loop(0, n_ctx, arrange, 0)
    window = min(MOST_LEN + QROWS, total)

    def attend(b, carry):
        q0 = pl.multiple_of(b * QROWS, QROWS)
        k0 = pl.multiple_of(jnp.maximum(q0 + QROWS - window, 0), QROWS)
        rows, keys = pl.ds(q0, QROWS), pl.ds(k0, window)
        kidx = lax.broadcasted_iota(jnp.int32, (window, QROWS), 0) + k0
        qidx = lax.broadcasted_iota(jnp.int32, (window, QROWS), 1) + q0
        allowed = (kidx <= qidx) & (kidx >= start_ref[:, rows])
        for g in range(kvh):
            heads = slice(g * group, (g + 1) * group)
            q = q_ref[heads, rows, :].reshape(group * QROWS, LANES)
            do = do_buf[heads, rows, :].reshape(group * QROWS, LANES)
            k, v = k_ref[g, keys, :], v_ref[g, keys, :]
            s, dp = dot(k, q, NT), dot(v, do, NT)
            probs, grads = [], []
            for i in range(group):
                h = g * group + i
                cols = slice(i * QROWS, (i + 1) * QROWS)
                p = jnp.where(allowed, jnp.exp(s[:, cols] - lse_ref[h : h + 1, rows]), 0.0)
                probs.append(p.astype(bf16))
                grads.append((p * (dp[:, cols] - del_buf[h : h + 1, rows])).astype(bf16))
            p, ds = jnp.concatenate(probs, axis=1), jnp.concatenate(grads, axis=1)
            dv_buf[g, keys, :] += dot(p, do)
            dk_buf[g, keys, :] += dot(ds, q)
            dq = dot(k, ds, TN)
            for i in range(group):
                h = g * group + i
                turned = dq[:HEAD_SIZE, i * QROWS : (i + 1) * QROWS] * HEAD_SIZE**-0.5
                half = HEAD_SIZE // 2
                low, high = turned[:half], turned[half:]
                cos, sin = cos_t[:, rows], sin_t[:, rows]
                turned = jnp.concatenate([low * cos + high * sin, high * cos - low * sin], axis=0)
                dq_buf[h * HEAD_SIZE : (h + 1) * HEAD_SIZE, rows] = turned.astype(bf16)
        return carry

    lax.fori_loop(0, total // QROWS, attend, 0)

    def turn_back(b, carry):
        rows = pl.ds(b * tok, tok)
        cos, sin = cos_ref[rows, :], sin_ref[rows, :]
        lane = lane_iota(tok)
        heads = [dk_buf[h, rows, :] for h in range(kvh)] + [dv_buf[h, rows, :] for h in range(kvh)]
        for j in range(2 * k_chunks):
            pair = jnp.where(lane < HEAD_SIZE, heads[2 * j], pltpu.roll(heads[2 * j + 1], HEAD_SIZE, 1))
            if j < k_chunks:
                pair = pair * cos - half_swap(pair) * sin
            kv_buf[rows, j * LANES : (j + 1) * LANES] = pair.astype(bf16)
        return carry

    lax.fori_loop(0, n_ctx, turn_back, 0)

    def scatter(m, carry):
        place = lax.broadcasted_iota(jnp.int32, (tok, total), 1)
        pick = (place == col_ref[pl.ds(m * tok, tok), :]).astype(f32).astype(bf16)
        out_ref[m, :, :q_width] = dot(pick, dq_buf[...], NT).astype(bf16)
        out_ref[m, :, q_width:] = dot(pick, kv_buf[...]).astype(bf16)
        return carry

    lax.fori_loop(0, n_ctx, scatter, 0)


def attn_bwd(db_pieces, wo, near, far, q, k, v, lse, row, col, start_row, tables, qh, kvh):
    n_ctx = len(db_pieces)
    tok = db_pieces[0].shape[0]
    total = n_ctx * tok
    width = (qh + 2 * kvh) * HEAD_SIZE
    return pl.pallas_call(
        functools.partial(attn_bwd_kernel, n_ctx, qh, kvh),
        out_shape=jax.ShapeDtypeStruct((n_ctx, tok, width), bf16),
        in_specs=[ANY] * n_ctx + [VMEM] * 14,
        out_specs=VMEM,
        scratch_shapes=[
            pltpu.VMEM((n_ctx, tok, MODEL_WIDTH), bf16),
            pltpu.VMEM((total, qh * HEAD_SIZE), bf16),
            pltpu.VMEM((3 * lse.shape[0], total), f32),
            pltpu.VMEM((qh, total, LANES), bf16),
            pltpu.VMEM((qh * HEAD_SIZE, total), bf16),
            pltpu.VMEM((kvh, total, LANES), f32),
            pltpu.VMEM((kvh, total, LANES), f32),
            pltpu.VMEM((total, 2 * kvh * HEAD_SIZE), bf16),
            pltpu.SemaphoreType.DMA((n_ctx,)),
        ],
        compiler_params=params(),
        cost_estimate=cost(25e9, 20e6),
        name="attn_bwd",
    )(*db_pieces, wo, near, far, q, k, v, lse, row, col, start_row, *tables)


def pick_rows(e, cap, routes):
    tok = routes.shape[1]
    before = lax.broadcasted_iota(jnp.int32, (tok, tok), 0) < lax.broadcasted_iota(
        jnp.int32, (tok, tok), 1
    )
    names = lax.broadcasted_iota(jnp.int32, (LANES, tok), 0)
    slots = lax.broadcasted_iota(jnp.int32, (cap, tok), 0).astype(f32)
    hit = jnp.zeros((1, tok), f32)
    named = jnp.zeros((LANES, tok), f32)
    for j in range(routes.shape[0]):
        hit = hit + jnp.where(routes[j : j + 1] == e, 1.0, 0.0)
        named = named + jnp.where(names == routes[j : j + 1], 1.0, 0.0)
    hits = jnp.broadcast_to(hit, (8, tok)).astype(bf16)
    slot = dot(hits, before.astype(f32).astype(bf16))[0:1]
    pick = jnp.where((slots == slot) & (hit > 0.5), 1.0, 0.0).astype(bf16)
    return pick, dot(pick, named.astype(bf16), NT)


TILE = 512


def expert_kernel(by_hand, cap, who_ref, *refs):
    n_in = len(PIECES) if by_hand else 1
    h_refs, dy_refs, refs = refs[:n_in], refs[n_in : 2 * n_in], refs[2 * n_in :]
    (routes_ref, wc_ref, wd_ref), refs = refs[:3], refs[3:]
    n_rows = 4 if by_hand else 2
    row_refs, refs = refs[:n_rows], refs[n_rows:]
    (xs_ref, deout_ref, act_ref, dgate_ref, dup_ref, coef_ref), refs = refs[:6], refs[6:]
    dcat, drow, yrow, refs = *refs[:3], refs[3:]
    step = pl.program_id(0)
    core = who_ref[1]
    e = who_ref[0]
    ff = wd_ref.shape[0]
    if by_hand:
        h_buf, dy_buf, sem = refs

        def copies(chip):
            got = []
            for n, (j, sib) in enumerate(PIECES):
                if j != chip:
                    continue
                col = pl.multiple_of((core + sib) % 2 * HALF, HALF)
                for i in range(2):
                    spot = (2 * j + (i ^ sib), slice(None), pl.ds(col, HALF))
                    for k, (src, buf) in enumerate(((h_refs, h_buf), (dy_refs, dy_buf))):
                        got.append(
                            pltpu.make_async_copy(src[n].at[i], buf.at[spot], sem.at[k, n, i])
                        )
            return got

        @pl.when(step == 0)
        def _():
            for j in range(4):
                for c in copies(j):
                    c.start()

        for j in range(4):

            @pl.when(step == j)
            def _():
                for c in copies(j):
                    c.wait()

        def load(buf, i, cols):
            return buf[2 * step + i, :, cols]

    else:
        h_buf, dy_buf = h_refs[0], dy_refs[0]

        def load(buf, i, cols):
            return buf[i, :, cols]

    picks, masks = [], []
    for i in range(2):
        pick, mask = pick_rows(e, cap, routes_ref[2 * step + i])
        picks.append(pick)
        masks.append(mask)
    mask = jnp.concatenate(masks, axis=0) > 0.5
    tiles = [slice(t, t + TILE) for t in range(0, MODEL_WIDTH, TILE)]
    for cols in tiles:
        for i in range(2):
            rows = slice(i * cap, (i + 1) * cap)
            xs_ref[rows, cols] = dot(picks[i], load(h_buf, i, cols)).astype(bf16)
            deout_ref[rows, cols] = dot(picks[i], load(dy_buf, i, cols)).astype(bf16)
    xs = xs_ref[...]
    logits = jnp.where(mask, dot(xs, wc_ref[:, 2 * ff :]), MASKED)
    ex = jnp.where(mask, jnp.exp(logits - jnp.max(logits, axis=1, keepdims=True)), 0.0)
    lane = lax.broadcasted_iota(jnp.int32, ex.shape, 1)
    own = lane == e
    denom = jnp.sum(ex, axis=1, keepdims=True)
    probs = ex / jnp.where(denom > 0.0, denom, 1.0)
    gp = jnp.sum(jnp.where(own, probs, 0.0), axis=1, keepdims=True)
    gate = dot(xs, wc_ref[:, :ff])
    up = dot(xs, wc_ref[:, ff : 2 * ff])
    sig = jax.nn.sigmoid(gate)
    silu = gate * sig
    act = (silu * up).astype(bf16)
    act_ref[...] = act
    dgp = jnp.zeros((2 * cap, LANES), f32)
    for cols in tiles:
        eout = dot(act, wd_ref[:, cols]).astype(bf16).astype(f32)
        dys = deout_ref[:, cols].astype(f32)
        both = dys * eout
        for c in range(0, TILE, LANES):
            dgp = dgp + both[:, c : c + LANES]
        deout_ref[:, cols] = (gp * dys).astype(bf16)
        yrow[:, cols] = (gp * eout).astype(bf16)
    dgp = jnp.sum(dgp, axis=1, keepdims=True)
    coef = gp * dgp * (jnp.where(own, 1.0, 0.0) - probs)
    hi = coef.astype(bf16).astype(f32)
    low = pltpu.roll(coef - hi, LANES // 2, 1)
    coef = jnp.where(lane < LANES // 2, hi, low).astype(bf16)
    coef_ref[...] = coef
    dact = dot(deout_ref[...], wd_ref[...], NT)
    dgate = (dact * up * sig * (1.0 + gate * (1.0 - sig))).astype(bf16)
    dup = (dact * silu).astype(bf16)
    dgate_ref[...] = dgate
    dup_ref[...] = dup
    dcat[:, :ff] = dgate
    dcat[:, ff : 2 * ff] = dup
    dcat[:, 2 * ff :] = coef
    for cols in tiles:
        drow[:, cols] = dot(dcat[...], wc_ref[cols, :], NT).astype(bf16)
    for k, buf in enumerate((drow, yrow)):
        for i in range(2):
            rows = slice(i * cap, (i + 1) * cap)
            if by_hand:
                mine = pl.multiple_of(core * HALF, HALF)
                other = pl.multiple_of((1 - core) * HALF, HALF)
                for ref, at, col in ((row_refs[2 * k], i, mine), (row_refs[2 * k + 1], 1 - i, other)):
                    ref[0, at] = dot(picks[i], buf[rows, pl.ds(col, HALF)], TN).astype(bf16)
            else:
                row_refs[k][0, i] = dot(picks[i], buf[rows, :], TN).astype(bf16)


def run_experts(who, by_hand, h_list, dy_list, routes_t, wc, wd, cap, tok):
    n_blocks = routes_t.shape[0]
    steps = n_blocks // 2
    ff = wd.shape[0]
    rows = 2 * cap
    shape = jax.ShapeDtypeStruct
    out_w = HALF if by_hand else MODEL_WIDTH
    block = pl.BlockSpec((1, 2, tok, out_w), lambda i, *_: (i, 0, 0, 0))
    other = pl.BlockSpec((1, 2, tok, out_w), lambda i, *_: (i // 2 + i % 2 * 2, 0, 0, 0))
    wide = pl.BlockSpec((rows, MODEL_WIDTH), lambda i, *_: (i, 0))
    thin = pl.BlockSpec((rows, ff), lambda i, *_: (i, 0))
    edge = pl.BlockSpec((rows, LANES), lambda i, *_: (i, 0))
    whole = pl.BlockSpec((2, tok, MODEL_WIDTH), lambda i, *_: (i, 0, 0))
    n_in = len(h_list)
    scratch = [
        pltpu.VMEM((rows, wc.shape[1]), bf16),
        pltpu.VMEM((rows, MODEL_WIDTH), bf16),
        pltpu.VMEM((rows, MODEL_WIDTH), bf16),
    ]
    if by_hand:
        scratch += [
            pltpu.VMEM((n_blocks, tok, MODEL_WIDTH), bf16),
            pltpu.VMEM((n_blocks, tok, MODEL_WIDTH), bf16),
            pltpu.SemaphoreType.DMA((2, n_in, 2)),
        ]
    row_specs = [block, other] * 2 if by_hand else [block] * 2
    grid_spec = pltpu.PrefetchScalarGridSpec(
        num_scalar_prefetch=1,
        grid=(steps,),
        in_specs=[ANY if by_hand else whole] * (2 * n_in) + [VMEM] * 3,
        out_specs=row_specs + [wide] * 2 + [thin] * 3 + [edge],
        scratch_shapes=scratch,
    )
    return pl.pallas_call(
        functools.partial(expert_kernel, by_hand, cap),
        out_shape=[shape((steps, 2, tok, out_w), bf16)] * len(row_specs)
        + [shape((steps * rows, MODEL_WIDTH), bf16)] * 2
        + [shape((steps * rows, ff), bf16)] * 3
        + [shape((steps * rows, LANES), bf16)],
        grid_spec=grid_spec,
        compiler_params=params(60),
        cost_estimate=cost(30e9, 30e6),
        name="experts",
    )(who, *h_list, *dy_list, routes_t, wc, wd)


def flip(v, axis, bit):
    n = lax.axis_size(axis)
    return lax.ppermute(v, axis, [(i, i ^ bit) for i in range(n)])


def step_up(v, axis):
    n = lax.axis_size(axis)
    return lax.ppermute(v, axis, [(i, (i + 1) % n) for i in range(n)])


def ctx_gather(v):
    n = lax.axis_size("context")
    pieces = {0: v}
    bit = n // 2
    while bit:
        for m in list(pieces):
            pieces[m | bit] = flip(pieces[m], "context", bit)
        bit //= 2
    return [pieces[m] for m in range(n)]


def add_low(a, b):
    return (a.astype(f32) + b.astype(f32)).astype(bf16)


def ring(v, axis, deps=()):
    pieces = [v]
    for i in range(lax.axis_size(axis) - 1):
        sent = after(pieces[-1], *deps[i]) if i < len(deps) else pieces[-1]
        pieces.append(step_up(sent, axis))
    return pieces


def send_all(v, axis):
    n = lax.axis_size(axis)
    return [v] + [
        lax.ppermute(v, axis, [(i, (i + k) % n) for i in range(n)]) for k in range(1, n)
    ]


def ring_sum(chunk, axis):
    n, d = lax.axis_size(axis), lax.axis_index(axis)
    part = chunk(lax.rem(d + n - 1, n)).astype(bf16)
    for hop in range(n - 1):
        got = step_up(part, axis)
        own = chunk(lax.rem(d + 2 * n - 2 - hop, n))
        part = (got.astype(f32) + own.astype(f32)).astype(bf16)
    return part


def direct_sum(chunk, axis, *deps):
    n, d = lax.axis_size(axis), lax.axis_index(axis)
    total = chunk(d).astype(f32)
    if deps:
        total = after(total, *deps)
    for k in range(1, n):
        sent = chunk(lax.rem(d + k, n)).astype(bf16)
        got = lax.ppermute(sent, axis, [(i, (i + k) % n) for i in range(n)])
        total = total + got.astype(f32)
    return total


def after(v, *deps):
    return lax.optimization_barrier((v, *deps))[0]


HALF = MODEL_WIDTH // 2
PLANE = ("expert", "context")
PIECES = ((0, 0), (1, 0), (2, 0), (3, 0), (0, 1), (2, 1), (1, 1), (3, 1))


def small_plane():
    return lax.axis_size("expert") == 2 and lax.axis_size("context") == 4


def hop_plane(v, second):
    pairs = []
    for i in range(8):
        along_context = (i % 2 == 0) != second
        pairs.append((i, i ^ 2 if along_context else i ^ 4))
    return lax.ppermute(v, PLANE, pairs)


def halves(v, core):
    left, right = v[..., :HALF], v[..., HALF:]
    return jnp.where(core == 0, left, right), jnp.where(core == 0, right, left)


def sync(*values):
    return lax.optimization_barrier(values)


def plane_near(v):
    core = lax.axis_index("context") % 2
    mine, given = halves(v, core)
    return jnp.stack([mine, flip(given, "context", 1)])


def plane_far(u0, u1):
    return hop_plane(u0, True), hop_plane(u1, True)


def plane_share(own):
    return list(own) + [flip(u, "context", 1) for u in own]


def plane_gather(v):
    if not small_plane():
        return [lax.all_gather(v, PLANE, axis=0, tiled=False)]
    u0 = plane_near(v)
    u1 = hop_plane(u0, False)
    return plane_share((u0, u1) + plane_far(u0, u1))


class PlaneSum:
    def __init__(self, rows):
        self.small = small_plane()
        self.rows = rows
        if self.small:
            self.keep, give = rows
            self.got = flip(give, "context", 1)
            self.far = add_low(self.keep[2:], self.got[2:])

    def first(self):
        if self.small:
            self.got2 = hop_plane(self.far, True)

    def second(self):
        if self.small:
            near = self.keep[:2].astype(f32) + self.got[:2].astype(f32) + self.got2.astype(f32)
            self.near = near[0]
            self.got1 = hop_plane(near[1].astype(bf16), False)

    def finish(self):
        if not self.small:
            (both,) = self.rows
            flat = both.reshape(-1, both.shape[-1])
            return lax.psum_scatter(flat, PLANE, scatter_dimension=0, tiled=True).astype(f32)
        core = lax.axis_index("context") % 2
        whole = self.near + self.got1.astype(f32)
        other = flip(whole[1].astype(bf16), "context", 1).astype(f32)
        left = jnp.where(core == 0, whole[0], other)
        right = jnp.where(core == 0, other, whole[0])
        return jnp.concatenate([left, right], axis=1)


def ctx_sum(p):
    far = add_low(p[2], flip(p[3], "context", 1))
    own = p[0].astype(f32) + flip(p[1], "context", 1).astype(f32)
    return own + flip(far, "context", 2).astype(f32)


def put_in_order(places, pieces, name):
    n = len(pieces)
    rows, width = pieces[0].shape

    def kernel(place_ref, *refs):
        out_ref, sem = refs[n:]
        copies = [
            pltpu.make_async_copy(refs[k], out_ref.at[place_ref[k]], sem.at[k]) for k in range(n)
        ]
        for c in copies:
            c.start()
        for c in copies:
            c.wait()

    return pl.pallas_call(
        kernel,
        out_shape=jax.ShapeDtypeStruct((n, rows, width), pieces[0].dtype),
        in_specs=[SMEM] + [ANY] * n,
        out_specs=VMEM,
        scratch_shapes=[pltpu.SemaphoreType.DMA((n,))],
        cost_estimate=cost(0, 2 * n * rows * width * 2),
        name=name,
    )(places, *pieces)


def columns_of(spots, near, far, qw, kw):
    n_ctx, part, width = near.shape

    def kernel(spot_ref, near_ref, far_ref, *outs):
        for k, ref in enumerate((near_ref, far_ref)):
            row = pl.multiple_of(spot_ref[n_ctx + k] * part, 16)
            for m in range(n_ctx):
                v = ref[m].astype(f32)
                lo = 0
                for out, w in zip(outs, (qw, kw, kw)):
                    col = pl.multiple_of(spot_ref[m] * w, LANES)
                    out[pl.ds(row, part), pl.ds(col, w)] = v[:, lo : lo + w]
                    lo += w

    shape = jax.ShapeDtypeStruct
    return pl.pallas_call(
        kernel,
        out_shape=tuple(shape((2 * part, n_ctx * w), f32) for w in (qw, kw, kw)),
        in_specs=[SMEM, VMEM, VMEM],
        out_specs=(VMEM,) * 3,
        cost_estimate=cost(0, 2e6),
        name="columns_of",
    )(spots, near, far)


def rms_back(dh, v, r, gain):
    inner = jnp.sum(gain * dh * v, axis=-1, keepdims=True)
    dv = r * gain * dh - v * (r * r * r) * (inner / MODEL_WIDTH)
    return dv, jnp.sum(dh * v * r, axis=0)


def body(
    hidden, cotangent, token_order, lengths, routes, attn_gain, w_query, key_weight,
    value_weight, w_out, ffn_gain, w_router, w_gate, w_up, w_down,
):
    tok, top = hidden.shape[1], routes.shape[2]
    n_exp, n_ctx, n_dp = (lax.axis_size(a) for a in ("expert", "context", "dp"))
    experts = n_exp * n_ctx
    cap = -(-(9 * tok * top // (8 * experts)) // 16) * 16
    qh, kvh = QUERY_HEADS // n_ctx, KEY_VALUE_HEADS // n_ctx
    qw, kw = qh * HEAD_SIZE, kvh * HEAD_SIZE
    rows = w_query.shape[0]
    ex, cx, dx = (lax.axis_index(a) for a in ("expert", "context", "dp"))
    my_expert = ex * n_ctx + cx
    total = n_ctx * tok

    def for_context(c):
        return jnp.concatenate(
            [
                lax.dynamic_slice_in_dim(w_query, c * qw, qw, 1),
                lax.dynamic_slice_in_dim(key_weight, c * kw, kw, 1),
                lax.dynamic_slice_in_dim(value_weight, c * kw, kw, 1),
            ],
            axis=1,
        )

    params_t = jnp.concatenate([attn_gain[None], ffn_gain[None], w_router.T], axis=0)
    p_rows = params_t.shape[0]
    params_t = jnp.pad(params_t, ((0, 0), (0, tok - rows)))
    note = jnp.concatenate([routes[0].T.astype(bf16), params_t], axis=0)
    k_of = jnp.arange(n_dp, dtype=jnp.int32)
    d_of = lax.rem(dx - k_of + n_dp, n_dp)
    c_of = cx ^ jnp.arange(n_ctx, dtype=jnp.int32)
    places = (c_of[None, :] * n_dp + d_of[:, None]).reshape(-1).astype(jnp.int32)

    def own_params(stack):
        stack = stack.reshape(n_dp * n_ctx, p_rows, -1)[:, :, :rows]
        at = d_of[None, :] * n_ctx + (cx ^ jnp.arange(n_ctx, dtype=jnp.int32))[:, None]
        flat = stack[at.reshape(-1)].transpose(1, 0, 2).reshape(p_rows, MODEL_WIDTH)
        router = jnp.pad(flat[2:].T, ((0, 0), (0, LANES // 2 - experts)))
        return flat[0:1].astype(f32), flat[1:2].astype(f32), router

    def own_routes(stack):
        return stack.reshape(experts, top, tok).astype(jnp.int32)

    def positions(order_row, lengths_row):
        order_rel = order_row.reshape(n_ctx, tok)[c_of].reshape(-1)
        both = jnp.concatenate([order_rel, jnp.arange(total, dtype=jnp.int32)])
        end = jnp.zeros((), jnp.int32)
        start = jnp.zeros_like(both)
        for j in range(lengths_row.shape[0]):
            end = end + lengths_row[j]
            start = start + jnp.where(both >= end, lengths_row[j], 0)
        lane = jnp.arange(LANES, dtype=jnp.int32) % HEAD_SIZE
        half = HEAD_SIZE // 2
        freq = ROPE_BASE ** (-((lane % half).astype(f32) * 2.0 / HEAD_SIZE))

        def tables(places):
            angle = places.astype(f32)[:, None] * freq[None, :]
            return jnp.cos(angle), jnp.where(lane < half, -1.0, 1.0)[None] * jnp.sin(angle)

        places_s = (both - start)[total:]
        turned = freq[:half, None] * places_s.astype(f32)[None, :]
        placed = (*tables(places_s), jnp.cos(turned), jnp.sin(turned))
        dealt = tables((both - start)[:total])
        return (order_rel[None, :], order_rel[:, None], start[None, total:], *dealt, *placed)

    order_row, ends_in = token_order[0], lengths[0]

    def gather_plane(v):
        return lax.all_gather(v, PLANE, axis=0, tiled=False)

    def gather_out(v):
        return lax.all_gather(v, "dp", axis=0, tiled=True)

    x_own, dy_own = hidden[0], cotangent[0]
    if small_plane():
        part = rows // 2

        def half_for(c):
            return lax.dynamic_slice_in_dim(for_context(c), ex * part, part, 0)

        got = [half_for(cx)] + [flip(half_for(cx ^ m), "context", m) for m in range(1, n_ctx)]
        note2 = jnp.stack([note, flip(note, "context", 2)])
        x2 = flip(x_own, "context", 2)
        dy0 = plane_near(dy_own)
        w0, note2, dy0 = sync(jnp.stack(got), note2, dy0)
        mine, theirs = [w0], []
        for k in range(n_dp - 1):
            nxt, other = step_up(mine[-1], "dp"), flip(mine[-1], "expert", 1)
            if k == 0:
                near = flip(note2, "context", 1)
                note4 = jnp.stack([note2[0], near[0], note2[1], near[1]])
                nxt, other, note4, order_row, ends_in = sync(nxt, other, note4, order_row, ends_in)
            elif k == 1:
                shards = send_all(note4[:, top:], "dp")
                routes_far = flip(note4[:, :top], "expert", 1)
                nxt, other, x2, routes_far, *shards = sync(nxt, other, x2, routes_far, *shards)
                x1, x3 = flip(x_own, "context", 1), flip(x2, "context", 1)
                gain_a, gain_b, router = own_params(jnp.stack(shards))
                where = positions(order_row, ends_in)
            elif k == 2:
                nxt, other, gain_a, *where = sync(nxt, other, gain_a, *where)
                h1 = norm_rows([x_own, x1, x2, x3], gain_a)
                dy1 = hop_plane(after(dy0, x2), False)
            mine.append(nxt)
            theirs.append(other)
        theirs.append(flip(mine[-1], "expert", 1))
        c = lax.rem(cx, 2)
        routes_rel = jnp.stack([note4[:, :top], routes_far]).reshape(8, top, tok)
        even = jnp.array([0, 1, 2, 3, 4, 5, 6, 7], jnp.int32)
        odd = jnp.array([0, 1, 4, 5, 2, 3, 6, 7], jnp.int32)
        routes_all = own_routes(routes_rel[jnp.where(c == 0, even, odd)])
        theirs[-1], router, h1, routes_all, dy1 = sync(theirs[-1], router, h1, routes_all, dy1)
        wo = gather_out(after(w_out, mine[-1]))
        dy2, dy3 = plane_far(dy0, dy1)
        w_pieces = mine + theirs
        spots = jnp.concatenate(
            [places, places, jnp.broadcast_to(ex, (n_dp,)), jnp.broadcast_to(1 - ex, (n_dp,))]
        ).astype(jnp.int32)
    else:
        got = [for_context(cx)]
        for m in range(1, n_ctx):
            got.append(flip(for_context(cx ^ m), "context", m))
        w_pieces = ring(jnp.stack(got), "dp")
        note4 = jnp.stack(ctx_gather(note))
        gain_a, gain_b, router = own_params(jnp.stack(send_all(note4[:, top:], "dp")))
        routes_all = own_routes(lax.all_gather(note[:top], PLANE, axis=0, tiled=False))
        h1 = norm_rows(ctx_gather(x_own), gain_a)
        dy_all, wo = gather_plane(cotangent[0]), gather_out(w_out)
        spots = jnp.concatenate([places, jnp.zeros((n_dp,), jnp.int32)])
        where = positions(order_row, ends_in)
    row, col, start_row, cos_d, sin_d, *placed = where
    near, far, q, k, v, lse, wqkv = attn_fwd(
        spots, w_pieces, n_dp, h1, row, col, start_row, cos_d, sin_d, qh, kvh
    )
    if small_plane():
        near, wo, dy2, dy3 = sync(near, wo, dy2, dy3)
        dy_list = plane_share((dy0, dy1, dy2, dy3))
    else:
        dy_list = [dy_all]
    partial_far = dot(far.reshape(-1, qw), wo).astype(bf16).reshape(-1, tok, MODEL_WIDTH)
    partial_near = dot(near.reshape(-1, qw), wo).astype(bf16).reshape(-1, tok, MODEL_WIDTH)
    late_gate = after(w_gate[0], partial_near)
    w_cat = jnp.concatenate([late_gate, w_up[0], router, router], axis=1)
    branch = ctx_sum([partial_near[0], partial_near[1], partial_far[0], partial_far[1]])
    branch, w_cat, *dy_list = sync(branch, w_cat, *dy_list)
    x_own = x_own.astype(f32)
    middle = x_own + branch
    r_b = lax.rsqrt(jnp.mean(middle * middle, axis=-1, keepdims=True) + NORM_EPS)
    h2 = (middle * r_b * gain_b).astype(bf16)
    h_list = plane_gather(h2)

    by_hand = small_plane()
    who = jnp.stack([my_expert, cx % 2]).astype(jnp.int32)
    out = run_experts(
        who, by_hand, h_list, dy_list, routes_all, w_cat, w_down[0], cap, tok
    )
    n_rows = 2 if by_hand else 1
    d_rows, y_rows, (xs, deout, act, dgate, dup, coef) = (
        out[:n_rows], out[n_rows : 2 * n_rows], out[2 * n_rows :],
    )
    d_sum, y_sum = PlaneSum(d_rows), PlaneSum(y_rows)
    small = small_plane()
    xs_late, deout_late = (after(xs, d_sum.far), after(deout, d_sum.far)) if small else (xs, deout)
    g_gate = dot(xs_late, dgate, TN).astype(bf16)
    g_up = dot(xs_late, dup, TN).astype(bf16)
    g_down = dot(deout_late, act, TN).astype(bf16)
    g_router = dot(xs_late, coef, TN)
    g_router = g_router[:, :experts] + g_router[:, LANES // 2 : LANES // 2 + experts]

    def over_dp(g, dim):
        return lax.psum_scatter(g, "dp", scatter_dimension=dim, tiled=True).astype(f32)

    if small:
        d_sum.first()
        sum_gate, sum_up, sum_down = over_dp(g_gate, 0), over_dp(g_up, 0), over_dp(g_down, 0)
        d_sum.got2, y_sum.far, g_gate, g_up, g_down, g_router = sync(
            d_sum.got2, y_sum.far, g_gate, g_up, g_down, g_router
        )
        d_sum.second()
    else:
        sum_gate, sum_up, sum_down = over_dp(g_gate, 0), over_dp(g_up, 0), over_dp(g_down, 0)
    dh2 = d_sum.finish()
    dy = dy_own.astype(f32)
    d_norm, g_gain_b = rms_back(dh2, middle, r_b, gain_b)
    d_middle = dy + d_norm
    if small:
        b0 = d_middle.astype(bf16)
        b2, b1 = flip(b0, "context", 2), flip(b0, "context", 1)
        b2, b1 = sync(b2, b1)
        db_pieces = [b0, b1, b2, flip(b2, "context", 1)]
        y_sum.far = after(y_sum.far, b2)
        y_sum.first()
    else:
        db_pieces = ctx_gather(d_middle.astype(bf16))
    db_all = jnp.concatenate(db_pieces, axis=0)
    attn = jnp.concatenate([near, far], axis=0).reshape(total, qw)
    g_out = dot(attn, db_all, TN).astype(bf16)
    db_last = after(db_pieces[-1], g_out, sum_gate)

    dqkv = attn_bwd(
        db_pieces[:-1] + [db_last], wo, near, far, q, k, v, lse, row, col, start_row, placed, qh, kvh
    )
    dqkv, sum_up = sync(dqkv, sum_up)
    dqkv_flat = dqkv.reshape(total, -1)
    h1_flat = h1.reshape(total, MODEL_WIDTH)
    g_qkv = dot(h1_flat, dqkv_flat, TN).astype(bf16)
    w_flat = wqkv.reshape(MODEL_WIDTH, -1)
    if small:
        part = rows // 2
        g5 = g_qkv.reshape(n_ctx * n_dp, 2, part, -1)
        theirs = lax.dynamic_index_in_dim(g5, 1 - ex, 1, keepdims=False)
        mine = lax.dynamic_index_in_dim(g5, ex, 1, keepdims=False)
        got = flip(theirs, "expert", 1)
        dh1_in = after(dqkv_flat, theirs, mine)
    else:
        dh1_in = dqkv_flat
    dh1_part = dot(dh1_in, w_flat, NT).astype(bf16)
    g_gain_a = jnp.sum(dh1_part.astype(f32) * h1_flat.astype(f32), axis=0) / gain_a[0]
    dh1_part = dh1_part.reshape(n_ctx, tok, MODEL_WIDTH)
    r_a = lax.rsqrt(jnp.mean(x_own * x_own, axis=-1, keepdims=True) + NORM_EPS)

    width = qw + 2 * kw
    s_out = lax.psum_scatter(g_out, "dp", scatter_dimension=0, tiled=True)

    def exchange(s):
        back = [lax.dynamic_index_in_dim(s, cx, 0, keepdims=False)]
        for m in range(1, n_ctx):
            one = lax.dynamic_index_in_dim(s, cx ^ m, 0, keepdims=False)
            back.append(flip(one, "context", m))
        return jnp.stack(back)

    tiny = jnp.concatenate([g_gain_a[None], g_gain_b[None], g_router.T], axis=0)

    def finish_rows(dh1):
        return (d_middle + rms_back(dh1, x_own, r_a, gain_a)[0]).astype(bf16)

    def spread(tiny):
        tiny = tiny.reshape(-1, n_ctx * n_dp, rows).transpose(1, 0, 2)
        tiny = lax.all_to_all(tiny, ("context", "dp"), split_axis=0, concat_axis=0, tiled=True)
        return jnp.sum(tiny, axis=0)

    if small:
        h3 = flip(dh1_part[3], "context", 1)
        hop = flip(add_low(dh1_part[2], h3), "context", 2)
        h1p = flip(dh1_part[1], "context", 1)
        dh1 = dh1_part[0].astype(f32) + h1p.astype(f32)
        y_sum.got2 = after(y_sum.got2, dqkv)
        got, hop, dh1, y_sum.got2, sum_down, s_out, tiny = sync(
            got, hop, dh1, y_sum.got2, sum_down, s_out, tiny
        )
        both_g = add_low(mine, got).reshape(n_ctx, n_dp, part, width)
        s_qkv = ring_sum(lambda d: lax.dynamic_index_in_dim(both_g, d, 1, keepdims=False), "dp")
        y_sum.got2 = after(y_sum.got2, both_g)
        y_sum.second()
        tiny = after(tiny, both_g)
        tiny = spread(tiny + flip(tiny, "expert", 1))
        grad_input = finish_rows(after(dh1, both_g) + hop.astype(f32))
        out_low = s_out.astype(bf16)
        s_qkv, out_low, y_sum.got1, grad_input, tiny = sync(
            s_qkv, out_low, y_sum.got1, grad_input, tiny
        )
        out_far = flip(out_low, "expert", 1)
        output = (middle + y_sum.finish()).astype(bf16)
        s_out = out_low.astype(f32) + out_far.astype(f32)
        near = exchange(s_qkv.astype(bf16))
        far = flip(near, "expert", 1)
        spots = jnp.concatenate([c_of, ex[None], 1 - ex[None]]).astype(jnp.int32)
        sum_q, sum_k, sum_v = columns_of(spots, near, far, qw, kw)
    else:
        dh1 = ctx_sum([dh1_part[m] for m in range(n_ctx)])
        grad_input = finish_rows(dh1)
        tiny = spread(lax.psum(tiny, "expert"))
        g4 = g_qkv.reshape(n_ctx, n_dp, rows, width)
        s_qkv = direct_sum(lambda d: lax.dynamic_index_in_dim(g4, d, 1, keepdims=False), "dp")
        s_qkv = lax.psum(s_qkv.astype(bf16), "expert")
        s_out = lax.psum(s_out.astype(bf16), "expert").astype(f32)
        back = exchange(s_qkv)[c_of]

        def columns(lo, hi):
            return back[:, :, lo:hi].transpose(1, 0, 2).reshape(rows, -1).astype(f32)

        sum_q, sum_k, sum_v = columns(0, qw), columns(qw, qw + kw), columns(qw + kw, width)
        output = (middle + y_sum.finish()).astype(bf16)

    return (
        output[None], grad_input[None], tiny[0], sum_q, sum_k, sum_v, s_out,
        tiny[1], tiny[2:].T, sum_gate[None], sum_up[None], sum_down.T[None],
    )


def solution(mesh):
    tokens = P(("expert", "dp"), "context", None)
    group = P(("expert", "dp"), None)
    vec, mat = P(("context", "dp")), P(("context", "dp"), None)
    expert = P(("expert", "context"), None, None)
    by_rows = P(("expert", "context"), "dp", None)
    by_cols = P(("expert", "context"), None, "dp")
    return jax.shard_map(
        body,
        mesh=mesh,
        in_specs=(
            tokens, tokens, group, group, tokens, vec, mat, mat, mat, mat, vec, mat,
            expert, expert, expert,
        ),
        out_specs=(
            tokens, tokens, vec, mat, mat, mat, mat, vec, mat, by_rows, by_rows, by_cols,
        ),
        check_vma=False,
    )
```

time: 538 us -> 432 us (0.80)
  waiting for transfers between devices: 223 us -> 150 us
  Pallas kernels: 131 us -> 91.4 us
  starting transfers between devices: 67 us -> 50.5 us
  between operations: 4.25 us -> 17.3 us
  other arithmetic: 49 us -> 60 us
  local copies, waits for them, and re-layouts: 35.4 us -> 26.3 us
  matrix products: 22.8 us -> 31.8 us
    ppermute x24 -> x6, waiting for transfers between devices: 115 us -> 16.1 us  [step_up(): return lax.ppermute(v, axis, [(i, (i + 1) % n) for i in range(n)])]
    ppermute x0 -> x13, waiting for transfers between devices: none -> 62.7 us  [the longest x10 60.3 us: hop_plane(): return lax.ppermute(v, PLANE, pairs)]
    pallas_call x3 -> x4, Pallas kernels: 98.2 us -> 63.8 us  [the longest x1 30.8 us: run_experts(): pl.pallas_call(functools.partial(expert_kernel, by_hand, cap), out_shape=...]
    ppermute x71 -> x43, waiting for transfers between devices: 105 us -> 71.1 us  [flip(): return lax.ppermute(v, axis, [(i, i ^ bit) for i in range(n)])]
    ppermute x71 -> x43, starting transfers between devices: 48.6 us -> 24.8 us  [flip(): return lax.ppermute(v, axis, [(i, i ^ bit) for i in range(n)])]
    ppermute x0 -> x13, starting transfers between devices: none -> 13.3 us  [the longest x10 8.88 us: hop_plane(): return lax.ppermute(v, PLANE, pairs)]
    add x5 -> x10, other arithmetic: 1.57 us -> 14.6 us  [the longest x2 5.32 us: second(): self.keep[:2].astype(f32) + self.got[:2].astype(f32) + self.got2.astype(f32)]
    dot_general x9, matrix products: 22.8 us -> 31.8 us  [dot(): return lax.dot_general(a, b, dims, preferred_element_type=f32)]
  transfers between devices with their start and end apart: 96 -> 68, of which waited for: 41 -> 23; matrix products, arithmetic and copies ran while one was open for 17% -> 24% of each run, Pallas kernels for 11% -> 14%
where the time goes in v2:
time: 432 us; the launch traced here: 428 us
  waiting for transfers between devices  150 us (35%)
  Pallas kernels  91.4 us (21%)
  other arithmetic  60 us (14%)
  starting transfers between devices  50.5 us (12%)
  matrix products  31.8 us (7%)
  local copies, waits for them, and re-layouts  26.3 us (6%)
  between operations  17.3 us (4%)
    ppermute x43, waiting for transfers between devices, flip(): return lax.ppermute(v, axis, [(i, i ^ bit) for i in range(n)])  71.1 us
    ppermute x10, waiting for transfers between devices, hop_plane(): return lax.ppermute(v, PLANE, pairs)  60.3 us
    dot_general x9, matrix products, dot(): return lax.dot_general(a, b, dims, preferred_element_type=f32)  31.8 us
    pallas_call x1, Pallas kernels, run_experts(): pl.pallas_call(functools.partial(expert_kernel, by_hand, cap), out_shape=...  30.8 us
    pallas_call x1, Pallas kernels, attn_bwd(): pl.pallas_call(functools.partial(attn_bwd_kernel, n_ctx, qh, kvh), out_sh...  27.6 us
    ppermute x43, starting transfers between devices, flip(): return lax.ppermute(v, axis, [(i, i ^ bit) for i in range(n)])  24.8 us
    pallas_call x1, Pallas kernels, attn_fwd(): pl.pallas_call(functools.partial(attn_fwd_kernel, n_ctx, n_w, qh, kvh), o...  24.4 us
    ppermute x6, waiting for transfers between devices, step_up(): return lax.ppermute(v, axis, [(i, (i + 1) % n) for i in range(n)])  16.1 us
  transfers between devices with their start and end apart: 68, of which 23 were waited for; matrix products, arithmetic and copies ran while one was open for 24% of the time, Pallas kernels for 14%

profile of v2, /device:TPU:0, one launch (start us, length us, event | category | flops | bytes accessed | tf_op | source)
XLA Modules:
  0.0 427.6 jit_solution(5144336399100987343)
XLA Ops:
  9.5 3.0 collective-permute-start.1
  15.2 1.8 collective-permute-done.3
  19.0 1.8 collective-permute-start.5
  20.9 1.5 collective-permute-start.6
  22.4 7.1 %collective-permute-done.5.refs_1_ = bf16[4,48,640]{2,1,0:T(8,128)(2,1)S(1)} collective-permute-done((bf16[4,48,640]{2,1,0:T(8,128)(2,1)S(1)}, bf16[4,48,640]{2,1,0:T(8,128)(2,1)S(1)}, u32[]{:S(2)}, u32[]{:S(2)}) %collective-permute-start.5) | collective-permute-done | bytes 245792 | tf_op jit(solution)/shard_map/ppermute | solution.py:578
  30.5 1.5 collective-permute-start.9
  32.6 1.6 collective-permute-start.12
  37.4 1.9 fusion.47
  39.4 1.9 collective-permute-start.13
  42.7 1.6 collective-permute-done.13
  45.3 5.5 %fusion.25 = (f32[1024,128]{1,0:T(8,128)}, f32[1024,128]{1,0:T(8,128)}, f32[1024,128]{1,0:T(8,128)}, f32[1024,128]{1,0:T(8,128)}) fusion(f32[1024]{0:T(1024)S(1)} %get-tuple-element.290, f32[128]{0:T(128)S(1)} %get-tuple-element.315, f32[128]{0:T(128)S(1)} %get-tuple-element.316, f32[1024]{0:T(1024)S(1)} %get-tuple-element.291), kind=kLoop, calls=%fused_computation.77 | loop fusion | flops 524288 | bytes 2106368 | tf_op jit(solution)/shard_map/mul | solution.py:837
  53.8 1.5 collective-permute-start.16
  58.2 5.4 %collective-permute-done.15.refs_3_ = bf16[4,48,640]{2,1,0:T(8,128)(2,1)S(1)} collective-permute-done((bf16[4,48,640]{2,1,0:T(8,128)(2,1)}, bf16[4,48,640]{2,1,0:T(8,128)(2,1)S(1)}, u32[]{:S(2)}, u32[]{:S(2)}) %collective-permute-start.15) | collective-permute-done | bytes 245792 | tf_op jit(solution)/shard_map/ppermute | solution.py:578
  64.1 1.5 collective-permute-start.17
  66.9 6.6 %norm_rows.1.refs_8_ = bf16[4,256,1536]{2,1,0:T(8,128)(2,1)} custom-call(bf16[256,1536]{1,0:T(8,128)(2,1)} %bitcast.175, bf16[256,1536]{1,0:T(8,128)(2,1)} %collective-permute-done.18.refs_1_, bf16[256,1536]{1,0:T(8,128)(2,1)} %copy-done.37, bf16[256,1536]{1,0:T(8,128)(2,1)} %collective-permute-done.19.refs_3_, f32[1,1536]{1,0:T(1,128)} %reshape.283.refs_4_), custom_call_target="tpu_custom_call" | custom-call | flops 3000000000 | bytes 6000000 | tf_op jit(solution)/shard_map/norm_rows/pallas_call | solution.py:81
  73.5 7.9 %collective-permute-done.17.refs_7_ = bf16[4,48,640]{2,1,0:T(8,128)(2,1)S(1)} collective-permute-done((bf16[4,48,640]{2,1,0:T(8,128)(2,1)S(1)}, bf16[4,48,640]{2,1,0:T(8,128)(2,1)S(1)}, u32[]{:S(2)}, u32[]{:S(2)}) %collective-permute-start.17) | collective-permute-done | bytes 245792 | tf_op jit(solution)/shard_map/ppermute | solution.py:573
  81.5 1.5 collective-permute-start.22
  82.9 24.4 %attn_fwd.1 = (bf16[2,256,384]{2,1,0:T(8,128)(2,1)}, bf16[2,256,384]{2,1,0:T(8,128)(2,1)}, bf16[6,1024,128]{2,1,0:T(8,128)(2,1)}, bf16[2,1024,128]{2,1,0:T(8,128...) custom-call(s32[40]{0:T(128)} %pad_add_fusion.1.place_ref, ...), custom_call_target="tpu_custom_call" | custom-call | flops 20000000000 | bytes 20000000 | tf_op jit(solution)/shard_map/attn_fwd/pallas_call | solution.py:220
  107.4 2.4 convolution_convert_fusion.4
  116.1 6.1 %concatenate.53.refs_17_ = bf16[1536,1152]{1,0:T(8,128)(2,1)} concatenate(bf16[1536,512]{1,0:T(8,128)(2,1)S(1)} %bitcast.185, bf16[1536,512]{1,0:T(8,128)(2,1)} %bitcast.186, bf16[1536,64]{1,0:T(8,128)(2,1)S(1)} %pad.9, bf16[1536,64]{1,0:T(8,128)(2,1)S(1)} %pad.9), dimensions={1} | concatenate | bytes 7077888 | tf_op jit(solution)/shard_map/concatenate | solution.py:922
  122.2 11.4 %collective-permute-done.25 = bf16[256,1536]{1,0:T(8,128)(2,1)} collective-permute-done((bf16[256,1536]{1,0:T(8,128)(2,1)}, bf16[256,1536]{1,0:T(8,128)(2,1)}, u32[]{:S(2)}, u32[]{:S(2)}) %collective-permute-start.25) | collective-permute-done | bytes 786464 | tf_op jit(solution)/shard_map/ppermute | solution.py:573
  133.6 1.6 convert_add_fusion.5
  135.9 1.7 collective-permute-done.30
  139.3 18.5 %collective-permute-done.31.refs_1_ = bf16[2,256,768]{2,1,0:T(8,128)(2,1)S(1)} collective-permute-done((bf16[2,256,768]{2,1,0:T(8,128)(2,1)S(1)}, bf16[2,256,768]{2,1,0:T(8,128)(2,1)S(1)}, u32[]{:S(2)}, u32[]{:S(2)}) %collective-permute-start.31) | collective-permute-done | bytes 786464 | tf_op jit(solution)/shard_map/ppermute | solution.py:651
  159.1 10.7 %collective-permute-done.33.refs_3_ = bf16[2,256,768]{2,1,0:T(8,128)(2,1)} collective-permute-done((bf16[2,256,768]{2,1,0:T(8,128)(2,1)S(1)}, bf16[2,256,768]{2,1,0:T(8,128)(2,1)}, u32[]{:S(2)}, u32[]{:S(2)}) %collective-permute-start.33) | collective-permute-done | bytes 786464 | tf_op jit(solution)/shard_map/ppermute | solution.py:651
  170.5 2.0 collective-permute-done.37.refs_7_
  172.5 30.8 %experts.1 = (bf16[4,2,256,768]{3,2,1,0:T(8,128)(2,1)}, bf16[4,2,256,768]{3,2,1,0:T(8,128)(2,1)}, bf16[4,2,256,768]{3,2,1,0:T(8,128)(2,1)}, bf16[4,2,256,768]{3,...) custom-call(s32[2]{0:T(128)} %pad_add_fusion.2.who_ref, ...), custom_call_target="tpu_custom_call" | custom-call | flops 30000001024 | bytes 30000000 | tf_op jit(solution)/shard_map/experts/pallas_call | solution.py:558
  203.8 8.5 %collective-permute-done.39 = bf16[4,2,256,768]{3,2,1,0:T(8,128)(2,1)S(1)} collective-permute-done((bf16[4,2,256,768]{3,2,1,0:T(8,128)(2,1)}, bf16[4,2,256,768]{3,2,1,0:T(8,128)(2,1)S(1)}, u32[]{:S(2)}, u32[]{:S(2)}) %collective-permute-start.39) | collective-permute-done | bytes 3145760 | tf_op jit(solution)/shard_map/ppermute | solution.py:573
  212.3 3.0 add_convert_fusion.1
  216.2 3.4 convolution_convert_fusion.2
  219.7 5.8 %convolution_convert_fusion.3 = bf16[1536,512]{1,0:T(8,128)(2,1)} fusion(bf16[1152,1536]{1,0:T(8,128)(2,1)} %get-tuple-element.161, bf16[1152,512]{1,0:T(8,128)(2,1)} %get-tuple-element.162), kind=kOutput, calls=%fused_computation.21 | convolution fusion | flops 1812725760 | bytes 6291456 | tf_op jit(solution)/shard_map/dot_general | solution.py:38
  225.5 2.9 fusion.63
  229.0 3.1 add_convert_fusion
  232.2 3.4 convolution_convert_fusion.1
  235.9 2.9 convert_add_fusion.1
  239.8 11.2 %collective-permute-done.41 = bf16[2,256,768]{2,1,0:T(8,128)(2,1)S(1)} collective-permute-done((bf16[2,256,768]{2,1,0:T(8,128)(2,1)S(1)}, bf16[2,256,768]{2,1,0:T(8,128)(2,1)S(1)}, u32[]{:S(2)}, u32[]{:S(2)}) %collective-permute-start.41) | collective-permute-done | bytes 786464 | tf_op jit(solution)/shard_map/ppermute | solution.py:651
  251.4 1.8 collective-permute-done.42
  255.4 1.7 fusion.57
  257.9 18.9 %collective-permute-done.43.refs_2_ = bf16[256,1536]{1,0:T(8,128)(2,1)} collective-permute-done((bf16[256,1536]{1,0:T(8,128)(2,1)S(1)}, bf16[256,1536]{1,0:T(8,128)(2,1)}, u32[]{:S(2)}, u32[]{:S(2)}) %collective-permute-start.43) | collective-permute-done | bytes 786464 | tf_op jit(solution)/shard_map/ppermute | solution.py:573
  278.8 2.0 convert_element_type.313
  280.8 4.1 fusion.9
  284.9 27.6 %attn_bwd.1 = bf16[4,256,640]{2,1,0:T(8,128)(2,1)} custom-call(bf16[256,1536]{1,0:T(8,128)(2,1)} %copy-done.17, bf16[256,1536]{1,0:T(8,128)(2,1)} %copy-done.39, bf16[256,1536]{1,0:T(8,128)(2,1)} %collective-permute-done.43.refs_2_, bf16[256,1536]{1,0:T(8,128)(2,1)} %collective-permute-done.45.refs_3_, ...), custom_call_target="tpu_custom_call" | custom-call | flops 24999999488 | bytes 20000000 | tf_op jit(solution)/shard_map/attn_bwd/pallas_call | solution.py:368
  312.5 4.0 bitcast_convert_fusion
  318.3 5.0 %fusion = (f32[1536]{0:T(1024)S(1)}, bf16[1024,1536]{1,0:T(8,128)(2,1)S(1)}) fusion(bf16[4,256,1536]{2,1,0:T(8,128)(2,1)} %norm_rows.1.refs_8_, bf16[1024,640]{1,0:T(8,128)(2,1)S(1)} %bitcast.229, bf16[1536,640]{1,0:T(8,128)(2,1)} %bitcast.228), kind=kOutput, calls=%fused_computation.4 | convolution fusion | flops 2021128704 | bytes 9574400 | tf_op jit(solution)/shard_map/dot_general | solution.py:38
  323.4 1.6 copy-done.8
  328.5 3.1 convert_add_fusion.4
  333.2 2.0 convert_element_type.321
  335.2 2.0 convert_bitcast_fusion
  337.2 19.5 %collective-permute-done.50 = bf16[2,2,256,768]{3,2,1,0:T(8,128)(2,1)} collective-permute-done((bf16[2,2,256,768]{3,2,1,0:T(8,128)(2,1)}, bf16[2,2,256,768]{3,2,1,0:T(8,128)(2,1)}, u32[]{:S(2)}, u32[]{:S(2)}) %collective-permute-start.50) | collective-permute-done | bytes 1572896 | tf_op jit(solution)/shard_map/ppermute | solution.py:651
  356.7 10.5 %collective-permute-done.46 = bf16[16,48,640]{2,1,0:T(8,128)(2,1)} collective-permute-done((bf16[16,48,640]{2,1,0:T(8,128)(2,1)}, bf16[16,48,640]{2,1,0:T(8,128)(2,1)}, u32[]{:S(2)}, u32[]{:S(2)}) %collective-permute-start.46) | collective-permute-done | bytes 983072 | tf_op jit(solution)/shard_map/ppermute | solution.py:573
  367.2 1.9 add_convert_fusion.2
  371.2 2.4 convert_add_fusion
  375.4 1.6 fusion.12
  377.0 1.7 collective-permute-done.51
  381.5 5.6 %all-to-all-start = ((f32[16,1,960]{2,1,0:T(1,128)}), f32[16,1,960]{2,1,0:T(1,128)S(1)}, u32[]{:S(2)}, u32[]{:S(2)}) async-start(f32[16,1,960]{2,1,0:T(1,128)} %reshape.328), calls=%async_computation.4 | async-start | bytes 131072 | tf_op jit(solution)/shard_map/all_to_all | solution.py:1018
  387.8 1.8 fusion.27
  389.6 1.6 collective-permute-start.53
  391.2 3.3 fusion.16
  394.4 2.3 copy.47
  402.0 1.7 collective-permute-start.58
  403.8 1.8 fusion.18
  408.7 1.8 convert_add_fusion.6
  410.6 5.6 %collective-permute-done.60.far_ref = bf16[4,48,640]{2,1,0:T(8,128)(2,1)} collective-permute-done((bf16[4,48,640]{2,1,0:T(8,128)(2,1)S(1)}, bf16[4,48,640]{2,1,0:T(8,128)(2,1)}, u32[]{:S(2)}, u32[]{:S(2)}) %collective-permute-start.60) | collective-permute-done | bytes 245792 | tf_op jit(solution)/shard_map/ppermute | solution.py:573
  416.2 2.1 columns_of.1
  (314 shorter events, 64.1 us)
Async XLA Ops:
  7.2 100.1 %all-gather.2.cloned.1.call-start = ((), (), s32[]{:S(2)}) async-start(), calls=%async_computation.5 | async-start | bytes 1474560 | tf_op jit(solution)/shard_map/all_gather | solution.py:851
  8.6 9.4 %collective-permute-start.4 = (bf16[256,768]{1,0:T(8,128)(2,1)S(1)}, bf16[256,768]{1,0:T(8,128)(2,1)S(1)}, u32[]{:S(2)}, u32[]{:S(2)}) collective-permute-start(bf16[256,768]{1,0:T(8,128)(2,1)S(1)} %get-tuple-element.265), channel_id=1, source_target_pairs={{0,4},{4,0},{8,12},{12,8},{1,5},{5,1},{9,13},{13,9},{2,6},{6,2},{1... | collective-permute-start | bytes 1179656 | tf_op jit(solution)/shard_map/ppermute | solution.py:573
  9.3 8.7 %collective-permute-start = (bf16[48,640]{1,0:T(8,128)(2,1)S(1)}, bf16[48,640]{1,0:T(8,128)(2,1)S(1)}, u32[]{:S(2)}, u32[]{:S(2)}) collective-permute-start(bf16[48,640]{1,0:T(8,128)(2,1)S(1)} %fusion.36), channel_id=1, source_target_pairs={{0,4},{4,0},{8,12},{12,8},{1,5},{5,1},{9,13},{13,9},{2,6},{6,2},{1... | collective-permute-start | bytes 184328 | tf_op jit(solution)/shard_map/ppermute | solution.py:573
  9.5 8.5 %collective-permute-start.1 = (bf16[48,640]{1,0:T(8,128)(2,1)S(1)}, bf16[48,640]{1,0:T(8,128)(2,1)S(1)}, u32[]{:S(2)}, u32[]{:S(2)}) collective-permute-start(bf16[48,640]{1,0:T(8,128)(2,1)S(1)} %fusion.34), channel_id=1, source_target_pairs={{0,8},{4,12},{8,0},{12,4},{1,9},{5,13},{9,1},{13,5},{2,10},{6,14},... | collective-permute-start | bytes 184328 | tf_op jit(solution)/shard_map/ppermute | solution.py:573
  12.5 5.5 %collective-permute-start.2 = (bf16[48,640]{1,0:T(8,128)(2,1)S(1)}, bf16[48,640]{1,0:T(8,128)(2,1)S(1)}, u32[]{:S(2)}, u32[]{:S(2)}) collective-permute-start(bf16[48,640]{1,0:T(8,128)(2,1)S(1)} %fusion.32), channel_id=1, source_target_pairs={{0,12},{4,8},{8,4},{12,0},{1,13},{5,9},{9,5},{13,1},{2,14},{6,10},... | collective-permute-start | bytes 184328 | tf_op jit(solution)/shard_map/ppermute | solution.py:573
  12.7 4.3 %collective-permute-start.3 = (bf16[14,256]{1,0:T(8,128)(2,1)S(1)}, bf16[14,256]{1,0:T(8,128)(2,1)S(1)}, u32[]{:S(2)}, u32[]{:S(2)}) collective-permute-start(bf16[14,256]{1,0:T(8,128)(2,1)S(1)} %pad_maximum_fusion.11), channel_id=1, source_target_pairs={{0,8},{4,12},{8,0},{12,4},{1,9},{5,13},{9,1},{13,5},{2,10},{6,14},... | collective-permute-start | bytes 21512 | tf_op jit(solution)/shard_map/ppermute | solution.py:573
  17.0 28.2 %collective-permute-start.10 = (bf16[256,1536]{1,0:T(8,128)(2,1)S(1)}, bf16[256,1536]{1,0:T(8,128)(2,1)S(1)}, u32[]{:S(2)}, u32[]{:S(2)}) collective-permute-start(bf16[256,1536]{1,0:T(8,128)(2,1)S(1)} %bitcast.176), channel_id=1, source_target_pairs={{0,8},{4,12},{8,0},{12,4},{1,9},{5,13},{9,1},{13,5},{2,10},{6,14},... | collective-permute-start | bytes 2359304 | tf_op jit(solution)/shard_map/ppermute | solution.py:573
  19.0 3.3 collective-permute-start.7
  19.0 10.5 %collective-permute-start.5 = (bf16[4,48,640]{2,1,0:T(8,128)(2,1)S(1)}, bf16[4,48,640]{2,1,0:T(8,128)(2,1)S(1)}, u32[]{:S(2)}, u32[]{:S(2)}) collective-permute-start(bf16[4,48,640]{2,1,0:T(8,128)(2,1)S(1)} %pad_maximum_fusion.4.refs_0_), channel_id=1, source_target_pairs={{0,1},{1,2},{2,3},{3,0},{4,5},{5,6},{6,7},{7,4},{8,9},{9,10},{10,1... | collective-permute-start | bytes 737288 | tf_op jit(solution)/shard_map/ppermute | solution.py:578
  20.9 8.7 %collective-permute-start.6 = (bf16[4,48,640]{2,1,0:T(8,128)(2,1)S(1)}, bf16[4,48,640]{2,1,0:T(8,128)(2,1)S(1)}, u32[]{:S(2)}, u32[]{:S(2)}) collective-permute-start(bf16[4,48,640]{2,1,0:T(8,128)(2,1)S(1)} %pad_maximum_fusion.4.refs_0_), channel_id=1, source_target_pairs={{0,16},{16,0},{1,17},{17,1},{2,18},{18,2},{3,19},{19,3},{4,20},{20... | collective-permute-start | bytes 737288 | tf_op jit(solution)/shard_map/ppermute | solution.py:573
  29.5 15.7 %collective-permute-start.8 = (bf16[4,48,640]{2,1,0:T(8,128)(2,1)S(1)}, bf16[4,48,640]{2,1,0:T(8,128)(2,1)}, u32[]{:S(2)}, u32[]{:S(2)}) collective-permute-start(bf16[4,48,640]{2,1,0:T(8,128)(2,1)S(1)} %collective-permute-done.5.refs_1_), channel_id=1, source_target_pairs={{0,1},{1,2},{2,3},{3,0},{4,5},{5,6},{6,7},{7,4},{8,9},{9,10},{10,1... | collective-permute-start | bytes 737288 | tf_op jit(solution)/shard_map/ppermute | solution.py:578
  30.5 14.7 %collective-permute-start.9 = (bf16[4,48,640]{2,1,0:T(8,128)(2,1)S(1)}, bf16[4,48,640]{2,1,0:T(8,128)(2,1)S(1)}, u32[]{:S(2)}, u32[]{:S(2)}) collective-permute-start(bf16[4,48,640]{2,1,0:T(8,128)(2,1)S(1)} %collective-permute-done.5.refs_1_), channel_id=1, source_target_pairs={{0,16},{16,0},{1,17},{17,1},{2,18},{18,2},{3,19},{19,3},{4,20},{20... | collective-permute-start | bytes 737288 | tf_op jit(solution)/shard_map/ppermute | solution.py:573
  32.6 8.7 %collective-permute-start.12 = (bf16[4,10,256]{2,1,0:T(8,128)(2,1)S(1)}, bf16[4,10,256]{2,1,0:T(8,128)(2,1)S(1)}, u32[]{:S(2)}, u32[]{:S(2)}) collective-permute-start(bf16[4,10,256]{2,1,0:T(8,128)(2,1)S(1)} %slice.180), channel_id=1, source_target_pairs={{0,1},{1,2},{2,3},{3,0},{4,5},{5,6},{6,7},{7,4},{8,9},{9,10},{10,1... | collective-permute-start | bytes 61448 | tf_op jit(solution)/shard_map/ppermute | solution.py:607
  34.3 5.1 %collective-permute-start.11 = (bf16[4,4,256]{2,1,0:T(4,128)(2,1)S(1)}, bf16[4,4,256]{2,1,0:T(4,128)(2,1)S(1)}, u32[]{:S(2)}, u32[]{:S(2)}) collective-permute-start(bf16[4,4,256]{2,1,0:T(4,128)(2,1)S(1)} %get-tuple-element.283), channel_id=1, source_target_pairs={{0,16},{16,0},{1,17},{17,1},{2,18},{18,2},{3,19},{19,3},{4,20},{20... | collective-permute-start | bytes 24584 | tf_op jit(solution)/shard_map/ppermute | solution.py:573
  39.4 5.0 %collective-permute-start.13 = (bf16[4,10,256]{2,1,0:T(8,128)(2,1)S(1)}, bf16[4,10,256]{2,1,0:T(8,128)(2,1)S(1)}, u32[]{:S(2)}, u32[]{:S(2)}) collective-permute-start(bf16[4,10,256]{2,1,0:T(8,128)(2,1)S(1)} %slice.180), channel_id=1, source_target_pairs={{0,2},{1,3},{2,0},{3,1},{4,6},{5,7},{6,4},{7,5},{8,10},{9,11},{10,... | collective-permute-start | bytes 61448 | tf_op jit(solution)/shard_map/ppermute | solution.py:607
  41.3 3.9 collective-permute-start.14
  44.4 22.5 %collective-permute-start.18 = (bf16[256,1536]{1,0:T(8,128)(2,1)S(1)}, bf16[256,1536]{1,0:T(8,128)(2,1)}, u32[]{:S(2)}, u32[]{:S(2)}) collective-permute-start(bf16[256,1536]{1,0:T(8,128)(2,1)S(1)} %bitcast.177), channel_id=1, source_target_pairs={{0,4},{4,0},{8,12},{12,8},{1,5},{5,1},{9,13},{13,9},{2,6},{6,2},{1... | collective-permute-start | bytes 2359304 | tf_op jit(solution)/shard_map/ppermute | solution.py:573
  45.2 21.7 %collective-permute-start.19 = (bf16[256,1536]{1,0:T(8,128)(2,1)S(1)}, bf16[256,1536]{1,0:T(8,128)(2,1)}, u32[]{:S(2)}, u32[]{:S(2)}) collective-permute-start(bf16[256,1536]{1,0:T(8,128)(2,1)S(1)} %collective-permute-done.10.refs_2_), channel_id=1, source_target_pairs={{0,4},{4,0},{8,12},{12,8},{1,5},{5,1},{9,13},{13,9},{2,6},{6,2},{1... | collective-permute-start | bytes 2359304 | tf_op jit(solution)/shard_map/ppermute | solution.py:573
  50.8 30.6 %collective-permute-start.20 = (bf16[2,256,768]{2,1,0:T(8,128)(2,1)}, bf16[2,256,768]{2,1,0:T(8,128)(2,1)}, u32[]{:S(2)}, u32[]{:S(2)}) collective-permute-start(bf16[2,256,768]{2,1,0:T(8,128)(2,1)} %pad_maximum_fusion.1.refs_8_), channel_id=1, source_target_pairs={{0,8},{4,20},{8,0},{12,28},{16,24},{20,4},{24,16},{28,12},{1,9},{5... | collective-permute-start | bytes 2359304 | tf_op jit(solution)/shard_map/ppermute | solution.py:651
  52.8 10.7 %collective-permute-start.15 = (bf16[4,48,640]{2,1,0:T(8,128)(2,1)}, bf16[4,48,640]{2,1,0:T(8,128)(2,1)S(1)}, u32[]{:S(2)}, u32[]{:S(2)}) collective-permute-start(bf16[4,48,640]{2,1,0:T(8,128)(2,1)} %collective-permute-done.8.refs_2_), channel_id=1, source_target_pairs={{0,1},{1,2},{2,3},{3,0},{4,5},{5,6},{6,7},{7,4},{8,9},{9,10},{10,1... | collective-permute-start | bytes 737288 | tf_op jit(solution)/shard_map/ppermute | solution.py:578
  53.8 10.3 %collective-permute-start.16 = (bf16[4,48,640]{2,1,0:T(8,128)(2,1)}, bf16[4,48,640]{2,1,0:T(8,128)(2,1)}, u32[]{:S(2)}, u32[]{:S(2)}) collective-permute-start(bf16[4,48,640]{2,1,0:T(8,128)(2,1)} %collective-permute-done.8.refs_2_), channel_id=1, source_target_pairs={{0,16},{16,0},{1,17},{17,1},{2,18},{18,2},{3,19},{19,3},{4,20},{20... | collective-permute-start | bytes 737288 | tf_op jit(solution)/shard_map/ppermute | solution.py:573
  63.6 43.7 %collective-permute-start.21 = (bf16[2,256,768]{2,1,0:T(8,128)(2,1)}, bf16[2,256,768]{2,1,0:T(8,128)(2,1)}, u32[]{:S(2)}, u32[]{:S(2)}) collective-permute-start(bf16[2,256,768]{2,1,0:T(8,128)(2,1)} %pad_maximum_fusion.1.refs_8_), channel_id=1, source_target_pairs={{0,16},{4,12},{8,24},{12,4},{16,0},{20,28},{24,8},{28,20},{1,17},{... | collective-permute-start | bytes 2359304 | tf_op jit(solution)/shard_map/ppermute | solution.py:651
  64.1 17.3 %collective-permute-start.17 = (bf16[4,48,640]{2,1,0:T(8,128)(2,1)S(1)}, bf16[4,48,640]{2,1,0:T(8,128)(2,1)S(1)}, u32[]{:S(2)}, u32[]{:S(2)}) collective-permute-start(bf16[4,48,640]{2,1,0:T(8,128)(2,1)S(1)} %collective-permute-done.15.refs_3_), channel_id=1, source_target_pairs={{0,16},{16,0},{1,17},{17,1},{2,18},{18,2},{3,19},{19,3},{4,20},{20... | collective-permute-start | bytes 737288 | tf_op jit(solution)/shard_map/ppermute | solution.py:573
  66.7 212.1 %reduce-scatter.7.cloned.1.call-start = ((), (), s32[]{:S(2)}) async-start(), calls=%async_computation.7 | async-start | bytes 1966080 | tf_op jit(solution)/shard_map/reduce_scatter | solution.py:950
  81.5 25.9 %collective-permute-start.22 = (bf16[2,256,768]{2,1,0:T(8,128)(2,1)}, bf16[2,256,768]{2,1,0:T(8,128)(2,1)}, u32[]{:S(2)}, u32[]{:S(2)}) collective-permute-start(bf16[2,256,768]{2,1,0:T(8,128)(2,1)} %collective-permute-done.20.refs_9_), channel_id=1, source_target_pairs={{0,16},{4,12},{8,24},{12,4},{16,0},{20,28},{24,8},{28,20},{1,17},{... | collective-permute-start | bytes 2359304 | tf_op jit(solution)/shard_map/ppermute | solution.py:651
  112.1 2.7 collective-permute-start.23
  113.3 20.3 %collective-permute-start.25 = (bf16[256,1536]{1,0:T(8,128)(2,1)}, bf16[256,1536]{1,0:T(8,128)(2,1)}, u32[]{:S(2)}, u32[]{:S(2)}) collective-permute-start(bf16[256,1536]{1,0:T(8,128)(2,1)} %add_convert_fusion.4), channel_id=1, source_target_pairs={{0,8},{4,12},{8,0},{12,4},{1,9},{5,13},{9,1},{13,5},{2,10},{6,14},... | collective-permute-start | bytes 2359304 | tf_op jit(solution)/shard_map/ppermute | solution.py:573
  114.1 21.1 %collective-permute-start.26 = (bf16[2,256,768]{2,1,0:T(8,128)(2,1)}, bf16[2,256,768]{2,1,0:T(8,128)(2,1)}, u32[]{:S(2)}, u32[]{:S(2)}) collective-permute-start(bf16[2,256,768]{2,1,0:T(8,128)(2,1)} %pad_maximum_fusion.1.refs_8_), channel_id=1, source_target_pairs={{0,4},{4,0},{8,12},{12,8},{1,5},{5,1},{9,13},{13,9},{2,6},{6,2},{1... | collective-permute-start | bytes 2359304 | tf_op jit(solution)/shard_map/ppermute | solution.py:573
  114.3 20.9 %collective-permute-start.27 = (bf16[2,256,768]{2,1,0:T(8,128)(2,1)}, bf16[2,256,768]{2,1,0:T(8,128)(2,1)}, u32[]{:S(2)}, u32[]{:S(2)}) collective-permute-start(bf16[2,256,768]{2,1,0:T(8,128)(2,1)} %collective-permute-done.20.refs_9_), channel_id=1, source_target_pairs={{0,4},{4,0},{8,12},{12,8},{1,5},{5,1},{9,13},{13,9},{2,6},{6,2},{1... | collective-permute-start | bytes 2359304 | tf_op jit(solution)/shard_map/ppermute | solution.py:573
  114.6 20.6 %collective-permute-start.28 = (bf16[2,256,768]{2,1,0:T(8,128)(2,1)}, bf16[2,256,768]{2,1,0:T(8,128)(2,1)}, u32[]{:S(2)}, u32[]{:S(2)}) collective-permute-start(bf16[2,256,768]{2,1,0:T(8,128)(2,1)} %collective-permute-done.21.refs_10_), channel_id=1, source_target_pairs={{0,4},{4,0},{8,12},{12,8},{1,5},{5,1},{9,13},{13,9},{2,6},{6,2},{1... | collective-permute-start | bytes 2359304 | tf_op jit(solution)/shard_map/ppermute | solution.py:573
  115.7 19.6 %collective-permute-start.29 = (bf16[2,256,768]{2,1,0:T(8,128)(2,1)}, bf16[2,256,768]{2,1,0:T(8,128)(2,1)}, u32[]{:S(2)}, u32[]{:S(2)}) collective-permute-start(bf16[2,256,768]{2,1,0:T(8,128)(2,1)} %collective-permute-done.22.refs_11_), channel_id=1, source_target_pairs={{0,4},{4,0},{8,12},{12,8},{1,5},{5,1},{9,13},{13,9},{2,6},{6,2},{1... | collective-permute-start | bytes 2359304 | tf_op jit(solution)/shard_map/ppermute | solution.py:573
  137.7 20.0 %collective-permute-start.31 = (bf16[2,256,768]{2,1,0:T(8,128)(2,1)S(1)}, bf16[2,256,768]{2,1,0:T(8,128)(2,1)S(1)}, u32[]{:S(2)}, u32[]{:S(2)}) collective-permute-start(bf16[2,256,768]{2,1,0:T(8,128)(2,1)S(1)} %pad_maximum_fusion.2.refs_0_), channel_id=1, source_target_pairs={{0,8},{4,20},{8,0},{12,28},{16,24},{20,4},{24,16},{28,12},{1,9},{5... | collective-permute-start | bytes 2359304 | tf_op jit(solution)/shard_map/ppermute | solution.py:651
  138.6 20.6 %collective-permute-start.32 = (bf16[2,256,768]{2,1,0:T(8,128)(2,1)S(1)}, bf16[2,256,768]{2,1,0:T(8,128)(2,1)}, u32[]{:S(2)}, u32[]{:S(2)}) collective-permute-start(bf16[2,256,768]{2,1,0:T(8,128)(2,1)S(1)} %pad_maximum_fusion.2.refs_0_), channel_id=1, source_target_pairs={{0,16},{4,12},{8,24},{12,4},{16,0},{20,28},{24,8},{28,20},{1,17},{... | collective-permute-start | bytes 2359304 | tf_op jit(solution)/shard_map/ppermute | solution.py:651
  157.7 12.1 %collective-permute-start.33 = (bf16[2,256,768]{2,1,0:T(8,128)(2,1)S(1)}, bf16[2,256,768]{2,1,0:T(8,128)(2,1)}, u32[]{:S(2)}, u32[]{:S(2)}) collective-permute-start(bf16[2,256,768]{2,1,0:T(8,128)(2,1)S(1)} %collective-permute-done.31.refs_1_), channel_id=1, source_target_pairs={{0,16},{4,12},{8,24},{12,4},{16,0},{20,28},{24,8},{28,20},{1,17},{... | collective-permute-start | bytes 2359304 | tf_op jit(solution)/shard_map/ppermute | solution.py:651
  158.6 11.9 %collective-permute-start.34 = (bf16[2,256,768]{2,1,0:T(8,128)(2,1)S(1)}, bf16[2,256,768]{2,1,0:T(8,128)(2,1)}, u32[]{:S(2)}, u32[]{:S(2)}) collective-permute-start(bf16[2,256,768]{2,1,0:T(8,128)(2,1)S(1)} %pad_maximum_fusion.2.refs_0_), channel_id=1, source_target_pairs={{0,4},{4,0},{8,12},{12,8},{1,5},{5,1},{9,13},{13,9},{2,6},{6,2},{1... | collective-permute-start | bytes 2359304 | tf_op jit(solution)/shard_map/ppermute | solution.py:573
  158.6 11.9 %collective-permute-start.35 = (bf16[2,256,768]{2,1,0:T(8,128)(2,1)S(1)}, bf16[2,256,768]{2,1,0:T(8,128)(2,1)}, u32[]{:S(2)}, u32[]{:S(2)}) collective-permute-start(bf16[2,256,768]{2,1,0:T(8,128)(2,1)S(1)} %collective-permute-done.31.refs_1_), channel_id=1, source_target_pairs={{0,4},{4,0},{8,12},{12,8},{1,5},{5,1},{9,13},{13,9},{2,6},{6,2},{1... | collective-permute-start | bytes 2359304 | tf_op jit(solution)/shard_map/ppermute | solution.py:573
  159.1 11.4 %collective-permute-start.36 = (bf16[2,256,768]{2,1,0:T(8,128)(2,1)}, bf16[2,256,768]{2,1,0:T(8,128)(2,1)}, u32[]{:S(2)}, u32[]{:S(2)}) collective-permute-start(bf16[2,256,768]{2,1,0:T(8,128)(2,1)} %collective-permute-done.32.refs_2_), channel_id=1, source_target_pairs={{0,4},{4,0},{8,12},{12,8},{1,5},{5,1},{9,13},{13,9},{2,6},{6,2},{1... | collective-permute-start | bytes 2359304 | tf_op jit(solution)/shard_map/ppermute | solution.py:573
  169.8 2.6 collective-permute-start.37
  203.3 9.0 %collective-permute-start.39 = (bf16[4,2,256,768]{3,2,1,0:T(8,128)(2,1)}, bf16[4,2,256,768]{3,2,1,0:T(8,128)(2,1)S(1)}, u32[]{:S(2)}, u32[]{:S(2)}) collective-permute-start(bf16[4,2,256,768]{3,2,1,0:T(8,128)(2,1)} %get-tuple-element.159), channel_id=1, source_target_pairs={{0,4},{4,0},{8,12},{12,8},{1,5},{5,1},{9,13},{13,9},{2,6},{6,2},{1... | collective-permute-start | bytes 9437192 | tf_op jit(solution)/shard_map/ppermute | solution.py:573
  203.5 25.6 %collective-permute-start.38 = (bf16[4,2,256,768]{3,2,1,0:T(8,128)(2,1)}, bf16[4,2,256,768]{3,2,1,0:T(8,128)(2,1)}, u32[]{:S(2)}, u32[]{:S(2)}) collective-permute-start(bf16[4,2,256,768]{3,2,1,0:T(8,128)(2,1)} %get-tuple-element.157), channel_id=1, source_target_pairs={{0,4},{4,0},{8,12},{12,8},{1,5},{5,1},{9,13},{13,9},{2,6},{6,2},{1... | collective-permute-start | bytes 9437192 | tf_op jit(solution)/shard_map/ppermute | solution.py:573
  215.3 20.6 %collective-permute-start.40 = (bf16[2,2,256,768]{3,2,1,0:T(8,128)(2,1)S(1)}, bf16[2,2,256,768]{3,2,1,0:T(8,128)(2,1)}, u32[]{:S(2)}, u32[]{:S(2)}) collective-permute-start(bf16[2,2,256,768]{3,2,1,0:T(8,128)(2,1)S(1)} %add_convert_fusion.1), channel_id=1, source_target_pairs={{0,16},{4,12},{8,24},{12,4},{16,0},{20,28},{24,8},{28,20},{1,17},{... | collective-permute-start | bytes 4718600 | tf_op jit(solution)/shard_map/ppermute | solution.py:651
  219.7 113.5 %reduce-scatter.9.cloned.1.call-start = ((), (), s32[]{:S(2)}) async-start(), calls=%async_computation.8 | async-start | bytes 1966080 | tf_op jit(solution)/shard_map/reduce_scatter | solution.py:950
  238.9 12.1 %collective-permute-start.41 = (bf16[2,256,768]{2,1,0:T(8,128)(2,1)S(1)}, bf16[2,256,768]{2,1,0:T(8,128)(2,1)S(1)}, u32[]{:S(2)}, u32[]{:S(2)}) collective-permute-start(bf16[2,256,768]{2,1,0:T(8,128)(2,1)S(1)} %fusion.22), channel_id=1, source_target_pairs={{0,8},{4,20},{8,0},{12,28},{16,24},{20,4},{24,16},{28,12},{1,9},{5... | collective-permute-start | bytes 2359304 | tf_op jit(solution)/shard_map/ppermute | solution.py:651
  251.3 83.9 %reduce-scatter.5.cloned.1.call-start = ((), (), s32[]{:S(2)}) async-start(), calls=%async_computation.6 | async-start | bytes 1966080 | tf_op jit(solution)/shard_map/reduce_scatter | solution.py:950
  257.1 19.7 %collective-permute-start.43 = (bf16[256,1536]{1,0:T(8,128)(2,1)S(1)}, bf16[256,1536]{1,0:T(8,128)(2,1)}, u32[]{:S(2)}, u32[]{:S(2)}) collective-permute-start(bf16[256,1536]{1,0:T(8,128)(2,1)S(1)} %get-tuple-element.248.refs_0_), channel_id=1, source_target_pairs={{0,8},{4,12},{8,0},{12,4},{1,9},{5,13},{9,1},{13,5},{2,10},{6,14},... | collective-permute-start | bytes 2359304 | tf_op jit(solution)/shard_map/ppermute | solution.py:573
  257.9 18.9 %collective-permute-start.44 = (bf16[256,1536]{1,0:T(8,128)(2,1)S(1)}, bf16[256,1536]{1,0:T(8,128)(2,1)S(1)}, u32[]{:S(2)}, u32[]{:S(2)}) collective-permute-start(bf16[256,1536]{1,0:T(8,128)(2,1)S(1)} %get-tuple-element.248.refs_0_), channel_id=1, source_target_pairs={{0,4},{4,0},{8,12},{12,8},{1,5},{5,1},{9,13},{13,9},{2,6},{6,2},{1... | collective-permute-start | bytes 2359304 | tf_op jit(solution)/shard_map/ppermute | solution.py:573
  277.7 3.1 collective-permute-start.45
  278.7 88.5 %reduce-scatter.11.cloned.1.call-start = ((), (), s32[]{:S(2)}) async-start(), calls=%async_computation.9 | async-start | bytes 1474560 | tf_op jit(solution)/shard_map/reduce_scatter | solution.py:1002
  325.3 3.2 collective-permute-start.49
  325.4 31.3 %collective-permute-start.50 = (bf16[2,2,256,768]{3,2,1,0:T(8,128)(2,1)}, bf16[2,2,256,768]{3,2,1,0:T(8,128)(2,1)}, u32[]{:S(2)}, u32[]{:S(2)}) collective-permute-start(bf16[2,2,256,768]{3,2,1,0:T(8,128)(2,1)} %add_convert_fusion), channel_id=1, source_target_pairs={{0,16},{4,12},{8,24},{12,4},{16,0},{20,28},{24,8},{28,20},{1,17},{... | collective-permute-start | bytes 4718600 | tf_op jit(solution)/shard_map/ppermute | solution.py:651
  326.3 41.0 %collective-permute-start.46 = (bf16[16,48,640]{2,1,0:T(8,128)(2,1)}, bf16[16,48,640]{2,1,0:T(8,128)(2,1)}, u32[]{:S(2)}, u32[]{:S(2)}) collective-permute-start(bf16[16,48,640]{2,1,0:T(8,128)(2,1)} %get-tuple-element.259), channel_id=1, source_target_pairs={{0,16},{16,0},{1,17},{17,1},{2,18},{18,2},{3,19},{19,3},{4,20},{20... | collective-permute-start | bytes 2949128 | tf_op jit(solution)/shard_map/ppermute | solution.py:573
  331.6 35.6 %collective-permute-start.48 = (bf16[256,1536]{1,0:T(8,128)(2,1)}, bf16[256,1536]{1,0:T(8,128)(2,1)}, u32[]{:S(2)}, u32[]{:S(2)}) collective-permute-start(bf16[256,1536]{1,0:T(8,128)(2,1)} %get-tuple-element.253), channel_id=1, source_target_pairs={{0,8},{4,12},{8,0},{12,4},{1,9},{5,13},{9,1},{13,5},{2,10},{6,14},... | collective-permute-start | bytes 2359304 | tf_op jit(solution)/shard_map/ppermute | solution.py:573
  369.1 11.4 %collective-permute-start.55 = (f32[10,1536]{1,0:T(8,128)S(1)}, f32[10,1536]{1,0:T(8,128)S(1)}, u32[]{:S(2)}, u32[]{:S(2)}) collective-permute-start(f32[10,1536]{1,0:T(8,128)S(1)} %pad_maximum_fusion.7), channel_id=1, source_target_pairs={{0,16},{16,0},{1,17},{17,1},{2,18},{18,2},{3,19},{19,3},{4,20},{20... | collective-permute-start | bytes 184328 | tf_op jit(solution)/shard_map/ppermute | solution.py:573
  370.1 8.6 %collective-permute-start.51 = (bf16[4,48,640]{2,1,0:T(8,128)(2,1)S(1)}, bf16[4,48,640]{2,1,0:T(8,128)(2,1)S(1)}, u32[]{:S(2)}, u32[]{:S(2)}) collective-permute-start(bf16[4,48,640]{2,1,0:T(8,128)(2,1)S(1)} %dynamic-slice_bitcast_fusion.2), channel_id=1, source_target_pairs={{0,1},{1,2},{2,3},{3,0},{4,5},{5,6},{6,7},{7,4},{8,9},{9,10},{10,1... | collective-permute-start | bytes 737288 | tf_op jit(solution)/shard_map/ppermute | solution.py:578
  379.5 8.3 %collective-permute-start.52 = (bf16[4,48,640]{2,1,0:T(8,128)(2,1)}, bf16[4,48,640]{2,1,0:T(8,128)(2,1)}, u32[]{:S(2)}, u32[]{:S(2)}) collective-permute-start(bf16[4,48,640]{2,1,0:T(8,128)(2,1)} %fusion.28), channel_id=1, source_target_pairs={{0,1},{1,2},{2,3},{3,0},{4,5},{5,6},{6,7},{7,4},{8,9},{9,10},{10,1... | collective-permute-start | bytes 737288 | tf_op jit(solution)/shard_map/ppermute | solution.py:578
  379.5 21.0 %collective-permute-start.54 = (bf16[2,256,768]{2,1,0:T(8,128)(2,1)}, bf16[2,256,768]{2,1,0:T(8,128)(2,1)}, u32[]{:S(2)}, u32[]{:S(2)}) collective-permute-start(bf16[2,256,768]{2,1,0:T(8,128)(2,1)} %fusion.23), channel_id=1, source_target_pairs={{0,8},{4,20},{8,0},{12,28},{16,24},{20,4},{24,16},{28,12},{1,9},{5... | collective-permute-start | bytes 2359304 | tf_op jit(solution)/shard_map/ppermute | solution.py:651
  381.5 15.2 %all-to-all-start = ((f32[16,1,960]{2,1,0:T(1,128)}), f32[16,1,960]{2,1,0:T(1,128)S(1)}, u32[]{:S(2)}, u32[]{:S(2)}) async-start(f32[16,1,960]{2,1,0:T(1,128)} %reshape.328), calls=%async_computation.4 | async-start | bytes 131072 | tf_op jit(solution)/shard_map/all_to_all | solution.py:1018
  389.6 9.9 %collective-permute-start.53 = (bf16[4,48,640]{2,1,0:T(8,128)(2,1)}, bf16[4,48,640]{2,1,0:T(8,128)(2,1)S(1)}, u32[]{:S(2)}, u32[]{:S(2)}) collective-permute-start(bf16[4,48,640]{2,1,0:T(8,128)(2,1)} %fusion.27), channel_id=1, source_target_pairs={{0,1},{1,2},{2,3},{3,0},{4,5},{5,6},{6,7},{7,4},{8,9},{9,10},{10,1... | collective-permute-start | bytes 737288 | tf_op jit(solution)/shard_map/ppermute | solution.py:578
  400.5 8.2 %collective-permute-start.61 = (bf16[96,1536]{1,0:T(8,128)(2,1)}, bf16[96,1536]{1,0:T(8,128)(2,1)S(1)}, u32[]{:S(2)}, u32[]{:S(2)}) collective-permute-start(bf16[96,1536]{1,0:T(8,128)(2,1)} %reduce-scatter.11.cloned.1.call-done), channel_id=1, source_target_pairs={{0,16},{16,0},{1,17},{17,1},{2,18},{18,2},{3,19},{19,3},{4,20},{20... | collective-permute-start | bytes 884744 | tf_op jit(solution)/shard_map/ppermute | solution.py:573
  401.9 6.0 %collective-permute-start.57 = (bf16[48,640]{1,0:T(8,128)(2,1)S(1)}, bf16[48,640]{1,0:T(8,128)(2,1)S(1)}, u32[]{:S(2)}, u32[]{:S(2)}) collective-permute-start(bf16[48,640]{1,0:T(8,128)(2,1)S(1)} %get-tuple-element.273), channel_id=1, source_target_pairs={{0,4},{4,0},{8,12},{12,8},{1,5},{5,1},{9,13},{13,9},{2,6},{6,2},{1... | collective-permute-start | bytes 184328 | tf_op jit(solution)/shard_map/ppermute | solution.py:573
  402.0 5.9 %collective-permute-start.58 = (bf16[48,640]{1,0:T(8,128)(2,1)S(1)}, bf16[48,640]{1,0:T(8,128)(2,1)S(1)}, u32[]{:S(2)}, u32[]{:S(2)}) collective-permute-start(bf16[48,640]{1,0:T(8,128)(2,1)S(1)} %get-tuple-element.272), channel_id=1, source_target_pairs={{0,8},{4,12},{8,0},{12,4},{1,9},{5,13},{9,1},{13,5},{2,10},{6,14},... | collective-permute-start | bytes 184328 | tf_op jit(solution)/shard_map/ppermute | solution.py:573
  403.7 4.1 collective-permute-start.59
  407.5 10.8 %collective-permute-start.56 = (bf16[256,768]{1,0:T(8,128)(2,1)}, bf16[256,768]{1,0:T(8,128)(2,1)}, u32[]{:S(2)}, u32[]{:S(2)}) collective-permute-start(bf16[256,768]{1,0:T(8,128)(2,1)} %fusion.30), channel_id=1, source_target_pairs={{0,4},{4,0},{8,12},{12,8},{1,5},{5,1},{9,13},{13,9},{2,6},{6,2},{1... | collective-permute-start | bytes 1179656 | tf_op jit(solution)/shard_map/ppermute | solution.py:573
  407.9 8.3 %collective-permute-start.60 = (bf16[4,48,640]{2,1,0:T(8,128)(2,1)S(1)}, bf16[4,48,640]{2,1,0:T(8,128)(2,1)}, u32[]{:S(2)}, u32[]{:S(2)}) collective-permute-start(bf16[4,48,640]{2,1,0:T(8,128)(2,1)S(1)} %pad_maximum_fusion.5.near_ref), channel_id=1, source_target_pairs={{0,16},{16,0},{1,17},{17,1},{2,18},{18,2},{3,19},{19,3},{4,20},{20... | collective-permute-start | bytes 737288 | tf_op jit(solution)/shard_map/ppermute | solution.py:573
  (55 other events, 494.3 us)
Sparse Core Ops, SparseCore 0:
  66.8 35.3 all-gather.1
  219.8 34.5 reduce-scatter.6
  256.7 34.2 reduce-scatter.8
  293.2 34.2 reduce-scatter.4
  329.6 28.1 reduce-scatter.10

commit v3 on v2

--- a/solution.py
+++ b/solution.py
@@ -88,7 +88,7 @@
             pltpu.SemaphoreType.DMA((n_ctx,)),
         ],
         compiler_params=params(),
-        cost_estimate=cost(3e9, 6e6),
+        cost_estimate=cost(7e9, 6e6),
         name="norm_rows",
     )(*x_pieces, gain)
 
@@ -608,12 +608,14 @@
     ]
 
 
-def ring_sum(chunk, axis):
+def ring_sum(chunk, axis, deps=()):
     n, d = lax.axis_size(axis), lax.axis_index(axis)
     part = chunk(lax.rem(d + n - 1, n)).astype(bf16)
     for hop in range(n - 1):
         got = step_up(part, axis)
         own = chunk(lax.rem(d + 2 * n - 2 - hop, n))
+        if hop < len(deps):
+            own = after(own, *deps[hop])
         part = (got.astype(f32) + own.astype(f32)).astype(bf16)
     return part
 
@@ -768,6 +770,88 @@
         cost_estimate=cost(0, 2e6),
         name="columns_of",
     )(spots, near, far)
+
+
+def position_tables(lengths_row, row, freq):
+    total = row.shape[1]
+    half = HEAD_SIZE // 2
+
+    def kernel(len_ref, row_ref, freq_ref, *outs):
+        cos_d, sin_d, cos_s, sin_s, cos_t, sin_t, start_ref = outs
+
+        def start_of(place):
+            end, start = 0, jnp.zeros_like(place)
+            for j in range(lengths_row.shape[0]):
+                end = end + len_ref[j]
+                start = start + jnp.where(place >= end, len_ref[j], 0)
+            return start
+
+        dealt = row_ref[...]
+        placed = lax.broadcasted_iota(jnp.int32, (1, total), 1)
+        start_ref[...] = start_of(placed)
+        for place, cos_ref, sin_ref in ((dealt, cos_d, sin_d), (placed, cos_s, sin_s)):
+            angle = freq_ref[...] * (place - start_of(place)).astype(f32)
+            cos, sin = jnp.cos(angle), jnp.sin(angle)
+            cos_ref[...] = jnp.concatenate([cos] * 4, axis=0).T
+            sin_ref[...] = jnp.concatenate([-sin, sin] * 2, axis=0).T
+        cos_t[...] = cos
+        sin_t[...] = sin
+
+    shape = jax.ShapeDtypeStruct
+    wide, thin = shape((total, LANES), f32), shape((half, total), f32)
+    return pl.pallas_call(
+        kernel,
+        out_shape=(wide, wide, wide, wide, thin, thin, shape((1, total), jnp.int32)),
+        in_specs=[SMEM, VMEM, VMEM],
+        out_specs=(VMEM,) * 7,
+        compiler_params=params(),
+        cost_estimate=cost(0, 0),
+        name="position_tables",
+    )(lengths_row, row, freq)
+
+
+def widen(gate, up, down):
+    def kernel(a_ref, b_ref, c_ref, a_out, b_out, c_out):
+        a_out[...] = a_ref[...].astype(f32)
+        b_out[...] = b_ref[...].astype(f32)
+        c_out[...] = c_ref[...].astype(f32).T
+
+    shape = jax.ShapeDtypeStruct
+    return pl.pallas_call(
+        kernel,
+        out_shape=(shape(gate.shape, f32), shape(up.shape, f32), shape(down.shape[::-1], f32)),
+        in_specs=[VMEM] * 3,
+        out_specs=(VMEM,) * 3,
+        compiler_params=params(),
+        cost_estimate=cost(0, 0),
+        name="widen",
+    )(gate, up, down)
+
+
+def finish_input(d_middle, near, far, x, gain):
+    tok = x.shape[0]
+
+    def kernel(dm_ref, near_ref, far_ref, x_ref, gain_ref, out_ref):
+        v = x_ref[...].astype(f32)
+        dh = near_ref[...] + far_ref[...].astype(f32)
+        r = lax.rsqrt(jnp.mean(v * v, axis=-1, keepdims=True) + NORM_EPS)
+        scaled = gain_ref[...] * dh
+        inner = jnp.sum(scaled * v, axis=-1, keepdims=True)
+        dv = r * scaled - v * (r * r * r) * (inner / MODEL_WIDTH)
+        out_ref[...] = (dm_ref[...] + dv).astype(bf16)
+
+    step = 64
+    rows = pl.BlockSpec((step, MODEL_WIDTH), lambda i: (i, 0))
+    return pl.pallas_call(
+        kernel,
+        out_shape=jax.ShapeDtypeStruct((tok, MODEL_WIDTH), bf16),
+        grid=(tok // step,),
+        in_specs=[rows] * 4 + [pl.BlockSpec((1, MODEL_WIDTH), lambda i: (0, 0))],
+        out_specs=rows,
+        compiler_params=params(),
+        cost_estimate=cost(0, 0),
+        name="finish_input",
+    )(d_middle, near, far, x, gain)
 
 
 def rms_back(dh, v, r, gain):
@@ -804,7 +888,7 @@
     params_t = jnp.concatenate([attn_gain[None], ffn_gain[None], w_router.T], axis=0)
     p_rows = params_t.shape[0]
     params_t = jnp.pad(params_t, ((0, 0), (0, tok - rows)))
-    note = jnp.concatenate([routes[0].T.astype(bf16), params_t], axis=0)
+    routes_t = routes[0].T.astype(bf16)
     k_of = jnp.arange(n_dp, dtype=jnp.int32)
     d_of = lax.rem(dx - k_of + n_dp, n_dp)
     c_of = cx ^ jnp.arange(n_ctx, dtype=jnp.int32)
@@ -822,25 +906,10 @@
 
     def positions(order_row, lengths_row):
         order_rel = order_row.reshape(n_ctx, tok)[c_of].reshape(-1)
-        both = jnp.concatenate([order_rel, jnp.arange(total, dtype=jnp.int32)])
-        end = jnp.zeros((), jnp.int32)
-        start = jnp.zeros_like(both)
-        for j in range(lengths_row.shape[0]):
-            end = end + lengths_row[j]
-            start = start + jnp.where(both >= end, lengths_row[j], 0)
-        lane = jnp.arange(LANES, dtype=jnp.int32) % HEAD_SIZE
         half = HEAD_SIZE // 2
-        freq = ROPE_BASE ** (-((lane % half).astype(f32) * 2.0 / HEAD_SIZE))
-
-        def tables(places):
-            angle = places.astype(f32)[:, None] * freq[None, :]
-            return jnp.cos(angle), jnp.where(lane < half, -1.0, 1.0)[None] * jnp.sin(angle)
-
-        places_s = (both - start)[total:]
-        turned = freq[:half, None] * places_s.astype(f32)[None, :]
-        placed = (*tables(places_s), jnp.cos(turned), jnp.sin(turned))
-        dealt = tables((both - start)[:total])
-        return (order_rel[None, :], order_rel[:, None], start[None, total:], *dealt, *placed)
+        freq = ROPE_BASE ** (-(jnp.arange(half, dtype=f32) * 2.0 / HEAD_SIZE))
+        row, col = order_rel[None, :], order_rel[:, None]
+        return (row, col, *position_tables(lengths_row, row, freq[:, None]))
 
     order_row, ends_in = token_order[0], lengths[0]
 
@@ -858,28 +927,30 @@
             return lax.dynamic_slice_in_dim(for_context(c), ex * part, part, 0)
 
         got = [half_for(cx)] + [flip(half_for(cx ^ m), "context", m) for m in range(1, n_ctx)]
-        note2 = jnp.stack([note, flip(note, "context", 2)])
-        x2 = flip(x_own, "context", 2)
+        shards = send_all(params_t, "dp")
         dy0 = plane_near(dy_own)
-        w0, note2, dy0 = sync(jnp.stack(got), note2, dy0)
+        w0, dy0, *shards = sync(jnp.stack(got), dy0, *shards)
+        note = jnp.concatenate([routes_t] + shards, axis=0)
         mine, theirs = [w0], []
         for k in range(n_dp - 1):
             nxt, other = step_up(mine[-1], "dp"), flip(mine[-1], "expert", 1)
             if k == 0:
+                note2 = jnp.stack([note, flip(note, "context", 2)])
+                x2 = flip(after(x_own, note2), "context", 2)
+                nxt, other, note2, order_row, ends_in = sync(nxt, other, note2, order_row, ends_in)
+            elif k == 1:
+                dy1 = hop_plane(after(dy0, mine[-1]), False)
                 near = flip(note2, "context", 1)
                 note4 = jnp.stack([note2[0], near[0], note2[1], near[1]])
-                nxt, other, note4, order_row, ends_in = sync(nxt, other, note4, order_row, ends_in)
-            elif k == 1:
-                shards = send_all(note4[:, top:], "dp")
+                nxt, other, x2, note4 = sync(nxt, other, x2, note4)
+                x1, x3 = flip(x_own, "context", 1), flip(x2, "context", 1)
+                where = positions(order_row, ends_in)
+                shards = note4[:, top:].reshape(n_ctx, n_dp, p_rows, tok).swapaxes(0, 1)
+                gain_a, gain_b, router = own_params(shards)
+            elif k == 2:
                 routes_far = flip(note4[:, :top], "expert", 1)
-                nxt, other, x2, routes_far, *shards = sync(nxt, other, x2, routes_far, *shards)
-                x1, x3 = flip(x_own, "context", 1), flip(x2, "context", 1)
-                gain_a, gain_b, router = own_params(jnp.stack(shards))
-                where = positions(order_row, ends_in)
-            elif k == 2:
-                nxt, other, gain_a, *where = sync(nxt, other, gain_a, *where)
+                nxt, other, gain_a, dy1 = sync(nxt, other, gain_a, dy1)
                 h1 = norm_rows([x_own, x1, x2, x3], gain_a)
-                dy1 = hop_plane(after(dy0, x2), False)
             mine.append(nxt)
             theirs.append(other)
         theirs.append(flip(mine[-1], "expert", 1))
@@ -890,7 +961,7 @@
         routes_all = own_routes(routes_rel[jnp.where(c == 0, even, odd)])
         theirs[-1], router, h1, routes_all, dy1 = sync(theirs[-1], router, h1, routes_all, dy1)
         wo = gather_out(after(w_out, mine[-1]))
-        dy2, dy3 = plane_far(dy0, dy1)
+        dy2, dy3 = plane_far(after(dy0, theirs[-1]), dy1)
         w_pieces = mine + theirs
         spots = jnp.concatenate(
             [places, places, jnp.broadcast_to(ex, (n_dp,)), jnp.broadcast_to(1 - ex, (n_dp,))]
@@ -900,14 +971,14 @@
         for m in range(1, n_ctx):
             got.append(flip(for_context(cx ^ m), "context", m))
         w_pieces = ring(jnp.stack(got), "dp")
-        note4 = jnp.stack(ctx_gather(note))
-        gain_a, gain_b, router = own_params(jnp.stack(send_all(note4[:, top:], "dp")))
-        routes_all = own_routes(lax.all_gather(note[:top], PLANE, axis=0, tiled=False))
+        shards = jnp.stack(send_all(jnp.stack(ctx_gather(params_t)), "dp"))
+        gain_a, gain_b, router = own_params(shards)
+        routes_all = own_routes(lax.all_gather(routes_t, PLANE, axis=0, tiled=False))
         h1 = norm_rows(ctx_gather(x_own), gain_a)
         dy_all, wo = gather_plane(cotangent[0]), gather_out(w_out)
         spots = jnp.concatenate([places, jnp.zeros((n_dp,), jnp.int32)])
         where = positions(order_row, ends_in)
-    row, col, start_row, cos_d, sin_d, *placed = where
+    row, col, cos_d, sin_d, *placed, start_row = where
     near, far, q, k, v, lse, wqkv = attn_fwd(
         spots, w_pieces, n_dp, h1, row, col, start_row, cos_d, sin_d, qh, kvh
     )
@@ -937,8 +1008,11 @@
     d_rows, y_rows, (xs, deout, act, dgate, dup, coef) = (
         out[:n_rows], out[n_rows : 2 * n_rows], out[2 * n_rows :],
     )
-    d_sum, y_sum = PlaneSum(d_rows), PlaneSum(y_rows)
     small = small_plane()
+    d_sum = PlaneSum(d_rows)
+    if small:
+        y_rows = (y_rows[0], after(y_rows[1], d_sum.far))
+    y_sum = PlaneSum(y_rows)
     xs_late, deout_late = (after(xs, d_sum.far), after(deout, d_sum.far)) if small else (xs, deout)
     g_gate = dot(xs_late, dgate, TN).astype(bf16)
     g_up = dot(xs_late, dup, TN).astype(bf16)
@@ -947,7 +1021,7 @@
     g_router = g_router[:, :experts] + g_router[:, LANES // 2 : LANES // 2 + experts]
 
     def over_dp(g, dim):
-        return lax.psum_scatter(g, "dp", scatter_dimension=dim, tiled=True).astype(f32)
+        return lax.psum_scatter(g, "dp", scatter_dimension=dim, tiled=True)
 
     if small:
         d_sum.first()
@@ -971,15 +1045,14 @@
         y_sum.first()
     else:
         db_pieces = ctx_gather(d_middle.astype(bf16))
-    db_all = jnp.concatenate(db_pieces, axis=0)
-    attn = jnp.concatenate([near, far], axis=0).reshape(total, qw)
-    g_out = dot(attn, db_all, TN).astype(bf16)
-    db_last = after(db_pieces[-1], g_out, sum_gate)
+    db_last = after(db_pieces[-1], sum_gate)
 
     dqkv = attn_bwd(
         db_pieces[:-1] + [db_last], wo, near, far, q, k, v, lse, row, col, start_row, placed, qh, kvh
     )
     dqkv, sum_up = sync(dqkv, sum_up)
+    attn = jnp.concatenate([near, after(far, dqkv)], axis=0).reshape(total, qw)
+    g_out = dot(attn, jnp.concatenate(db_pieces, axis=0), TN).astype(bf16)
     dqkv_flat = dqkv.reshape(total, -1)
     h1_flat = h1.reshape(total, MODEL_WIDTH)
     g_qkv = dot(h1_flat, dqkv_flat, TN).astype(bf16)
@@ -1024,21 +1097,31 @@
         h1p = flip(dh1_part[1], "context", 1)
         dh1 = dh1_part[0].astype(f32) + h1p.astype(f32)
         y_sum.got2 = after(y_sum.got2, dqkv)
-        got, hop, dh1, y_sum.got2, sum_down, s_out, tiny = sync(
-            got, hop, dh1, y_sum.got2, sum_down, s_out, tiny
-        )
-        both_g = add_low(mine, got).reshape(n_ctx, n_dp, part, width)
-        s_qkv = ring_sum(lambda d: lax.dynamic_index_in_dim(both_g, d, 1, keepdims=False), "dp")
+        both_g = add_low(after(mine, dh1_part), got).reshape(n_ctx, n_dp, part, width)
+        sum_gate, sum_up, sum_down = widen(after(sum_gate, both_g), sum_up, sum_down)
+        grad_input = finish_input(d_middle, after(dh1, both_g), hop, hidden[0], gain_a)
         y_sum.got2 = after(y_sum.got2, both_g)
         y_sum.second()
-        tiny = after(tiny, both_g)
-        tiny = spread(tiny + flip(tiny, "expert", 1))
-        grad_input = finish_rows(after(dh1, both_g) + hop.astype(f32))
+        s_qkv = ring_sum(
+            lambda d: lax.dynamic_index_in_dim(both_g, d, 1, keepdims=False),
+            "dp",
+            [(), (hop,), (y_sum.got1,)],
+        )
+        tiny = after(tiny, both_g).reshape(-1, n_ctx * n_dp, rows).transpose(1, 0, 2)
+        tiny = (tiny + flip(tiny, "expert", 1)).reshape(2, 2, n_dp, -1, rows)
+        cy, cc = cx // 2, lax.rem(cx, 2)
+        give = lax.dynamic_index_in_dim(tiny, 1 - cy, 0, keepdims=False)
+        tiny = lax.dynamic_index_in_dim(tiny, cy, 0, keepdims=False) + flip(give, "context", 2)
+        give = lax.dynamic_index_in_dim(tiny, 1 - cc, 0, keepdims=False)
+        tiny = lax.dynamic_index_in_dim(tiny, cc, 0, keepdims=False) + flip(give, "context", 1)
         out_low = s_out.astype(bf16)
-        s_qkv, out_low, y_sum.got1, grad_input, tiny = sync(
-            s_qkv, out_low, y_sum.got1, grad_input, tiny
-        )
         out_far = flip(out_low, "expert", 1)
+        s_qkv, out_far, y_sum.got1, tiny = sync(s_qkv, out_far, y_sum.got1, tiny)
+        d_total = lax.dynamic_index_in_dim(tiny, dx, 0, keepdims=False)
+        for k in range(1, n_dp):
+            sent = lax.dynamic_index_in_dim(tiny, lax.rem(dx + k, n_dp), 0, keepdims=False)
+            d_total = d_total + lax.ppermute(sent, "dp", [(i, (i + k) % n_dp) for i in range(n_dp)])
+        tiny = d_total
         output = (middle + y_sum.finish()).astype(bf16)
         s_out = out_low.astype(f32) + out_far.astype(f32)
         near = exchange(s_qkv.astype(bf16))
@@ -1047,6 +1130,7 @@
         sum_q, sum_k, sum_v = columns_of(spots, near, far, qw, kw)
     else:
         dh1 = ctx_sum([dh1_part[m] for m in range(n_ctx)])
+        sum_gate, sum_up, sum_down = widen(sum_gate, sum_up, sum_down)
         grad_input = finish_rows(dh1)
         tiny = spread(lax.psum(tiny, "expert"))
         g4 = g_qkv.reshape(n_ctx, n_dp, rows, width)
@@ -1063,7 +1147,7 @@
 
     return (
         output[None], grad_input[None], tiny[0], sum_q, sum_k, sum_v, s_out,
-        tiny[1], tiny[2:].T, sum_gate[None], sum_up[None], sum_down.T[None],
+        tiny[1], tiny[2:].T, sum_gate[None], sum_up[None], sum_down[None],
     )
 
 

time: 432 us -> 400 us (0.926)
  other arithmetic: 60 us -> 37.9 us
  waiting for transfers between devices: 150 us -> 128 us
  Pallas kernels: 91.4 us -> 101 us
  starting transfers between devices: 50.5 us -> 58.6 us
    ppermute x10, waiting for transfers between devices: 60.3 us -> 38.3 us  [hop_plane(): return lax.ppermute(v, PLANE, pairs)]
    ppermute x43 -> x45, waiting for transfers between devices: 71.1 us -> 59.5 us  [flip(): return lax.ppermute(v, axis, [(i, i ^ bit) for i in range(n)])]
    ppermute x6, waiting for transfers between devices: 16.1 us -> 27.5 us  [step_up(): return lax.ppermute(v, axis, [(i, (i + 1) % n) for i in range(n)])]
    pallas_call x0 -> x3, Pallas kernels: none -> 10.2 us  [the longest x1 4.5 us: finish_input(): pl.pallas_call(kernel, out_shape=jax.ShapeDtypeStruct((tok, MODEL_WIDTH),...]
    convert_element_type x5 -> x1, other arithmetic: 7.3 us -> 0.01 us  [body(): routes_t = routes[0].T.astype(bf16)]
    ppermute x43 -> x45, starting transfers between devices: 24.8 us -> 30.9 us  [flip(): return lax.ppermute(v, axis, [(i, i ^ bit) for i in range(n)])]
    all_to_all x1 -> x0, starting transfers between devices: 5.62 us -> none  [spread(): lax.all_to_all(tiny, ('context', 'dp'), split_axis=0, concat_axis=0, tile...]
    mul x1 -> x0, other arithmetic: 5.49 us -> none  [tables(): jnp.where(lane < half, -1.0, 1.0)[None] * jnp.sin(angle)]
  transfers between devices with their start and end apart: 68 -> 72, of which waited for: 23 -> 25; matrix products, arithmetic and copies ran while one was open for 24% -> 19% of each run, Pallas kernels for 14% -> 18%
where the time goes in v3:
time: 400 us; the launch traced here: 395 us
  waiting for transfers between devices  128 us (32%)
  Pallas kernels  101 us (25%)
  starting transfers between devices  58.6 us (15%)
  other arithmetic  37.9 us (9%)
  matrix products  31.4 us (8%)
  local copies, waits for them, and re-layouts  22.7 us (6%)
  between operations  15.4 us (4%)
    ppermute x45, waiting for transfers between devices, flip(): return lax.ppermute(v, axis, [(i, i ^ bit) for i in range(n)])  59.5 us
    ppermute x10, waiting for transfers between devices, hop_plane(): return lax.ppermute(v, PLANE, pairs)  38.3 us
    dot_general x9, matrix products, dot(): return lax.dot_general(a, b, dims, preferred_element_type=f32)  31.4 us
    ppermute x45, starting transfers between devices, flip(): return lax.ppermute(v, axis, [(i, i ^ bit) for i in range(n)])  30.9 us
    pallas_call x1, Pallas kernels, run_experts(): pl.pallas_call(functools.partial(expert_kernel, by_hand, cap), out_shape=...  30.7 us
    ppermute x6, waiting for transfers between devices, step_up(): return lax.ppermute(v, axis, [(i, (i + 1) % n) for i in range(n)])  27.5 us
    pallas_call x1, Pallas kernels, attn_bwd(): pl.pallas_call(functools.partial(attn_bwd_kernel, n_ctx, qh, kvh), out_sh...  27.4 us
    pallas_call x1, Pallas kernels, attn_fwd(): pl.pallas_call(functools.partial(attn_fwd_kernel, n_ctx, n_w, qh, kvh), o...  24.3 us
  transfers between devices with their start and end apart: 72, of which 25 were waited for; matrix products, arithmetic and copies ran while one was open for 19% of the time, Pallas kernels for 18%

profile of v3, /device:TPU:0, one launch (start us, length us, event | category | flops | bytes accessed | tf_op | source)
XLA Modules:
  0.0 395.0 jit_solution(7191022389196345944)
XLA Ops:
  9.5 3.0 collective-permute-start.1
  12.6 1.7 collective-permute-start.4
  15.1 2.7 collective-permute-start.5
  19.8 1.7 collective-permute-done.6
  21.8 1.4 collective-permute-start.9
  23.5 1.5 collective-permute-start.8
  25.7 1.4 collective-permute-start.12
  27.2 4.4 %collective-permute-done.7.refs_1_ = bf16[4,48,640]{2,1,0:T(8,128)(2,1)S(1)} collective-permute-done((bf16[4,48,640]{2,1,0:T(8,128)(2,1)S(1)}, bf16[4,48,640]{2,1,0:T(8,128)(2,1)S(1)}, u32[]{:S(2)}, u32[]{:S(2)}) %collective-permute-start.7) | collective-permute-done | bytes 245792 | tf_op jit(solution)/shard_map/ppermute | solution.py:578
  31.8 1.6 collective-permute-start.11
  33.9 8.0 %collective-permute-done.10.refs_2_ = bf16[4,48,640]{2,1,0:T(8,128)(2,1)S(1)} collective-permute-done((bf16[4,48,640]{2,1,0:T(8,128)(2,1)S(1)}, bf16[4,48,640]{2,1,0:T(8,128)(2,1)S(1)}, u32[]{:S(2)}, u32[]{:S(2)}) %collective-permute-start.10) | collective-permute-done | bytes 245792 | tf_op jit(solution)/shard_map/ppermute | solution.py:578
  45.1 1.9 collective-permute-done.20
  50.6 2.9 position_tables.1
  58.4 6.6 %norm_rows.1.refs_8_ = bf16[4,256,1536]{2,1,0:T(8,128)(2,1)} custom-call(bf16[256,1536]{1,0:T(8,128)(2,1)} %bitcast.177, bf16[256,1536]{1,0:T(8,128)(2,1)} %copy-done.37, bf16[256,1536]{1,0:T(8,128)(2,1)} %collective-permute-done.12.refs_2_, bf16[256,1536]{1,0:T(8,128)(2,1)} %collective-permute-done.19.refs_3_, f32[1,1536]{1,0:T(1,128)} %reshape.244.refs_4_.gain_ref), custom_call_target="tpu_custom_call" | custom-call | flops 7000000000 | bytes 6000000 | tf_op jit(solution)/shard_map/norm_rows/pallas_call | solution.py:81
  67.1 24.3 %attn_fwd.1 = (bf16[2,256,384]{2,1,0:T(8,128)(2,1)}, bf16[2,256,384]{2,1,0:T(8,128)(2,1)}, bf16[6,1024,128]{2,1,0:T(8,128)(2,1)}, bf16[2,1024,128]{2,1,0:T(8,128...) custom-call(s32[40]{0:T(128)} %pad_add_fusion.place_ref, ...), custom_call_target="tpu_custom_call" | custom-call | flops 20000000000 | bytes 20000000 | tf_op jit(solution)/shard_map/attn_fwd/pallas_call | solution.py:220
  91.5 2.4 convolution_convert_fusion.4
  101.3 6.6 %concatenate.49.refs_17_ = bf16[1536,1152]{1,0:T(8,128)(2,1)} concatenate(bf16[1536,512]{1,0:T(8,128)(2,1)} %bitcast.182, bf16[1536,512]{1,0:T(8,128)(2,1)} %bitcast.183, bf16[1536,64]{1,0:T(8,128)(2,1)S(1)} %pad.9, bf16[1536,64]{1,0:T(8,128)(2,1)S(1)} %pad.9), dimensions={1} | concatenate | bytes 7077888 | tf_op jit(solution)/shard_map/concatenate | solution.py:993
  107.9 10.1 %collective-permute-done.25 = bf16[256,1536]{1,0:T(8,128)(2,1)} collective-permute-done((bf16[256,1536]{1,0:T(8,128)(2,1)}, bf16[256,1536]{1,0:T(8,128)(2,1)}, u32[]{:S(2)}, u32[]{:S(2)}) %collective-permute-start.25) | collective-permute-done | bytes 786464 | tf_op jit(solution)/shard_map/ppermute | solution.py:573
  118.0 1.6 convert_add_fusion.3
  120.4 1.7 collective-permute-done.30
  122.2 1.6 collective-permute-start.31
  124.8 17.6 %collective-permute-done.31.refs_1_ = bf16[2,256,768]{2,1,0:T(8,128)(2,1)S(1)} collective-permute-done((bf16[2,256,768]{2,1,0:T(8,128)(2,1)S(1)}, bf16[2,256,768]{2,1,0:T(8,128)(2,1)S(1)}, u32[]{:S(2)}, u32[]{:S(2)}) %collective-permute-start.31) | collective-permute-done | bytes 786464 | tf_op jit(solution)/shard_map/ppermute | solution.py:653
  144.1 10.4 %collective-permute-done.33.refs_3_ = bf16[2,256,768]{2,1,0:T(8,128)(2,1)} collective-permute-done((bf16[2,256,768]{2,1,0:T(8,128)(2,1)S(1)}, bf16[2,256,768]{2,1,0:T(8,128)(2,1)}, u32[]{:S(2)}, u32[]{:S(2)}) %collective-permute-start.33) | collective-permute-done | bytes 786464 | tf_op jit(solution)/shard_map/ppermute | solution.py:653
  155.1 2.0 collective-permute-done.37.refs_7_
  157.1 30.7 %experts.1 = (bf16[4,2,256,768]{3,2,1,0:T(8,128)(2,1)}, bf16[4,2,256,768]{3,2,1,0:T(8,128)(2,1)}, bf16[4,2,256,768]{3,2,1,0:T(8,128)(2,1)}, bf16[4,2,256,768]{3,...) custom-call(s32[2]{0:T(128)} %pad_add_fusion.1.who_ref, ...), custom_call_target="tpu_custom_call" | custom-call | flops 30000001024 | bytes 30000000 | tf_op jit(solution)/shard_map/experts/pallas_call | solution.py:558
  188.0 5.7 %collective-permute-done.38 = bf16[4,2,256,768]{3,2,1,0:T(8,128)(2,1)S(1)} collective-permute-done((bf16[4,2,256,768]{3,2,1,0:T(8,128)(2,1)}, bf16[4,2,256,768]{3,2,1,0:T(8,128)(2,1)S(1)}, u32[]{:S(2)}, u32[]{:S(2)}) %collective-permute-start.38) | collective-permute-done | bytes 3145760 | tf_op jit(solution)/shard_map/ppermute | solution.py:573
  193.8 3.0 add_convert_fusion.1
  198.2 3.4 convolution_convert_fusion.3
  201.7 5.8 %convolution_convert_fusion.2 = bf16[1536,512]{1,0:T(8,128)(2,1)} fusion(bf16[1152,1536]{1,0:T(8,128)(2,1)} %get-tuple-element.162, bf16[1152,512]{1,0:T(8,128)(2,1)} %get-tuple-element.164), kind=kOutput, calls=%fused_computation.20 | convolution fusion | flops 1812725760 | bytes 6291456 | tf_op jit(solution)/shard_map/dot_general | solution.py:38
  207.5 3.0 fusion.46
  211.1 3.5 convolution_convert_fusion.1
  214.6 3.5 add_convert_fusion
  218.1 2.5 convert_add_fusion.1
  220.7 1.7 collective-permute-start.41
  222.4 10.3 %collective-permute-done.41 = bf16[2,256,768]{2,1,0:T(8,128)(2,1)S(1)} collective-permute-done((bf16[2,256,768]{2,1,0:T(8,128)(2,1)S(1)}, bf16[2,256,768]{2,1,0:T(8,128)(2,1)S(1)}, u32[]{:S(2)}, u32[]{:S(2)}) %collective-permute-start.41) | collective-permute-done | bytes 786464 | tf_op jit(solution)/shard_map/ppermute | solution.py:653
  233.2 1.8 collective-permute-done.42
  237.2 1.7 fusion.42
  238.9 1.6 collective-permute-start.43
  240.5 17.9 %collective-permute-done.43.refs_2_ = bf16[256,1536]{1,0:T(8,128)(2,1)S(1)} collective-permute-done((bf16[256,1536]{1,0:T(8,128)(2,1)S(1)}, bf16[256,1536]{1,0:T(8,128)(2,1)S(1)}, u32[]{:S(2)}, u32[]{:S(2)}) %collective-permute-start.43) | collective-permute-done | bytes 786464 | tf_op jit(solution)/shard_map/ppermute | solution.py:573
  261.8 27.4 %attn_bwd.1 = bf16[4,256,640]{2,1,0:T(8,128)(2,1)} custom-call(bf16[256,1536]{1,0:T(8,128)(2,1)} %copy-done.14, bf16[256,1536]{1,0:T(8,128)(2,1)} %copy-done.38, bf16[256,1536]{1,0:T(8,128)(2,1)} %copy-done.35, bf16[256,1536]{1,0:T(8,128)(2,1)} %collective-permute-done.46.refs_3_, bf16[384,1536]{1,0:T(8,128)(2,1)} %all-gather.2.cloned.1.call-done.refs_4_, ...), custom_call_target="tpu_custom_call" | custom-call | flops 24999999488 | bytes 20000000 | tf_op jit(solution)/shard_map/attn_bwd/pallas_call | solution.py:368
  289.2 5.1 %bitcast_convert_fusion = bf16[1536,640]{1,0:T(8,128)(2,1)S(1)} fusion(bf16[4,256,1536]{2,1,0:T(8,128)(2,1)} %norm_rows.1.refs_8_, bf16[4,256,640]{2,1,0:T(8,128)(2,1)} %attn_bwd.1), kind=kOutput, calls=%fused_computation.5 | convolution fusion | flops 2014248960 | bytes 6422528 | tf_op jit(solution)/shard_map/dot_general | solution.py:38
  296.2 3.8 fusion
  303.6 3.6 fusion.9
  308.6 1.5 pad_maximum_fusion.7
  310.0 3.6 convert_add_fusion.2
  313.7 1.6 collective-permute-start.51
  315.3 3.2 collective-permute-done.47
  318.5 1.4 add_convert_fusion.2
  319.9 1.6 reshape.242
  322.6 2.1 collective-permute-start.48
  324.8 2.9 convert_add_fusion
  329.4 1.5 collective-permute-start.56
  330.9 7.0 %collective-permute-done.48 = bf16[4,48,640]{2,1,0:T(8,128)(2,1)S(1)} collective-permute-done((bf16[4,48,640]{2,1,0:T(8,128)(2,1)S(1)}, bf16[4,48,640]{2,1,0:T(8,128)(2,1)S(1)}, u32[]{:S(2)}, u32[]{:S(2)}) %collective-permute-start.48) | collective-permute-done | bytes 245792 | tf_op jit(solution)/shard_map/ppermute | solution.py:578
  338.0 3.7 collective-permute-start.49
  342.9 8.0 %collective-permute-done.49 = bf16[4,48,640]{2,1,0:T(8,128)(2,1)S(1)} collective-permute-done((bf16[4,48,640]{2,1,0:T(8,128)(2,1)S(1)}, bf16[4,48,640]{2,1,0:T(8,128)(2,1)S(1)}, u32[]{:S(2)}, u32[]{:S(2)}) %collective-permute-start.49) | collective-permute-done | bytes 245792 | tf_op jit(solution)/shard_map/ppermute | solution.py:578
  351.7 2.8 widen.1
  354.5 1.5 collective-permute-start.54
  356.0 4.5 %finish_input.1 = bf16[256,1536]{1,0:T(8,128)(2,1)} custom-call(f32[256,1536]{1,0:T(8,128)} %get-tuple-element.211.dm_ref, f32[256,1536]{1,0:T(8,128)} %get-tuple-element.194.near_ref, bf16[256,1536]{1,0:T(8,128)(2,1)} %collective-permute-done.51.far_ref, bf16[256,1536]{1,0:T(8,128)(2,1)} %bitcast.178, f32[1,1536]{1,0:T(1,128)} %reshape.244.refs_4_.gain_ref), custom_call_target="tpu_custom_call" | custom-call | tf_op jit(solution)/shard_map/finish_input/pallas_call | solution.py:845
  360.6 2.0 collective-permute-done.54
  362.7 1.8 collective-permute-start.64
  364.6 4.1 %collective-permute-start.61 = (f32[10,96]{1,0:T(8,128)S(1)}, f32[10,96]{1,0:T(8,128)S(1)}, u32[]{:S(2)}, u32[]{:S(2)}) collective-permute-start(f32[10,96]{1,0:T(8,128)S(1)} %bitcast.215), channel_id=1, source_target_pairs={{0,2},{1,3},{2,0},{3,1},{4,6},{5,7},{6,4},{7,5},{8,10},{9,11},{10,... | collective-permute-start | bytes 11528 | tf_op jit(solution)/shard_map/ppermute | solution.py:1123
  372.3 3.4 collective-permute-done.65
  375.8 1.5 collective-permute-start.66
  378.5 5.3 %collective-permute-done.66.far_ref = bf16[4,48,640]{2,1,0:T(8,128)(2,1)} collective-permute-done((bf16[4,48,640]{2,1,0:T(8,128)(2,1)S(1)}, bf16[4,48,640]{2,1,0:T(8,128)(2,1)}, u32[]{:S(2)}, u32[]{:S(2)}) %collective-permute-start.66) | collective-permute-done | bytes 245792 | tf_op jit(solution)/shard_map/ppermute | solution.py:573
  383.8 2.1 columns_of.1
  (317 shorter events, 59.3 us)
Async XLA Ops:
  7.2 84.2 %all-gather.2.cloned.1.call-start = ((), (), s32[]{:S(2)}) async-start(), calls=%async_computation.4 | async-start | bytes 1474560 | tf_op jit(solution)/shard_map/all_gather | solution.py:920
  8.6 10.6 %collective-permute-start.3 = (bf16[256,768]{1,0:T(8,128)(2,1)S(1)}, bf16[256,768]{1,0:T(8,128)(2,1)S(1)}, u32[]{:S(2)}, u32[]{:S(2)}) collective-permute-start(bf16[256,768]{1,0:T(8,128)(2,1)S(1)} %get-tuple-element.231), channel_id=1, source_target_pairs={{0,4},{4,0},{8,12},{12,8},{1,5},{5,1},{9,13},{13,9},{2,6},{6,2},{1... | collective-permute-start | bytes 1179656 | tf_op jit(solution)/shard_map/ppermute | solution.py:573
  9.3 5.8 %collective-permute-start = (bf16[48,640]{1,0:T(8,128)(2,1)S(1)}, bf16[48,640]{1,0:T(8,128)(2,1)S(1)}, u32[]{:S(2)}, u32[]{:S(2)}) collective-permute-start(bf16[48,640]{1,0:T(8,128)(2,1)S(1)} %fusion.25), channel_id=1, source_target_pairs={{0,4},{4,0},{8,12},{12,8},{1,5},{5,1},{9,13},{13,9},{2,6},{6,2},{1... | collective-permute-start | bytes 184328 | tf_op jit(solution)/shard_map/ppermute | solution.py:573
  9.5 8.3 %collective-permute-start.1 = (bf16[48,640]{1,0:T(8,128)(2,1)S(1)}, bf16[48,640]{1,0:T(8,128)(2,1)S(1)}, u32[]{:S(2)}, u32[]{:S(2)}) collective-permute-start(bf16[48,640]{1,0:T(8,128)(2,1)S(1)} %fusion.23), channel_id=1, source_target_pairs={{0,8},{4,12},{8,0},{12,4},{1,9},{5,13},{9,1},{13,5},{2,10},{6,14},... | collective-permute-start | bytes 184328 | tf_op jit(solution)/shard_map/ppermute | solution.py:573
  12.5 6.7 %collective-permute-start.2 = (bf16[48,640]{1,0:T(8,128)(2,1)S(1)}, bf16[48,640]{1,0:T(8,128)(2,1)S(1)}, u32[]{:S(2)}, u32[]{:S(2)}) collective-permute-start(bf16[48,640]{1,0:T(8,128)(2,1)S(1)} %fusion.21), channel_id=1, source_target_pairs={{0,12},{4,8},{8,4},{12,0},{1,13},{5,9},{9,5},{13,1},{2,14},{6,10},... | collective-permute-start | bytes 184328 | tf_op jit(solution)/shard_map/ppermute | solution.py:573
  12.6 6.7 %collective-permute-start.4 = (bf16[10,256]{1,0:T(8,128)(2,1)S(1)}, bf16[10,256]{1,0:T(8,128)(2,1)S(1)}, u32[]{:S(2)}, u32[]{:S(2)}) collective-permute-start(bf16[10,256]{1,0:T(8,128)(2,1)S(1)} %fusion.33), channel_id=1, source_target_pairs={{0,1},{1,2},{2,3},{3,0},{4,5},{5,6},{6,7},{7,4},{8,9},{9,10},{10,1... | collective-permute-start | bytes 15368 | tf_op jit(solution)/shard_map/ppermute | solution.py:607
  15.1 4.6 %collective-permute-start.5 = (bf16[10,256]{1,0:T(8,128)(2,1)S(1)}, bf16[10,256]{1,0:T(8,128)(2,1)S(1)}, u32[]{:S(2)}, u32[]{:S(2)}) collective-permute-start(bf16[10,256]{1,0:T(8,128)(2,1)S(1)} %fusion.33), channel_id=1, source_target_pairs={{0,2},{1,3},{2,0},{3,1},{4,6},{5,7},{6,4},{7,5},{8,10},{9,11},{10,... | collective-permute-start | bytes 15368 | tf_op jit(solution)/shard_map/ppermute | solution.py:607
  19.2 38.3 %collective-permute-start.18 = (bf16[256,1536]{1,0:T(8,128)(2,1)S(1)}, bf16[256,1536]{1,0:T(8,128)(2,1)S(1)}, u32[]{:S(2)}, u32[]{:S(2)}) collective-permute-start(bf16[256,1536]{1,0:T(8,128)(2,1)S(1)} %bitcast.179), channel_id=1, source_target_pairs={{0,4},{4,0},{8,12},{12,8},{1,5},{5,1},{9,13},{13,9},{2,6},{6,2},{1... | collective-permute-start | bytes 2359304 | tf_op jit(solution)/shard_map/ppermute | solution.py:573
  21.8 3.9 collective-permute-start.9
  23.2 8.4 %collective-permute-start.7 = (bf16[4,48,640]{2,1,0:T(8,128)(2,1)S(1)}, bf16[4,48,640]{2,1,0:T(8,128)(2,1)S(1)}, u32[]{:S(2)}, u32[]{:S(2)}) collective-permute-start(bf16[4,48,640]{2,1,0:T(8,128)(2,1)S(1)} %pad_maximum_fusion.4.refs_0_), channel_id=1, source_target_pairs={{0,1},{1,2},{2,3},{3,0},{4,5},{5,6},{6,7},{7,4},{8,9},{9,10},{10,1... | collective-permute-start | bytes 737288 | tf_op jit(solution)/shard_map/ppermute | solution.py:578
  23.5 8.2 %collective-permute-start.8 = (bf16[4,48,640]{2,1,0:T(8,128)(2,1)S(1)}, bf16[4,48,640]{2,1,0:T(8,128)(2,1)S(1)}, u32[]{:S(2)}, u32[]{:S(2)}) collective-permute-start(bf16[4,48,640]{2,1,0:T(8,128)(2,1)S(1)} %pad_maximum_fusion.4.refs_0_), channel_id=1, source_target_pairs={{0,16},{16,0},{1,17},{17,1},{2,18},{18,2},{3,19},{19,3},{4,20},{20... | collective-permute-start | bytes 737288 | tf_op jit(solution)/shard_map/ppermute | solution.py:573
  25.7 17.5 %collective-permute-start.12 = (bf16[256,1536]{1,0:T(8,128)(2,1)S(1)}, bf16[256,1536]{1,0:T(8,128)(2,1)}, u32[]{:S(2)}, u32[]{:S(2)}) collective-permute-start(bf16[256,1536]{1,0:T(8,128)(2,1)S(1)} %bitcast.180), channel_id=1, source_target_pairs={{0,8},{4,12},{8,0},{12,4},{1,9},{5,13},{9,1},{13,5},{2,10},{6,14},... | collective-permute-start | bytes 2359304 | tf_op jit(solution)/shard_map/ppermute | solution.py:573
  31.7 10.1 %collective-permute-start.10 = (bf16[4,48,640]{2,1,0:T(8,128)(2,1)S(1)}, bf16[4,48,640]{2,1,0:T(8,128)(2,1)S(1)}, u32[]{:S(2)}, u32[]{:S(2)}) collective-permute-start(bf16[4,48,640]{2,1,0:T(8,128)(2,1)S(1)} %collective-permute-done.7.refs_1_), channel_id=1, source_target_pairs={{0,1},{1,2},{2,3},{3,0},{4,5},{5,6},{6,7},{7,4},{8,9},{9,10},{10,1... | collective-permute-start | bytes 737288 | tf_op jit(solution)/shard_map/ppermute | solution.py:578
  31.8 10.1 %collective-permute-start.11 = (bf16[4,48,640]{2,1,0:T(8,128)(2,1)S(1)}, bf16[4,48,640]{2,1,0:T(8,128)(2,1)S(1)}, u32[]{:S(2)}, u32[]{:S(2)}) collective-permute-start(bf16[4,48,640]{2,1,0:T(8,128)(2,1)S(1)} %collective-permute-done.7.refs_1_), channel_id=1, source_target_pairs={{0,16},{16,0},{1,17},{17,1},{2,18},{18,2},{3,19},{19,3},{4,20},{20... | collective-permute-start | bytes 737288 | tf_op jit(solution)/shard_map/ppermute | solution.py:573
  33.4 23.1 %collective-permute-start.16 = (bf16[2,256,768]{2,1,0:T(8,128)(2,1)S(1)}, bf16[2,256,768]{2,1,0:T(8,128)(2,1)}, u32[]{:S(2)}, u32[]{:S(2)}) collective-permute-start(bf16[2,256,768]{2,1,0:T(8,128)(2,1)S(1)} %pad_maximum_fusion.1.refs_8_), channel_id=1, source_target_pairs={{0,8},{4,20},{8,0},{12,28},{16,24},{20,4},{24,16},{28,12},{1,9},{5... | collective-permute-start | bytes 2359304 | tf_op jit(solution)/shard_map/ppermute | solution.py:653
  43.2 14.3 %collective-permute-start.19 = (bf16[256,1536]{1,0:T(8,128)(2,1)}, bf16[256,1536]{1,0:T(8,128)(2,1)}, u32[]{:S(2)}, u32[]{:S(2)}) collective-permute-start(bf16[256,1536]{1,0:T(8,128)(2,1)} %collective-permute-done.12.refs_2_), channel_id=1, source_target_pairs={{0,4},{4,0},{8,12},{12,8},{1,5},{5,1},{9,13},{13,9},{2,6},{6,2},{1... | collective-permute-start | bytes 2359304 | tf_op jit(solution)/shard_map/ppermute | solution.py:573
  43.2 3.9 collective-permute-start.20
  44.7 11.8 %collective-permute-start.14 = (bf16[4,48,640]{2,1,0:T(8,128)(2,1)}, bf16[4,48,640]{2,1,0:T(8,128)(2,1)}, u32[]{:S(2)}, u32[]{:S(2)}) collective-permute-start(bf16[4,48,640]{2,1,0:T(8,128)(2,1)} %copy-done.43), channel_id=1, source_target_pairs={{0,1},{1,2},{2,3},{3,0},{4,5},{5,6},{6,7},{7,4},{8,9},{9,10},{10,1... | collective-permute-start | bytes 737288 | tf_op jit(solution)/shard_map/ppermute | solution.py:578
  47.1 9.4 %collective-permute-start.15 = (bf16[4,48,640]{2,1,0:T(8,128)(2,1)}, bf16[4,48,640]{2,1,0:T(8,128)(2,1)}, u32[]{:S(2)}, u32[]{:S(2)}) collective-permute-start(bf16[4,48,640]{2,1,0:T(8,128)(2,1)} %copy-done.43), channel_id=1, source_target_pairs={{0,16},{16,0},{1,17},{17,1},{2,18},{18,2},{3,19},{19,3},{4,20},{20... | collective-permute-start | bytes 737288 | tf_op jit(solution)/shard_map/ppermute | solution.py:573
  56.5 8.5 %collective-permute-start.17 = (bf16[4,48,640]{2,1,0:T(8,128)(2,1)}, bf16[4,48,640]{2,1,0:T(8,128)(2,1)S(1)}, u32[]{:S(2)}, u32[]{:S(2)}) collective-permute-start(bf16[4,48,640]{2,1,0:T(8,128)(2,1)} %collective-permute-done.14.refs_3_), channel_id=1, source_target_pairs={{0,16},{16,0},{1,17},{17,1},{2,18},{18,2},{3,19},{19,3},{4,20},{20... | collective-permute-start | bytes 737288 | tf_op jit(solution)/shard_map/ppermute | solution.py:573
  57.2 203.3 %reduce-scatter.5.cloned.1.call-start = ((), (), s32[]{:S(2)}) async-start(), calls=%async_computation.5 | async-start | bytes 1966080 | tf_op jit(solution)/shard_map/reduce_scatter | solution.py:1024
  65.0 26.5 %collective-permute-start.21 = (bf16[2,256,768]{2,1,0:T(8,128)(2,1)S(1)}, bf16[2,256,768]{2,1,0:T(8,128)(2,1)}, u32[]{:S(2)}, u32[]{:S(2)}) collective-permute-start(bf16[2,256,768]{2,1,0:T(8,128)(2,1)S(1)} %pad_maximum_fusion.1.refs_8_), channel_id=1, source_target_pairs={{0,16},{4,12},{8,24},{12,4},{16,0},{20,28},{24,8},{28,20},{1,17},{... | collective-permute-start | bytes 2359304 | tf_op jit(solution)/shard_map/ppermute | solution.py:653
  66.4 25.1 %collective-permute-start.22 = (bf16[2,256,768]{2,1,0:T(8,128)(2,1)}, bf16[2,256,768]{2,1,0:T(8,128)(2,1)}, u32[]{:S(2)}, u32[]{:S(2)}) collective-permute-start(bf16[2,256,768]{2,1,0:T(8,128)(2,1)} %collective-permute-done.16.refs_9_), channel_id=1, source_target_pairs={{0,16},{4,12},{8,24},{12,4},{16,0},{20,28},{24,8},{28,20},{1,17},{... | collective-permute-start | bytes 2359304 | tf_op jit(solution)/shard_map/ppermute | solution.py:653
  96.2 3.8 collective-permute-start.23
  98.2 19.8 %collective-permute-start.25 = (bf16[256,1536]{1,0:T(8,128)(2,1)}, bf16[256,1536]{1,0:T(8,128)(2,1)}, u32[]{:S(2)}, u32[]{:S(2)}) collective-permute-start(bf16[256,1536]{1,0:T(8,128)(2,1)} %add_convert_fusion.4), channel_id=1, source_target_pairs={{0,8},{4,12},{8,0},{12,4},{1,9},{5,13},{9,1},{13,5},{2,10},{6,14},... | collective-permute-start | bytes 2359304 | tf_op jit(solution)/shard_map/ppermute | solution.py:573
  99.3 20.4 %collective-permute-start.26 = (bf16[2,256,768]{2,1,0:T(8,128)(2,1)S(1)}, bf16[2,256,768]{2,1,0:T(8,128)(2,1)}, u32[]{:S(2)}, u32[]{:S(2)}) collective-permute-start(bf16[2,256,768]{2,1,0:T(8,128)(2,1)S(1)} %copy-done.17), channel_id=1, source_target_pairs={{0,4},{4,0},{8,12},{12,8},{1,5},{5,1},{9,13},{13,9},{2,6},{6,2},{1... | collective-permute-start | bytes 2359304 | tf_op jit(solution)/shard_map/ppermute | solution.py:573
  99.5 20.2 %collective-permute-start.27 = (bf16[2,256,768]{2,1,0:T(8,128)(2,1)}, bf16[2,256,768]{2,1,0:T(8,128)(2,1)}, u32[]{:S(2)}, u32[]{:S(2)}) collective-permute-start(bf16[2,256,768]{2,1,0:T(8,128)(2,1)} %collective-permute-done.16.refs_9_), channel_id=1, source_target_pairs={{0,4},{4,0},{8,12},{12,8},{1,5},{5,1},{9,13},{13,9},{2,6},{6,2},{1... | collective-permute-start | bytes 2359304 | tf_op jit(solution)/shard_map/ppermute | solution.py:573
  99.8 19.9 %collective-permute-start.28 = (bf16[2,256,768]{2,1,0:T(8,128)(2,1)}, bf16[2,256,768]{2,1,0:T(8,128)(2,1)}, u32[]{:S(2)}, u32[]{:S(2)}) collective-permute-start(bf16[2,256,768]{2,1,0:T(8,128)(2,1)} %collective-permute-done.21.refs_10_), channel_id=1, source_target_pairs={{0,4},{4,0},{8,12},{12,8},{1,5},{5,1},{9,13},{13,9},{2,6},{6,2},{1... | collective-permute-start | bytes 2359304 | tf_op jit(solution)/shard_map/ppermute | solution.py:573
  100.9 18.8 %collective-permute-start.29 = (bf16[2,256,768]{2,1,0:T(8,128)(2,1)}, bf16[2,256,768]{2,1,0:T(8,128)(2,1)}, u32[]{:S(2)}, u32[]{:S(2)}) collective-permute-start(bf16[2,256,768]{2,1,0:T(8,128)(2,1)} %collective-permute-done.22.refs_11_), channel_id=1, source_target_pairs={{0,4},{4,0},{8,12},{12,8},{1,5},{5,1},{9,13},{13,9},{2,6},{6,2},{1... | collective-permute-start | bytes 2359304 | tf_op jit(solution)/shard_map/ppermute | solution.py:573
  122.2 20.2 %collective-permute-start.31 = (bf16[2,256,768]{2,1,0:T(8,128)(2,1)S(1)}, bf16[2,256,768]{2,1,0:T(8,128)(2,1)S(1)}, u32[]{:S(2)}, u32[]{:S(2)}) collective-permute-start(bf16[2,256,768]{2,1,0:T(8,128)(2,1)S(1)} %pad_maximum_fusion.2.refs_0_), channel_id=1, source_target_pairs={{0,8},{4,20},{8,0},{12,28},{16,24},{20,4},{24,16},{28,12},{1,9},{5... | collective-permute-start | bytes 2359304 | tf_op jit(solution)/shard_map/ppermute | solution.py:653
  123.8 20.3 %collective-permute-start.32 = (bf16[2,256,768]{2,1,0:T(8,128)(2,1)S(1)}, bf16[2,256,768]{2,1,0:T(8,128)(2,1)}, u32[]{:S(2)}, u32[]{:S(2)}) collective-permute-start(bf16[2,256,768]{2,1,0:T(8,128)(2,1)S(1)} %pad_maximum_fusion.2.refs_0_), channel_id=1, source_target_pairs={{0,16},{4,12},{8,24},{12,4},{16,0},{20,28},{24,8},{28,20},{1,17},{... | collective-permute-start | bytes 2359304 | tf_op jit(solution)/shard_map/ppermute | solution.py:653
  142.3 12.1 %collective-permute-start.33 = (bf16[2,256,768]{2,1,0:T(8,128)(2,1)S(1)}, bf16[2,256,768]{2,1,0:T(8,128)(2,1)}, u32[]{:S(2)}, u32[]{:S(2)}) collective-permute-start(bf16[2,256,768]{2,1,0:T(8,128)(2,1)S(1)} %collective-permute-done.31.refs_1_), channel_id=1, source_target_pairs={{0,16},{4,12},{8,24},{12,4},{16,0},{20,28},{24,8},{28,20},{1,17},{... | collective-permute-start | bytes 2359304 | tf_op jit(solution)/shard_map/ppermute | solution.py:653
  143.6 11.5 %collective-permute-start.34 = (bf16[2,256,768]{2,1,0:T(8,128)(2,1)S(1)}, bf16[2,256,768]{2,1,0:T(8,128)(2,1)}, u32[]{:S(2)}, u32[]{:S(2)}) collective-permute-start(bf16[2,256,768]{2,1,0:T(8,128)(2,1)S(1)} %pad_maximum_fusion.2.refs_0_), channel_id=1, source_target_pairs={{0,4},{4,0},{8,12},{12,8},{1,5},{5,1},{9,13},{13,9},{2,6},{6,2},{1... | collective-permute-start | bytes 2359304 | tf_op jit(solution)/shard_map/ppermute | solution.py:573
  143.6 11.5 %collective-permute-start.35 = (bf16[2,256,768]{2,1,0:T(8,128)(2,1)S(1)}, bf16[2,256,768]{2,1,0:T(8,128)(2,1)}, u32[]{:S(2)}, u32[]{:S(2)}) collective-permute-start(bf16[2,256,768]{2,1,0:T(8,128)(2,1)S(1)} %collective-permute-done.31.refs_1_), channel_id=1, source_target_pairs={{0,4},{4,0},{8,12},{12,8},{1,5},{5,1},{9,13},{13,9},{2,6},{6,2},{1... | collective-permute-start | bytes 2359304 | tf_op jit(solution)/shard_map/ppermute | solution.py:573
  144.1 11.0 %collective-permute-start.36 = (bf16[2,256,768]{2,1,0:T(8,128)(2,1)}, bf16[2,256,768]{2,1,0:T(8,128)(2,1)}, u32[]{:S(2)}, u32[]{:S(2)}) collective-permute-start(bf16[2,256,768]{2,1,0:T(8,128)(2,1)} %collective-permute-done.32.refs_2_), channel_id=1, source_target_pairs={{0,4},{4,0},{8,12},{12,8},{1,5},{5,1},{9,13},{13,9},{2,6},{6,2},{1... | collective-permute-start | bytes 2359304 | tf_op jit(solution)/shard_map/ppermute | solution.py:573
  187.8 5.9 %collective-permute-start.38 = (bf16[4,2,256,768]{3,2,1,0:T(8,128)(2,1)}, bf16[4,2,256,768]{3,2,1,0:T(8,128)(2,1)S(1)}, u32[]{:S(2)}, u32[]{:S(2)}) collective-permute-start(bf16[4,2,256,768]{3,2,1,0:T(8,128)(2,1)} %get-tuple-element.159), channel_id=1, source_target_pairs={{0,4},{4,0},{8,12},{12,8},{1,5},{5,1},{9,13},{13,9},{2,6},{6,2},{1... | collective-permute-start | bytes 9437192 | tf_op jit(solution)/shard_map/ppermute | solution.py:573
  196.8 17.8 %collective-permute-start.39 = (bf16[4,2,256,768]{3,2,1,0:T(8,128)(2,1)}, bf16[4,2,256,768]{3,2,1,0:T(8,128)(2,1)}, u32[]{:S(2)}, u32[]{:S(2)}) collective-permute-start(bf16[4,2,256,768]{3,2,1,0:T(8,128)(2,1)} %get-tuple-element.160), channel_id=1, source_target_pairs={{0,4},{4,0},{8,12},{12,8},{1,5},{5,1},{9,13},{13,9},{2,6},{6,2},{1... | collective-permute-start | bytes 9437192 | tf_op jit(solution)/shard_map/ppermute | solution.py:573
  197.0 21.1 %collective-permute-start.40 = (bf16[2,2,256,768]{3,2,1,0:T(8,128)(2,1)S(1)}, bf16[2,2,256,768]{3,2,1,0:T(8,128)(2,1)}, u32[]{:S(2)}, u32[]{:S(2)}) collective-permute-start(bf16[2,2,256,768]{3,2,1,0:T(8,128)(2,1)S(1)} %add_convert_fusion.1), channel_id=1, source_target_pairs={{0,16},{4,12},{8,24},{12,4},{16,0},{20,28},{24,8},{28,20},{1,17},{... | collective-permute-start | bytes 4718600 | tf_op jit(solution)/shard_map/ppermute | solution.py:653
  201.6 87.6 %reduce-scatter.7.cloned.1.call-start = ((), (), s32[]{:S(2)}) async-start(), calls=%async_computation.6 | async-start | bytes 1966080 | tf_op jit(solution)/shard_map/reduce_scatter | solution.py:1024
  220.7 12.1 %collective-permute-start.41 = (bf16[2,256,768]{2,1,0:T(8,128)(2,1)S(1)}, bf16[2,256,768]{2,1,0:T(8,128)(2,1)S(1)}, u32[]{:S(2)}, u32[]{:S(2)}) collective-permute-start(bf16[2,256,768]{2,1,0:T(8,128)(2,1)S(1)} %fusion.16), channel_id=1, source_target_pairs={{0,8},{4,20},{8,0},{12,28},{16,24},{20,4},{24,16},{28,12},{1,9},{5... | collective-permute-start | bytes 2359304 | tf_op jit(solution)/shard_map/ppermute | solution.py:653
  233.1 118.6 %reduce-scatter.11.cloned.1.call-start = ((), (), s32[]{:S(2)}) async-start(), calls=%async_computation.8 | async-start | bytes 1966080 | tf_op jit(solution)/shard_map/reduce_scatter | solution.py:1024
  238.9 19.6 %collective-permute-start.43 = (bf16[256,1536]{1,0:T(8,128)(2,1)S(1)}, bf16[256,1536]{1,0:T(8,128)(2,1)S(1)}, u32[]{:S(2)}, u32[]{:S(2)}) collective-permute-start(bf16[256,1536]{1,0:T(8,128)(2,1)S(1)} %get-tuple-element.210.refs_0_), channel_id=1, source_target_pairs={{0,8},{4,12},{8,0},{12,4},{1,9},{5,13},{9,1},{13,5},{2,10},{6,14},... | collective-permute-start | bytes 2359304 | tf_op jit(solution)/shard_map/ppermute | solution.py:573
  240.5 17.9 %collective-permute-start.44 = (bf16[256,1536]{1,0:T(8,128)(2,1)S(1)}, bf16[256,1536]{1,0:T(8,128)(2,1)S(1)}, u32[]{:S(2)}, u32[]{:S(2)}) collective-permute-start(bf16[256,1536]{1,0:T(8,128)(2,1)S(1)} %get-tuple-element.210.refs_0_), channel_id=1, source_target_pairs={{0,4},{4,0},{8,12},{12,8},{1,5},{5,1},{9,13},{13,9},{2,6},{6,2},{1... | collective-permute-start | bytes 2359304 | tf_op jit(solution)/shard_map/ppermute | solution.py:573
  259.4 95.1 %reduce-scatter.9.cloned.1.call-start = ((), (), s32[]{:S(2)}) async-start(), calls=%async_computation.7 | async-start | bytes 1474560 | tf_op jit(solution)/shard_map/reduce_scatter | solution.py:1075
  259.5 55.9 %collective-permute-start.45 = (bf16[2,2,256,768]{3,2,1,0:T(8,128)(2,1)}, bf16[2,2,256,768]{3,2,1,0:T(8,128)(2,1)}, u32[]{:S(2)}, u32[]{:S(2)}) collective-permute-start(bf16[2,2,256,768]{3,2,1,0:T(8,128)(2,1)} %add_convert_fusion), channel_id=1, source_target_pairs={{0,16},{4,12},{8,24},{12,4},{16,0},{20,28},{24,8},{28,20},{1,17},{... | collective-permute-start | bytes 4718600 | tf_op jit(solution)/shard_map/ppermute | solution.py:653
  294.5 24.0 %collective-permute-start.47 = (bf16[16,48,640]{2,1,0:T(8,128)(2,1)S(1)}, bf16[16,48,640]{2,1,0:T(8,128)(2,1)}, u32[]{:S(2)}, u32[]{:S(2)}) collective-permute-start(bf16[16,48,640]{2,1,0:T(8,128)(2,1)S(1)} %get-tuple-element.221), channel_id=1, source_target_pairs={{0,16},{16,0},{1,17},{17,1},{2,18},{18,2},{3,19},{19,3},{4,20},{20... | collective-permute-start | bytes 2949128 | tf_op jit(solution)/shard_map/ppermute | solution.py:573
  302.2 7.8 %collective-permute-start.50 = (bf16[256,1536]{1,0:T(8,128)(2,1)}, bf16[256,1536]{1,0:T(8,128)(2,1)}, u32[]{:S(2)}, u32[]{:S(2)}) collective-permute-start(bf16[256,1536]{1,0:T(8,128)(2,1)} %get-tuple-element.217), channel_id=1, source_target_pairs={{0,4},{4,0},{8,12},{12,8},{1,5},{5,1},{9,13},{13,9},{2,6},{6,2},{1... | collective-permute-start | bytes 2359304 | tf_op jit(solution)/shard_map/ppermute | solution.py:573
  302.4 7.7 %collective-permute-start.59 = (bf16[256,1536]{1,0:T(8,128)(2,1)}, bf16[256,1536]{1,0:T(8,128)(2,1)}, u32[]{:S(2)}, u32[]{:S(2)}) collective-permute-start(bf16[256,1536]{1,0:T(8,128)(2,1)} %get-tuple-element.216), channel_id=1, source_target_pairs={{0,4},{4,0},{8,12},{12,8},{1,5},{5,1},{9,13},{13,9},{2,6},{6,2},{1... | collective-permute-start | bytes 2359304 | tf_op jit(solution)/shard_map/ppermute | solution.py:573
  313.7 29.2 %collective-permute-start.51 = (bf16[256,1536]{1,0:T(8,128)(2,1)}, bf16[256,1536]{1,0:T(8,128)(2,1)}, u32[]{:S(2)}, u32[]{:S(2)}) collective-permute-start(bf16[256,1536]{1,0:T(8,128)(2,1)} %get-tuple-element.215), channel_id=1, source_target_pairs={{0,8},{4,12},{8,0},{12,4},{1,9},{5,13},{9,1},{13,5},{2,10},{6,14},... | collective-permute-start | bytes 2359304 | tf_op jit(solution)/shard_map/ppermute | solution.py:573
  321.6 6.8 %collective-permute-start.55 = (f32[16,10,96]{2,0,1:T(8,128)}, f32[16,10,96]{2,0,1:T(8,128)S(1)}, u32[]{:S(2)}, u32[]{:S(2)}) collective-permute-start(f32[16,10,96]{2,0,1:T(8,128)} %bitcast.57), channel_id=1, source_target_pairs={{0,16},{16,0},{1,17},{17,1},{2,18},{18,2},{3,19},{19,3},{4,20},{20... | collective-permute-start | bytes 184328 | tf_op jit(solution)/shard_map/ppermute | solution.py:573
  322.6 15.3 %collective-permute-start.48 = (bf16[4,48,640]{2,1,0:T(8,128)(2,1)S(1)}, bf16[4,48,640]{2,1,0:T(8,128)(2,1)S(1)}, u32[]{:S(2)}, u32[]{:S(2)}) collective-permute-start(bf16[4,48,640]{2,1,0:T(8,128)(2,1)S(1)} %get-tuple-element.224), channel_id=1, source_target_pairs={{0,1},{1,2},{2,3},{3,0},{4,5},{5,6},{6,7},{7,4},{8,9},{9,10},{10,1... | collective-permute-start | bytes 737288 | tf_op jit(solution)/shard_map/ppermute | solution.py:578
  327.8 32.7 %collective-permute-start.53 = (bf16[2,256,768]{2,1,0:T(8,128)(2,1)S(1)}, bf16[2,256,768]{2,1,0:T(8,128)(2,1)}, u32[]{:S(2)}, u32[]{:S(2)}) collective-permute-start(bf16[2,256,768]{2,1,0:T(8,128)(2,1)S(1)} %fusion.17), channel_id=1, source_target_pairs={{0,8},{4,20},{8,0},{12,28},{16,24},{20,4},{24,16},{28,12},{1,9},{5... | collective-permute-start | bytes 2359304 | tf_op jit(solution)/shard_map/ppermute | solution.py:653
  329.4 13.4 %collective-permute-start.56 = (f32[2,4,10,96]{3,1,2,0:T(4,128)S(1)}, f32[2,4,10,96]{3,1,2,0:T(4,128)S(1)}, u32[]{:S(2)}, u32[]{:S(2)}) collective-permute-start(f32[2,4,10,96]{3,1,2,0:T(4,128)S(1)} %bitcast.207), channel_id=1, source_target_pairs={{0,8},{4,12},{8,0},{12,4},{1,9},{5,13},{9,1},{13,5},{2,10},{6,14},... | collective-permute-start | bytes 92168 | tf_op jit(solution)/shard_map/ppermute | solution.py:573
  338.0 12.9 %collective-permute-start.49 = (bf16[4,48,640]{2,1,0:T(8,128)(2,1)S(1)}, bf16[4,48,640]{2,1,0:T(8,128)(2,1)S(1)}, u32[]{:S(2)}, u32[]{:S(2)}) collective-permute-start(bf16[4,48,640]{2,1,0:T(8,128)(2,1)S(1)} %add_convert_fusion.7), channel_id=1, source_target_pairs={{0,1},{1,2},{2,3},{3,0},{4,5},{5,6},{6,7},{7,4},{8,9},{9,10},{10,1... | collective-permute-start | bytes 737288 | tf_op jit(solution)/shard_map/ppermute | solution.py:578
  342.8 13.2 %collective-permute-start.57 = (f32[4,10,96]{2,0,1:T(4,128)S(1)}, f32[4,10,96]{2,0,1:T(4,128)S(1)}, u32[]{:S(2)}, u32[]{:S(2)}) collective-permute-start(f32[4,10,96]{2,0,1:T(4,128)S(1)} %dynamic-slice_bitcast_fusion.9), channel_id=1, source_target_pairs={{0,4},{4,0},{8,12},{12,8},{1,5},{5,1},{9,13},{13,9},{2,6},{6,2},{1... | collective-permute-start | bytes 46088 | tf_op jit(solution)/shard_map/ppermute | solution.py:573
  351.0 9.5 %collective-permute-start.52 = (bf16[4,48,640]{2,1,0:T(8,128)(2,1)S(1)}, bf16[4,48,640]{2,1,0:T(8,128)(2,1)S(1)}, u32[]{:S(2)}, u32[]{:S(2)}) collective-permute-start(bf16[4,48,640]{2,1,0:T(8,128)(2,1)S(1)} %add_convert_fusion.6), channel_id=1, source_target_pairs={{0,1},{1,2},{2,3},{3,0},{4,5},{5,6},{6,7},{7,4},{8,9},{9,10},{10,1... | collective-permute-start | bytes 737288 | tf_op jit(solution)/shard_map/ppermute | solution.py:578
  354.5 8.1 %collective-permute-start.54 = (bf16[96,1536]{1,0:T(8,128)(2,1)}, bf16[96,1536]{1,0:T(8,128)(2,1)S(1)}, u32[]{:S(2)}, u32[]{:S(2)}) collective-permute-start(bf16[96,1536]{1,0:T(8,128)(2,1)} %reduce-scatter.9.cloned.1.call-done), channel_id=1, source_target_pairs={{0,16},{16,0},{1,17},{17,1},{2,18},{18,2},{3,19},{19,3},{4,20},{20... | collective-permute-start | bytes 884744 | tf_op jit(solution)/shard_map/ppermute | solution.py:573
  362.6 9.7 %collective-permute-start.63 = (bf16[48,640]{1,0:T(8,128)(2,1)S(1)}, bf16[48,640]{1,0:T(8,128)(2,1)S(1)}, u32[]{:S(2)}, u32[]{:S(2)}) collective-permute-start(bf16[48,640]{1,0:T(8,128)(2,1)S(1)} %get-tuple-element.239), channel_id=1, source_target_pairs={{0,4},{4,0},{8,12},{12,8},{1,5},{5,1},{9,13},{13,9},{2,6},{6,2},{1... | collective-permute-start | bytes 184328 | tf_op jit(solution)/shard_map/ppermute | solution.py:573
  362.7 9.6 %collective-permute-start.64 = (bf16[48,640]{1,0:T(8,128)(2,1)S(1)}, bf16[48,640]{1,0:T(8,128)(2,1)S(1)}, u32[]{:S(2)}, u32[]{:S(2)}) collective-permute-start(bf16[48,640]{1,0:T(8,128)(2,1)S(1)} %get-tuple-element.238), channel_id=1, source_target_pairs={{0,8},{4,12},{8,0},{12,4},{1,9},{5,13},{9,1},{13,5},{2,10},{6,14},... | collective-permute-start | bytes 184328 | tf_op jit(solution)/shard_map/ppermute | solution.py:573
  364.5 7.2 %collective-permute-start.60 = (f32[10,96]{1,0:T(8,128)S(1)}, f32[10,96]{1,0:T(8,128)S(1)}, u32[]{:S(2)}, u32[]{:S(2)}) collective-permute-start(f32[10,96]{1,0:T(8,128)S(1)} %bitcast.216), channel_id=1, source_target_pairs={{0,1},{1,2},{2,3},{3,0},{4,5},{5,6},{6,7},{7,4},{8,9},{9,10},{10,1... | collective-permute-start | bytes 11528 | tf_op jit(solution)/shard_map/ppermute | solution.py:1123
  364.6 7.1 %collective-permute-start.61 = (f32[10,96]{1,0:T(8,128)S(1)}, f32[10,96]{1,0:T(8,128)S(1)}, u32[]{:S(2)}, u32[]{:S(2)}) collective-permute-start(f32[10,96]{1,0:T(8,128)S(1)} %bitcast.215), channel_id=1, source_target_pairs={{0,2},{1,3},{2,0},{3,1},{4,6},{5,7},{6,4},{7,5},{8,10},{9,11},{10,... | collective-permute-start | bytes 11528 | tf_op jit(solution)/shard_map/ppermute | solution.py:1123
  371.7 4.1 %collective-permute-start.65 = (bf16[48,640]{1,0:T(8,128)(2,1)S(1)}, bf16[48,640]{1,0:T(8,128)(2,1)S(1)}, u32[]{:S(2)}, u32[]{:S(2)}) collective-permute-start(bf16[48,640]{1,0:T(8,128)(2,1)S(1)} %get-tuple-element.237), channel_id=1, source_target_pairs={{0,12},{4,8},{8,4},{12,0},{1,13},{5,9},{9,5},{13,1},{2,14},{6,10},... | collective-permute-start | bytes 184328 | tf_op jit(solution)/shard_map/ppermute | solution.py:573
  371.7 14.2 %collective-permute-start.58 = (bf16[256,768]{1,0:T(8,128)(2,1)}, bf16[256,768]{1,0:T(8,128)(2,1)}, u32[]{:S(2)}, u32[]{:S(2)}) collective-permute-start(bf16[256,768]{1,0:T(8,128)(2,1)} %fusion.19), channel_id=1, source_target_pairs={{0,4},{4,0},{8,12},{12,8},{1,5},{5,1},{9,13},{13,9},{2,6},{6,2},{1... | collective-permute-start | bytes 1179656 | tf_op jit(solution)/shard_map/ppermute | solution.py:573
  375.8 7.9 %collective-permute-start.66 = (bf16[4,48,640]{2,1,0:T(8,128)(2,1)S(1)}, bf16[4,48,640]{2,1,0:T(8,128)(2,1)}, u32[]{:S(2)}, u32[]{:S(2)}) collective-permute-start(bf16[4,48,640]{2,1,0:T(8,128)(2,1)S(1)} %pad_maximum_fusion.5.near_ref), channel_id=1, source_target_pairs={{0,16},{16,0},{1,17},{17,1},{2,18},{18,2},{3,19},{19,3},{4,20},{20... | collective-permute-start | bytes 737288 | tf_op jit(solution)/shard_map/ppermute | solution.py:573
  (61 other events, 454.3 us)
Sparse Core Ops, SparseCore 0:
  57.4 31.6 all-gather.1
  201.8 35.6 reduce-scatter.4
  239.7 34.2 reduce-scatter.6
  276.2 34.2 reduce-scatter.10
  312.6 34.2 reduce-scatter.8

commit v4 on v3

--- a/solution.py
+++ b/solution.py
@@ -382,7 +382,7 @@
             pltpu.SemaphoreType.DMA((n_ctx,)),
         ],
         compiler_params=params(),
-        cost_estimate=cost(25e9, 20e6),
+        cost_estimate=cost(10e9, 20e6),
         name="attn_bwd",
     )(*db_pieces, wo, near, far, q, k, v, lse, row, col, start_row, *tables)
 
@@ -414,7 +414,7 @@
     (routes_ref, wc_ref, wd_ref), refs = refs[:3], refs[3:]
     n_rows = 4 if by_hand else 2
     row_refs, refs = refs[:n_rows], refs[n_rows:]
-    (xs_ref, deout_ref, act_ref, dgate_ref, dup_ref, coef_ref), refs = refs[:6], refs[6:]
+    (xs_ref, deout_ref, act_ref, dgu_ref, coef_ref), refs = refs[:5], refs[5:]
     dcat, drow, yrow, refs = *refs[:3], refs[3:]
     step = pl.program_id(0)
     core = who_ref[1]
@@ -503,8 +503,8 @@
     dact = dot(deout_ref[...], wd_ref[...], NT)
     dgate = (dact * up * sig * (1.0 + gate * (1.0 - sig))).astype(bf16)
     dup = (dact * silu).astype(bf16)
-    dgate_ref[...] = dgate
-    dup_ref[...] = dup
+    dgu_ref[:, :ff] = dgate
+    dgu_ref[:, ff:] = dup
     dcat[:, :ff] = dgate
     dcat[:, ff : 2 * ff] = dup
     dcat[:, 2 * ff :] = coef
@@ -533,6 +533,7 @@
     other = pl.BlockSpec((1, 2, tok, out_w), lambda i, *_: (i // 2 + i % 2 * 2, 0, 0, 0))
     wide = pl.BlockSpec((rows, MODEL_WIDTH), lambda i, *_: (i, 0))
     thin = pl.BlockSpec((rows, ff), lambda i, *_: (i, 0))
+    twin = pl.BlockSpec((rows, 2 * ff), lambda i, *_: (i, 0))
     edge = pl.BlockSpec((rows, LANES), lambda i, *_: (i, 0))
     whole = pl.BlockSpec((2, tok, MODEL_WIDTH), lambda i, *_: (i, 0, 0))
     n_in = len(h_list)
@@ -552,15 +553,14 @@
         num_scalar_prefetch=1,
         grid=(steps,),
         in_specs=[ANY if by_hand else whole] * (2 * n_in) + [VMEM] * 3,
-        out_specs=row_specs + [wide] * 2 + [thin] * 3 + [edge],
+        out_specs=row_specs + [wide] * 2 + [thin, twin, edge],
         scratch_shapes=scratch,
     )
     return pl.pallas_call(
         functools.partial(expert_kernel, by_hand, cap),
         out_shape=[shape((steps, 2, tok, out_w), bf16)] * len(row_specs)
         + [shape((steps * rows, MODEL_WIDTH), bf16)] * 2
-        + [shape((steps * rows, ff), bf16)] * 3
-        + [shape((steps * rows, LANES), bf16)],
+        + [shape((steps * rows, w), bf16) for w in (ff, 2 * ff, LANES)],
         grid_spec=grid_spec,
         compiler_params=params(60),
         cost_estimate=cost(30e9, 30e6),
@@ -747,10 +747,11 @@
     )(places, *pieces)
 
 
-def columns_of(spots, near, far, qw, kw):
+def columns_of(spots, near, far, weights, qw, kw):
     n_ctx, part, width = near.shape
 
-    def kernel(spot_ref, near_ref, far_ref, *outs):
+    def kernel(spot_ref, near_ref, far_ref, *refs):
+        w_refs, outs, gain_ref = refs[:3], refs[3:6], refs[6]
         for k, ref in enumerate((near_ref, far_ref)):
             row = pl.multiple_of(spot_ref[n_ctx + k] * part, 16)
             for m in range(n_ctx):
@@ -760,16 +761,23 @@
                     col = pl.multiple_of(spot_ref[m] * w, LANES)
                     out[pl.ds(row, part), pl.ds(col, w)] = v[:, lo : lo + w]
                     lo += w
+        total = jnp.zeros((2 * part, LANES), f32)
+        for out, w_ref in zip(outs, w_refs):
+            both = out[...] * w_ref[...].astype(f32)
+            for c in range(0, both.shape[1], LANES):
+                total = total + both[:, c : c + LANES]
+        gain_ref[...] = jnp.sum(total, axis=1, keepdims=True)
 
     shape = jax.ShapeDtypeStruct
     return pl.pallas_call(
         kernel,
-        out_shape=tuple(shape((2 * part, n_ctx * w), f32) for w in (qw, kw, kw)),
-        in_specs=[SMEM, VMEM, VMEM],
-        out_specs=(VMEM,) * 3,
+        out_shape=tuple(shape((2 * part, n_ctx * w), f32) for w in (qw, kw, kw))
+        + (shape((2 * part, 1), f32),),
+        in_specs=[SMEM] + [VMEM] * 5,
+        out_specs=(VMEM,) * 4,
         cost_estimate=cost(0, 2e6),
         name="columns_of",
-    )(spots, near, far)
+    )(spots, near, far, *weights)
 
 
 def position_tables(lengths_row, row, freq):
@@ -810,22 +818,24 @@
     )(lengths_row, row, freq)
 
 
-def widen(gate, up, down):
-    def kernel(a_ref, b_ref, c_ref, a_out, b_out, c_out):
-        a_out[...] = a_ref[...].astype(f32)
-        b_out[...] = b_ref[...].astype(f32)
-        c_out[...] = c_ref[...].astype(f32).T
+def widen(twin, down):
+    rows, ff = down.shape
+
+    def kernel(twin_ref, down_ref, gate_out, up_out, down_out):
+        gate_out[...] = twin_ref[:, :ff].astype(f32)
+        up_out[...] = twin_ref[:, ff:].astype(f32)
+        down_out[...] = down_ref[...].astype(f32).T
 
     shape = jax.ShapeDtypeStruct
     return pl.pallas_call(
         kernel,
-        out_shape=(shape(gate.shape, f32), shape(up.shape, f32), shape(down.shape[::-1], f32)),
-        in_specs=[VMEM] * 3,
+        out_shape=(shape((rows, ff), f32), shape((rows, ff), f32), shape((ff, rows), f32)),
+        in_specs=[VMEM] * 2,
         out_specs=(VMEM,) * 3,
         compiler_params=params(),
         cost_estimate=cost(0, 0),
         name="widen",
-    )(gate, up, down)
+    )(twin, down)
 
 
 def finish_input(d_middle, near, far, x, gain):
@@ -1005,7 +1015,7 @@
         who, by_hand, h_list, dy_list, routes_all, w_cat, w_down[0], cap, tok
     )
     n_rows = 2 if by_hand else 1
-    d_rows, y_rows, (xs, deout, act, dgate, dup, coef) = (
+    d_rows, y_rows, (xs, deout, act, dgu, coef) = (
         out[:n_rows], out[n_rows : 2 * n_rows], out[2 * n_rows :],
     )
     small = small_plane()
@@ -1014,8 +1024,7 @@
         y_rows = (y_rows[0], after(y_rows[1], d_sum.far))
     y_sum = PlaneSum(y_rows)
     xs_late, deout_late = (after(xs, d_sum.far), after(deout, d_sum.far)) if small else (xs, deout)
-    g_gate = dot(xs_late, dgate, TN).astype(bf16)
-    g_up = dot(xs_late, dup, TN).astype(bf16)
+    g_twin = dot(xs_late, dgu, TN).astype(bf16)
     g_down = dot(deout_late, act, TN).astype(bf16)
     g_router = dot(xs_late, coef, TN)
     g_router = g_router[:, :experts] + g_router[:, LANES // 2 : LANES // 2 + experts]
@@ -1025,34 +1034,47 @@
 
     if small:
         d_sum.first()
-        sum_gate, sum_up, sum_down = over_dp(g_gate, 0), over_dp(g_up, 0), over_dp(g_down, 0)
-        d_sum.got2, y_sum.far, g_gate, g_up, g_down, g_router = sync(
-            d_sum.got2, y_sum.far, g_gate, g_up, g_down, g_router
+        sum_twin, sum_down = over_dp(g_twin, 0), over_dp(g_down, 0)
+        d_sum.got2, y_sum.far, g_twin, g_down, g_router = sync(
+            d_sum.got2, y_sum.far, g_twin, g_down, g_router
         )
         d_sum.second()
     else:
-        sum_gate, sum_up, sum_down = over_dp(g_gate, 0), over_dp(g_up, 0), over_dp(g_down, 0)
+        sum_twin, sum_down = over_dp(g_twin, 0), over_dp(g_down, 0)
     dh2 = d_sum.finish()
     dy = dy_own.astype(f32)
     d_norm, g_gain_b = rms_back(dh2, middle, r_b, gain_b)
     d_middle = dy + d_norm
+    tiny = jnp.concatenate([g_gain_b[None], g_router.T], axis=0)
+    tiny = tiny.reshape(-1, n_ctx * n_dp, rows).transpose(1, 0, 2)
     if small:
+        cy, cc = cx // 2, lax.rem(cx, 2)
+        tiny = tiny.reshape(2, 2, n_dp, -1, rows)
+        whole = lax.dynamic_index_in_dim(tiny, dx, 2, keepdims=False)
+        for up in range(1, n_dp):
+            sent = lax.dynamic_index_in_dim(tiny, lax.rem(dx + up, n_dp), 2, keepdims=False)
+            pairs = [(i, (i + up) % n_dp) for i in range(n_dp)]
+            whole = whole + lax.ppermute(sent, "dp", pairs)
+        tiny = whole
         b0 = d_middle.astype(bf16)
         b2, b1 = flip(b0, "context", 2), flip(b0, "context", 1)
-        b2, b1 = sync(b2, b1)
+        b2, b1, tiny = sync(b2, b1, tiny)
         db_pieces = [b0, b1, b2, flip(b2, "context", 1)]
         y_sum.far = after(y_sum.far, b2)
         y_sum.first()
     else:
         db_pieces = ctx_gather(d_middle.astype(bf16))
-    db_last = after(db_pieces[-1], sum_gate)
-
+    db_last = db_pieces[-1]
+    if small:
+        tiny_far = flip(tiny, "expert", 1)
     dqkv = attn_bwd(
         db_pieces[:-1] + [db_last], wo, near, far, q, k, v, lse, row, col, start_row, placed, qh, kvh
     )
-    dqkv, sum_up = sync(dqkv, sum_up)
-    attn = jnp.concatenate([near, after(far, dqkv)], axis=0).reshape(total, qw)
-    g_out = dot(attn, jnp.concatenate(db_pieces, axis=0), TN).astype(bf16)
+    if small:
+        dqkv, sum_twin, tiny_far = sync(dqkv, sum_twin, tiny_far)
+        tiny = tiny + tiny_far
+        give = lax.dynamic_index_in_dim(tiny, 1 - cc, 1, keepdims=False)
+        tiny_far = flip(give, "context", 1)
     dqkv_flat = dqkv.reshape(total, -1)
     h1_flat = h1.reshape(total, MODEL_WIDTH)
     g_qkv = dot(h1_flat, dqkv_flat, TN).astype(bf16)
@@ -1067,7 +1089,9 @@
     else:
         dh1_in = dqkv_flat
     dh1_part = dot(dh1_in, w_flat, NT).astype(bf16)
-    g_gain_a = jnp.sum(dh1_part.astype(f32) * h1_flat.astype(f32), axis=0) / gain_a[0]
+    attn = jnp.concatenate([near, after(far, dh1_part)], axis=0).reshape(total, qw)
+    g_out = dot(attn, jnp.concatenate(db_pieces, axis=0), TN).astype(bf16)
+    g_out = after(g_out, sum_down)
     dh1_part = dh1_part.reshape(n_ctx, tok, MODEL_WIDTH)
     r_a = lax.rsqrt(jnp.mean(x_own * x_own, axis=-1, keepdims=True) + NORM_EPS)
 
@@ -1081,15 +1105,9 @@
             back.append(flip(one, "context", m))
         return jnp.stack(back)
 
-    tiny = jnp.concatenate([g_gain_a[None], g_gain_b[None], g_router.T], axis=0)
 
     def finish_rows(dh1):
         return (d_middle + rms_back(dh1, x_own, r_a, gain_a)[0]).astype(bf16)
-
-    def spread(tiny):
-        tiny = tiny.reshape(-1, n_ctx * n_dp, rows).transpose(1, 0, 2)
-        tiny = lax.all_to_all(tiny, ("context", "dp"), split_axis=0, concat_axis=0, tiled=True)
-        return jnp.sum(tiny, axis=0)
 
     if small:
         h3 = flip(dh1_part[3], "context", 1)
@@ -1098,41 +1116,38 @@
         dh1 = dh1_part[0].astype(f32) + h1p.astype(f32)
         y_sum.got2 = after(y_sum.got2, dqkv)
         both_g = add_low(after(mine, dh1_part), got).reshape(n_ctx, n_dp, part, width)
-        sum_gate, sum_up, sum_down = widen(after(sum_gate, both_g), sum_up, sum_down)
+        tiny = lax.dynamic_index_in_dim(tiny, cc, 1, keepdims=False) + after(tiny_far, both_g)
+        give = lax.dynamic_index_in_dim(tiny, 1 - cy, 0, keepdims=False)
+        tiny_far = flip(give, "context", 2)
+        sum_gate, sum_up, sum_down = widen(after(sum_twin, both_g), sum_down)
         grad_input = finish_input(d_middle, after(dh1, both_g), hop, hidden[0], gain_a)
         y_sum.got2 = after(y_sum.got2, both_g)
         y_sum.second()
-        s_qkv = ring_sum(
+        s_qkv = direct_sum(
             lambda d: lax.dynamic_index_in_dim(both_g, d, 1, keepdims=False),
             "dp",
-            [(), (hop,), (y_sum.got1,)],
         )
-        tiny = after(tiny, both_g).reshape(-1, n_ctx * n_dp, rows).transpose(1, 0, 2)
-        tiny = (tiny + flip(tiny, "expert", 1)).reshape(2, 2, n_dp, -1, rows)
-        cy, cc = cx // 2, lax.rem(cx, 2)
-        give = lax.dynamic_index_in_dim(tiny, 1 - cy, 0, keepdims=False)
-        tiny = lax.dynamic_index_in_dim(tiny, cy, 0, keepdims=False) + flip(give, "context", 2)
-        give = lax.dynamic_index_in_dim(tiny, 1 - cc, 0, keepdims=False)
-        tiny = lax.dynamic_index_in_dim(tiny, cc, 0, keepdims=False) + flip(give, "context", 1)
         out_low = s_out.astype(bf16)
         out_far = flip(out_low, "expert", 1)
-        s_qkv, out_far, y_sum.got1, tiny = sync(s_qkv, out_far, y_sum.got1, tiny)
-        d_total = lax.dynamic_index_in_dim(tiny, dx, 0, keepdims=False)
-        for k in range(1, n_dp):
-            sent = lax.dynamic_index_in_dim(tiny, lax.rem(dx + k, n_dp), 0, keepdims=False)
-            d_total = d_total + lax.ppermute(sent, "dp", [(i, (i + k) % n_dp) for i in range(n_dp)])
-        tiny = d_total
-        output = (middle + y_sum.finish()).astype(bf16)
+        s_qkv, out_far, tiny_far = sync(s_qkv, out_far, tiny_far)
+        tiny = lax.dynamic_index_in_dim(tiny, cy, 0, keepdims=False) + tiny_far
         s_out = out_low.astype(f32) + out_far.astype(f32)
         near = exchange(s_qkv.astype(bf16))
+        near, y_sum.got1 = sync(near, y_sum.got1, hop)[:2]
+        output = (middle + y_sum.finish()).astype(bf16)
         far = flip(near, "expert", 1)
         spots = jnp.concatenate([c_of, ex[None], 1 - ex[None]]).astype(jnp.int32)
-        sum_q, sum_k, sum_v = columns_of(spots, near, far, qw, kw)
+        weights = (w_query, key_weight, value_weight)
+        sum_q, sum_k, sum_v, g_gain_a = columns_of(spots, near, far, weights, qw, kw)
+        g_gain_a = g_gain_a[:, 0] / attn_gain.astype(f32)
     else:
         dh1 = ctx_sum([dh1_part[m] for m in range(n_ctx)])
-        sum_gate, sum_up, sum_down = widen(sum_gate, sum_up, sum_down)
+        sum_gate, sum_up, sum_down = widen(sum_twin, sum_down)
         grad_input = finish_rows(dh1)
-        tiny = spread(lax.psum(tiny, "expert"))
+        tiny = lax.all_to_all(
+            lax.psum(tiny, "expert"), ("context", "dp"), split_axis=0, concat_axis=0, tiled=True
+        )
+        tiny = jnp.sum(tiny, axis=0)
         g4 = g_qkv.reshape(n_ctx, n_dp, rows, width)
         s_qkv = direct_sum(lambda d: lax.dynamic_index_in_dim(g4, d, 1, keepdims=False), "dp")
         s_qkv = lax.psum(s_qkv.astype(bf16), "expert")
@@ -1143,11 +1158,15 @@
             return back[:, :, lo:hi].transpose(1, 0, 2).reshape(rows, -1).astype(f32)
 
         sum_q, sum_k, sum_v = columns(0, qw), columns(qw, qw + kw), columns(qw + kw, width)
+        g_gain_a = sum(
+            jnp.sum(w.astype(f32) * g, axis=1)
+            for w, g in ((w_query, sum_q), (key_weight, sum_k), (value_weight, sum_v))
+        ) / attn_gain.astype(f32)
         output = (middle + y_sum.finish()).astype(bf16)
 
     return (
-        output[None], grad_input[None], tiny[0], sum_q, sum_k, sum_v, s_out,
-        tiny[1], tiny[2:].T, sum_gate[None], sum_up[None], sum_down[None],
+        output[None], grad_input[None], g_gain_a, sum_q, sum_k, sum_v, s_out,
+        tiny[0], tiny[1:].T, sum_gate[None], sum_up[None], sum_down[None],
     )
 
 

time: 400 us -> 393 us (0.983)
  waiting for transfers between devices: 128 us -> 124 us
    ppermute x6 -> x3, waiting for transfers between devices: 27.5 us -> 12.4 us  [step_up(): return lax.ppermute(v, axis, [(i, (i + 1) % n) for i in range(n)])]
    ppermute x3 -> x6, waiting for transfers between devices: 0.18 us -> 11.3 us  [the longest x3 5.79 us: body(): whole = whole + lax.ppermute(sent, 'dp', pairs)]
    ppermute x6 -> x3, starting transfers between devices: 6.65 us -> 0.71 us  [step_up(): return lax.ppermute(v, axis, [(i, (i + 1) % n) for i in range(n)])]
    ppermute x3 -> x6, starting transfers between devices: 4.12 us -> 10 us  [the longest x3 5.38 us: direct_sum(): got = lax.ppermute(sent, axis, [(i, (i + k) % n) for i in range(n)])]
    unnamed x111 -> x97, local copies, waits for them, and re-layouts: 7.21 us -> 11 us
    dot_general x9 -> x8, matrix products: 31.4 us -> 28.6 us  [dot(): return lax.dot_general(a, b, dims, preferred_element_type=f32)]
  transfers between devices with their start and end apart: 72 -> 71, of which waited for: 25 -> 27; matrix products, arithmetic and copies ran while one was open for 19% -> 18% of each run, Pallas kernels for 18% -> 18%
where the time goes in v4:
time: 393 us; the launch traced here: 387 us
  waiting for transfers between devices  124 us (32%)
  Pallas kernels  102 us (26%)
  starting transfers between devices  57.4 us (15%)
  other arithmetic  34.2 us (9%)
  matrix products  28.6 us (7%)
  local copies, waits for them, and re-layouts  25.9 us (7%)
  between operations  15.3 us (4%)
    ppermute x45, waiting for transfers between devices, flip(): return lax.ppermute(v, axis, [(i, i ^ bit) for i in range(n)])  57.6 us
    ppermute x10, waiting for transfers between devices, hop_plane(): return lax.ppermute(v, PLANE, pairs)  39.6 us
    pallas_call x1, Pallas kernels, run_experts(): pl.pallas_call(functools.partial(expert_kernel, by_hand, cap), out_shape=...  30.8 us
    ppermute x45, starting transfers between devices, flip(): return lax.ppermute(v, axis, [(i, i ^ bit) for i in range(n)])  29.6 us
    dot_general x8, matrix products, dot(): return lax.dot_general(a, b, dims, preferred_element_type=f32)  28.6 us
    pallas_call x1, Pallas kernels, attn_bwd(): pl.pallas_call(functools.partial(attn_bwd_kernel, n_ctx, qh, kvh), out_sh...  27.3 us
    pallas_call x1, Pallas kernels, attn_fwd(): pl.pallas_call(functools.partial(attn_fwd_kernel, n_ctx, n_w, qh, kvh), o...  24.4 us
    ppermute x3, waiting for transfers between devices, step_up(): return lax.ppermute(v, axis, [(i, (i + 1) % n) for i in range(n)])  12.4 us
  transfers between devices with their start and end apart: 71, of which 27 were waited for; matrix products, arithmetic and copies ran while one was open for 18% of the time, Pallas kernels for 18%

profile of v4, /device:TPU:0, one launch (start us, length us, event | category | flops | bytes accessed | tf_op | source)
XLA Modules:
  0.0 386.5 jit_solution(2171612321583395904)
XLA Ops:
  9.5 3.0 collective-permute-start.1
  12.6 1.7 collective-permute-start.4
  15.1 2.7 collective-permute-start.5
  17.8 1.3 collective-permute-start.6
  19.7 1.7 collective-permute-done.6
  21.8 1.4 collective-permute-start.9
  23.4 1.5 collective-permute-start.8
  25.7 1.4 collective-permute-start.12
  27.2 4.4 %collective-permute-done.7.refs_1_ = bf16[4,48,640]{2,1,0:T(8,128)(2,1)S(1)} collective-permute-done((bf16[4,48,640]{2,1,0:T(8,128)(2,1)S(1)}, bf16[4,48,640]{2,1,0:T(8,128)(2,1)S(1)}, u32[]{:S(2)}, u32[]{:S(2)}) %collective-permute-start.7) | collective-permute-done | bytes 245792 | tf_op jit(solution)/shard_map/ppermute | solution.py:578
  31.8 1.6 collective-permute-start.11
  33.9 8.0 %collective-permute-done.10.refs_2_ = bf16[4,48,640]{2,1,0:T(8,128)(2,1)S(1)} collective-permute-done((bf16[4,48,640]{2,1,0:T(8,128)(2,1)S(1)}, bf16[4,48,640]{2,1,0:T(8,128)(2,1)S(1)}, u32[]{:S(2)}, u32[]{:S(2)}) %collective-permute-start.10) | collective-permute-done | bytes 245792 | tf_op jit(solution)/shard_map/ppermute | solution.py:578
  43.2 1.4 collective-permute-start.20
  45.1 1.9 collective-permute-done.20
  50.6 2.9 position_tables.1
  57.5 6.6 %norm_rows.1.refs_8_ = bf16[4,256,1536]{2,1,0:T(8,128)(2,1)} custom-call(bf16[256,1536]{1,0:T(8,128)(2,1)} %bitcast.175, bf16[256,1536]{1,0:T(8,128)(2,1)} %collective-permute-done.18.refs_1_, bf16[256,1536]{1,0:T(8,128)(2,1)} %collective-permute-done.12.refs_2_, bf16[256,1536]{1,0:T(8,128)(2,1)} %collective-permute-done.19.refs_3_, ...), custom_call_target="tpu_custom_call" | custom-call | flops 7000000000 | bytes 6000000 | tf_op jit(solution)/shard_map/norm_rows/pallas_call | solution.py:81
  66.8 24.4 %attn_fwd.1 = (bf16[2,256,384]{2,1,0:T(8,128)(2,1)}, bf16[2,256,384]{2,1,0:T(8,128)(2,1)}, bf16[6,1024,128]{2,1,0:T(8,128)(2,1)}, bf16[2,1024,128]{2,1,0:T(8,128...) custom-call(s32[40]{0:T(128)} %pad_add_fusion.place_ref, ...), custom_call_target="tpu_custom_call" | custom-call | flops 20000000000 | bytes 20000000 | tf_op jit(solution)/shard_map/attn_fwd/pallas_call | solution.py:220
  91.2 2.4 convolution_convert_fusion.3
  97.4 1.9 collective-permute-start.25
  101.3 6.6 %concatenate.54.refs_17_ = bf16[1536,1152]{1,0:T(8,128)(2,1)} concatenate(bf16[1536,512]{1,0:T(8,128)(2,1)} %bitcast.180, bf16[1536,512]{1,0:T(8,128)(2,1)} %bitcast.181, bf16[1536,64]{1,0:T(8,128)(2,1)S(1)} %pad.9, bf16[1536,64]{1,0:T(8,128)(2,1)S(1)} %pad.9), dimensions={1} | concatenate | bytes 7077888 | tf_op jit(solution)/shard_map/concatenate | solution.py:1003
  107.9 9.9 %collective-permute-done.25 = bf16[256,1536]{1,0:T(8,128)(2,1)} collective-permute-done((bf16[256,1536]{1,0:T(8,128)(2,1)}, bf16[256,1536]{1,0:T(8,128)(2,1)}, u32[]{:S(2)}, u32[]{:S(2)}) %collective-permute-start.25) | collective-permute-done | bytes 786464 | tf_op jit(solution)/shard_map/ppermute | solution.py:573
  117.8 1.6 convert_add_fusion.3
  120.2 1.7 collective-permute-done.30
  122.0 1.8 collective-permute-start.31
  124.4 17.8 %collective-permute-done.31.refs_1_ = bf16[2,256,768]{2,1,0:T(8,128)(2,1)S(1)} collective-permute-done((bf16[2,256,768]{2,1,0:T(8,128)(2,1)S(1)}, bf16[2,256,768]{2,1,0:T(8,128)(2,1)S(1)}, u32[]{:S(2)}, u32[]{:S(2)}) %collective-permute-start.31) | collective-permute-done | bytes 786464 | tf_op jit(solution)/shard_map/ppermute | solution.py:653
  143.7 10.5 %collective-permute-done.33.refs_3_ = bf16[2,256,768]{2,1,0:T(8,128)(2,1)} collective-permute-done((bf16[2,256,768]{2,1,0:T(8,128)(2,1)S(1)}, bf16[2,256,768]{2,1,0:T(8,128)(2,1)}, u32[]{:S(2)}, u32[]{:S(2)}) %collective-permute-start.33) | collective-permute-done | bytes 786464 | tf_op jit(solution)/shard_map/ppermute | solution.py:653
  154.9 2.0 collective-permute-done.37.refs_7_
  156.9 30.8 %experts.1 = (bf16[4,2,256,768]{3,2,1,0:T(8,128)(2,1)}, bf16[4,2,256,768]{3,2,1,0:T(8,128)(2,1)}, bf16[4,2,256,768]{3,2,1,0:T(8,128)(2,1)}, bf16[4,2,256,768]{3,...) custom-call(s32[2]{0:T(128)} %pad_add_fusion.1.who_ref, ...), custom_call_target="tpu_custom_call" | custom-call | flops 30000001024 | bytes 30000000 | tf_op jit(solution)/shard_map/experts/pallas_call | solution.py:559
  187.9 5.7 %collective-permute-done.38 = bf16[4,2,256,768]{3,2,1,0:T(8,128)(2,1)S(1)} collective-permute-done((bf16[4,2,256,768]{3,2,1,0:T(8,128)(2,1)}, bf16[4,2,256,768]{3,2,1,0:T(8,128)(2,1)S(1)}, u32[]{:S(2)}, u32[]{:S(2)}) %collective-permute-start.38) | collective-permute-done | bytes 3145760 | tf_op jit(solution)/shard_map/ppermute | solution.py:573
  193.6 3.0 add_convert_fusion.1
  197.9 7.3 %convolution_convert_fusion.1 = bf16[1536,1024]{1,0:T(8,128)(2,1)} fusion(bf16[1152,1536]{1,0:T(8,128)(2,1)S(1)} %copy-done.2, bf16[1152,1024]{1,0:T(8,128)(2,1)} %get-tuple-element.164), kind=kOutput, calls=%fused_computation.5 | convolution fusion | flops 3625451520 | bytes 9043968 | tf_op jit(solution)/shard_map/dot_general | solution.py:38
  206.2 2.9 fusion.47
  209.6 3.4 convolution_convert_fusion.2
  213.0 3.6 add_convert_fusion
  217.4 2.4 convert_add_fusion.1
  219.9 1.6 collective-permute-start.41
  221.5 10.5 %collective-permute-done.41 = bf16[2,256,768]{2,1,0:T(8,128)(2,1)S(1)} collective-permute-done((bf16[2,256,768]{2,1,0:T(8,128)(2,1)S(1)}, bf16[2,256,768]{2,1,0:T(8,128)(2,1)S(1)}, u32[]{:S(2)}, u32[]{:S(2)}) %collective-permute-start.41) | collective-permute-done | bytes 786464 | tf_op jit(solution)/shard_map/ppermute | solution.py:653
  232.3 1.7 collective-permute-done.42
  235.3 1.7 fusion.43
  237.0 1.5 collective-permute-start.43
  239.2 3.6 collective-permute-start.46
  243.5 1.5 collective-permute-done.45
  245.8 3.5 collective-permute-done.47
  249.3 7.4 %collective-permute-done.43.refs_2_ = bf16[256,1536]{1,0:T(8,128)(2,1)} collective-permute-done((bf16[256,1536]{1,0:T(8,128)(2,1)S(1)}, bf16[256,1536]{1,0:T(8,128)(2,1)}, u32[]{:S(2)}, u32[]{:S(2)}) %collective-permute-start.43) | collective-permute-done | bytes 786464 | tf_op jit(solution)/shard_map/ppermute | solution.py:573
  260.1 27.3 %attn_bwd.1 = bf16[4,256,640]{2,1,0:T(8,128)(2,1)} custom-call(bf16[256,1536]{1,0:T(8,128)(2,1)} %copy-done.16, bf16[256,1536]{1,0:T(8,128)(2,1)} %collective-permute-done.44.refs_1_, bf16[256,1536]{1,0:T(8,128)(2,1)} %collective-permute-done.43.refs_2_, bf16[256,1536]{1,0:T(8,128)(2,1)} %copy-done.34, ...), custom_call_target="tpu_custom_call" | custom-call | flops 10000000000 | bytes 20000000 | tf_op jit(solution)/shard_map/attn_bwd/pallas_call | solution.py:368
  287.5 5.0 %bitcast_convert_fusion = bf16[1536,640]{1,0:T(8,128)(2,1)S(1)} fusion(bf16[4,256,1536]{2,1,0:T(8,128)(2,1)} %norm_rows.1.refs_8_, bf16[4,256,640]{2,1,0:T(8,128)(2,1)} %attn_bwd.1), kind=kOutput, calls=%fused_computation.3 | convolution fusion | flops 2014248960 | bytes 6422528 | tf_op jit(solution)/shard_map/dot_general | solution.py:38
  294.4 2.9 convolution_convert_fusion
  300.8 3.8 fusion.8
  305.0 1.5 collective-permute-start.51
  308.1 3.6 convert_add_fusion.2
  311.7 1.5 collective-permute-start.63
  313.2 15.5 %collective-permute-done.51 = bf16[16,48,640]{2,1,0:T(8,128)(2,1)} collective-permute-done((bf16[16,48,640]{2,1,0:T(8,128)(2,1)S(1)}, bf16[16,48,640]{2,1,0:T(8,128)(2,1)}, u32[]{:S(2)}, u32[]{:S(2)}) %collective-permute-start.51) | collective-permute-done | bytes 983072 | tf_op jit(solution)/shard_map/ppermute | solution.py:573
  328.7 1.4 add_convert_fusion.2
  331.0 1.4 collective-permute-start.52
  332.4 2.7 collective-permute-start.53
  336.4 2.4 convert_add_fusion
  338.8 1.7 copy-done
  341.8 2.8 widen.1
  345.5 5.5 %collective-permute-done.53 = bf16[4,48,640]{2,1,0:T(8,128)(2,1)} collective-permute-done((bf16[4,48,640]{2,1,0:T(8,128)(2,1)}, bf16[4,48,640]{2,1,0:T(8,128)(2,1)}, u32[]{:S(2)}, u32[]{:S(2)}) %collective-permute-start.53) | collective-permute-done | bytes 245792 | tf_op jit(solution)/shard_map/ppermute | solution.py:630
  351.0 1.5 collective-permute-start.61
  353.8 4.5 %finish_input.1 = bf16[256,1536]{1,0:T(8,128)(2,1)} custom-call(f32[256,1536]{1,0:T(8,128)} %get-tuple-element.213.dm_ref, f32[256,1536]{1,0:T(8,128)} %get-tuple-element.195.near_ref, bf16[256,1536]{1,0:T(8,128)(2,1)} %collective-permute-done.63.far_ref, bf16[256,1536]{1,0:T(8,128)(2,1)} %bitcast.176, f32[1,1536]{1,0:T(1,128)} %reshape.243.refs_4_.gain_ref), custom_call_target="tpu_custom_call" | custom-call | tf_op jit(solution)/shard_map/finish_input/pallas_call | solution.py:855
  361.8 3.2 collective-permute-done.59
  365.1 1.4 collective-permute-start.66
  368.1 5.5 %collective-permute-done.66.far_ref = bf16[4,48,640]{2,1,0:T(8,128)(2,1)} collective-permute-done((bf16[4,48,640]{2,1,0:T(8,128)(2,1)S(1)}, bf16[4,48,640]{2,1,0:T(8,128)(2,1)}, u32[]{:S(2)}, u32[]{:S(2)}) %collective-permute-start.66) | collective-permute-done | bytes 245792 | tf_op jit(solution)/shard_map/ppermute | solution.py:573
  373.6 2.3 columns_of.1
  (301 shorter events, 59.5 us)
Async XLA Ops:
  7.2 84.0 %all-gather.2.cloned.1.call-start = ((), (), s32[]{:S(2)}) async-start(), calls=%async_computation.3 | async-start | bytes 1474560 | tf_op jit(solution)/shard_map/all_gather | solution.py:930
  8.6 10.6 %collective-permute-start.3 = (bf16[256,768]{1,0:T(8,128)(2,1)S(1)}, bf16[256,768]{1,0:T(8,128)(2,1)S(1)}, u32[]{:S(2)}, u32[]{:S(2)}) collective-permute-start(bf16[256,768]{1,0:T(8,128)(2,1)S(1)} %get-tuple-element.232), channel_id=1, source_target_pairs={{0,4},{4,0},{8,12},{12,8},{1,5},{5,1},{9,13},{13,9},{2,6},{6,2},{1... | collective-permute-start | bytes 1179656 | tf_op jit(solution)/shard_map/ppermute | solution.py:573
  9.3 5.8 %collective-permute-start = (bf16[48,640]{1,0:T(8,128)(2,1)S(1)}, bf16[48,640]{1,0:T(8,128)(2,1)S(1)}, u32[]{:S(2)}, u32[]{:S(2)}) collective-permute-start(bf16[48,640]{1,0:T(8,128)(2,1)S(1)} %fusion.26), channel_id=1, source_target_pairs={{0,4},{4,0},{8,12},{12,8},{1,5},{5,1},{9,13},{13,9},{2,6},{6,2},{1... | collective-permute-start | bytes 184328 | tf_op jit(solution)/shard_map/ppermute | solution.py:573
  9.5 8.3 %collective-permute-start.1 = (bf16[48,640]{1,0:T(8,128)(2,1)S(1)}, bf16[48,640]{1,0:T(8,128)(2,1)S(1)}, u32[]{:S(2)}, u32[]{:S(2)}) collective-permute-start(bf16[48,640]{1,0:T(8,128)(2,1)S(1)} %fusion.24), channel_id=1, source_target_pairs={{0,8},{4,12},{8,0},{12,4},{1,9},{5,13},{9,1},{13,5},{2,10},{6,14},... | collective-permute-start | bytes 184328 | tf_op jit(solution)/shard_map/ppermute | solution.py:573
  12.5 6.7 %collective-permute-start.2 = (bf16[48,640]{1,0:T(8,128)(2,1)S(1)}, bf16[48,640]{1,0:T(8,128)(2,1)S(1)}, u32[]{:S(2)}, u32[]{:S(2)}) collective-permute-start(bf16[48,640]{1,0:T(8,128)(2,1)S(1)} %fusion.22), channel_id=1, source_target_pairs={{0,12},{4,8},{8,4},{12,0},{1,13},{5,9},{9,5},{13,1},{2,14},{6,10},... | collective-permute-start | bytes 184328 | tf_op jit(solution)/shard_map/ppermute | solution.py:573
  12.6 6.7 %collective-permute-start.4 = (bf16[10,256]{1,0:T(8,128)(2,1)S(1)}, bf16[10,256]{1,0:T(8,128)(2,1)S(1)}, u32[]{:S(2)}, u32[]{:S(2)}) collective-permute-start(bf16[10,256]{1,0:T(8,128)(2,1)S(1)} %fusion.36), channel_id=1, source_target_pairs={{0,1},{1,2},{2,3},{3,0},{4,5},{5,6},{6,7},{7,4},{8,9},{9,10},{10,1... | collective-permute-start | bytes 15368 | tf_op jit(solution)/shard_map/ppermute | solution.py:607
  15.1 4.6 %collective-permute-start.5 = (bf16[10,256]{1,0:T(8,128)(2,1)S(1)}, bf16[10,256]{1,0:T(8,128)(2,1)S(1)}, u32[]{:S(2)}, u32[]{:S(2)}) collective-permute-start(bf16[10,256]{1,0:T(8,128)(2,1)S(1)} %fusion.36), channel_id=1, source_target_pairs={{0,2},{1,3},{2,0},{3,1},{4,6},{5,7},{6,4},{7,5},{8,10},{9,11},{10,... | collective-permute-start | bytes 15368 | tf_op jit(solution)/shard_map/ppermute | solution.py:607
  17.8 3.7 collective-permute-start.6
  19.1 38.3 %collective-permute-start.18 = (bf16[256,1536]{1,0:T(8,128)(2,1)S(1)}, bf16[256,1536]{1,0:T(8,128)(2,1)}, u32[]{:S(2)}, u32[]{:S(2)}) collective-permute-start(bf16[256,1536]{1,0:T(8,128)(2,1)S(1)} %bitcast.177), channel_id=1, source_target_pairs={{0,4},{4,0},{8,12},{12,8},{1,5},{5,1},{9,13},{13,9},{2,6},{6,2},{1... | collective-permute-start | bytes 2359304 | tf_op jit(solution)/shard_map/ppermute | solution.py:573
  21.8 3.9 %collective-permute-start.9 = (bf16[44,256]{1,0:T(8,128)(2,1)S(1)}, bf16[44,256]{1,0:T(8,128)(2,1)S(1)}, u32[]{:S(2)}, u32[]{:S(2)}) collective-permute-start(bf16[44,256]{1,0:T(8,128)(2,1)S(1)} %concatenate.53), channel_id=1, source_target_pairs={{0,8},{4,12},{8,0},{12,4},{1,9},{5,13},{9,1},{13,5},{2,10},{6,14},... | collective-permute-start | bytes 67592 | tf_op jit(solution)/shard_map/ppermute | solution.py:573
  23.2 8.4 %collective-permute-start.7 = (bf16[4,48,640]{2,1,0:T(8,128)(2,1)S(1)}, bf16[4,48,640]{2,1,0:T(8,128)(2,1)S(1)}, u32[]{:S(2)}, u32[]{:S(2)}) collective-permute-start(bf16[4,48,640]{2,1,0:T(8,128)(2,1)S(1)} %pad_maximum_fusion.4.refs_0_), channel_id=1, source_target_pairs={{0,1},{1,2},{2,3},{3,0},{4,5},{5,6},{6,7},{7,4},{8,9},{9,10},{10,1... | collective-permute-start | bytes 737288 | tf_op jit(solution)/shard_map/ppermute | solution.py:578
  23.4 8.2 %collective-permute-start.8 = (bf16[4,48,640]{2,1,0:T(8,128)(2,1)S(1)}, bf16[4,48,640]{2,1,0:T(8,128)(2,1)S(1)}, u32[]{:S(2)}, u32[]{:S(2)}) collective-permute-start(bf16[4,48,640]{2,1,0:T(8,128)(2,1)S(1)} %pad_maximum_fusion.4.refs_0_), channel_id=1, source_target_pairs={{0,16},{16,0},{1,17},{17,1},{2,18},{18,2},{3,19},{19,3},{4,20},{20... | collective-permute-start | bytes 737288 | tf_op jit(solution)/shard_map/ppermute | solution.py:573
  25.7 17.5 %collective-permute-start.12 = (bf16[256,1536]{1,0:T(8,128)(2,1)S(1)}, bf16[256,1536]{1,0:T(8,128)(2,1)}, u32[]{:S(2)}, u32[]{:S(2)}) collective-permute-start(bf16[256,1536]{1,0:T(8,128)(2,1)S(1)} %bitcast.178), channel_id=1, source_target_pairs={{0,8},{4,12},{8,0},{12,4},{1,9},{5,13},{9,1},{13,5},{2,10},{6,14},... | collective-permute-start | bytes 2359304 | tf_op jit(solution)/shard_map/ppermute | solution.py:573
  31.7 10.1 %collective-permute-start.10 = (bf16[4,48,640]{2,1,0:T(8,128)(2,1)S(1)}, bf16[4,48,640]{2,1,0:T(8,128)(2,1)S(1)}, u32[]{:S(2)}, u32[]{:S(2)}) collective-permute-start(bf16[4,48,640]{2,1,0:T(8,128)(2,1)S(1)} %collective-permute-done.7.refs_1_), channel_id=1, source_target_pairs={{0,1},{1,2},{2,3},{3,0},{4,5},{5,6},{6,7},{7,4},{8,9},{9,10},{10,1... | collective-permute-start | bytes 737288 | tf_op jit(solution)/shard_map/ppermute | solution.py:578
  31.8 10.1 %collective-permute-start.11 = (bf16[4,48,640]{2,1,0:T(8,128)(2,1)S(1)}, bf16[4,48,640]{2,1,0:T(8,128)(2,1)S(1)}, u32[]{:S(2)}, u32[]{:S(2)}) collective-permute-start(bf16[4,48,640]{2,1,0:T(8,128)(2,1)S(1)} %collective-permute-done.7.refs_1_), channel_id=1, source_target_pairs={{0,16},{16,0},{1,17},{17,1},{2,18},{18,2},{3,19},{19,3},{4,20},{20... | collective-permute-start | bytes 737288 | tf_op jit(solution)/shard_map/ppermute | solution.py:573
  33.3 23.1 %collective-permute-start.16 = (bf16[2,256,768]{2,1,0:T(8,128)(2,1)S(1)}, bf16[2,256,768]{2,1,0:T(8,128)(2,1)}, u32[]{:S(2)}, u32[]{:S(2)}) collective-permute-start(bf16[2,256,768]{2,1,0:T(8,128)(2,1)S(1)} %pad_maximum_fusion.1.refs_8_), channel_id=1, source_target_pairs={{0,8},{4,20},{8,0},{12,28},{16,24},{20,4},{24,16},{28,12},{1,9},{5... | collective-permute-start | bytes 2359304 | tf_op jit(solution)/shard_map/ppermute | solution.py:653
  43.1 14.3 %collective-permute-start.19 = (bf16[256,1536]{1,0:T(8,128)(2,1)}, bf16[256,1536]{1,0:T(8,128)(2,1)}, u32[]{:S(2)}, u32[]{:S(2)}) collective-permute-start(bf16[256,1536]{1,0:T(8,128)(2,1)} %collective-permute-done.12.refs_2_), channel_id=1, source_target_pairs={{0,4},{4,0},{8,12},{12,8},{1,5},{5,1},{9,13},{13,9},{2,6},{6,2},{1... | collective-permute-start | bytes 2359304 | tf_op jit(solution)/shard_map/ppermute | solution.py:573
  43.2 3.9 %collective-permute-start.20 = (bf16[4,4,256]{2,1,0:T(4,128)(2,1)S(1)}, bf16[4,4,256]{2,1,0:T(4,128)(2,1)S(1)}, u32[]{:S(2)}, u32[]{:S(2)}) collective-permute-start(bf16[4,4,256]{2,1,0:T(4,128)(2,1)S(1)} %get-tuple-element.242), channel_id=1, source_target_pairs={{0,16},{16,0},{1,17},{17,1},{2,18},{18,2},{3,19},{19,3},{4,20},{20... | collective-permute-start | bytes 24584 | tf_op jit(solution)/shard_map/ppermute | solution.py:573
  44.7 11.8 %collective-permute-start.14 = (bf16[4,48,640]{2,1,0:T(8,128)(2,1)S(1)}, bf16[4,48,640]{2,1,0:T(8,128)(2,1)}, u32[]{:S(2)}, u32[]{:S(2)}) collective-permute-start(bf16[4,48,640]{2,1,0:T(8,128)(2,1)S(1)} %collective-permute-done.10.refs_2_), channel_id=1, source_target_pairs={{0,1},{1,2},{2,3},{3,0},{4,5},{5,6},{6,7},{7,4},{8,9},{9,10},{10,1... | collective-permute-start | bytes 737288 | tf_op jit(solution)/shard_map/ppermute | solution.py:578
  47.0 9.4 %collective-permute-start.15 = (bf16[4,48,640]{2,1,0:T(8,128)(2,1)S(1)}, bf16[4,48,640]{2,1,0:T(8,128)(2,1)}, u32[]{:S(2)}, u32[]{:S(2)}) collective-permute-start(bf16[4,48,640]{2,1,0:T(8,128)(2,1)S(1)} %collective-permute-done.10.refs_2_), channel_id=1, source_target_pairs={{0,16},{16,0},{1,17},{17,1},{2,18},{18,2},{3,19},{19,3},{4,20},{20... | collective-permute-start | bytes 737288 | tf_op jit(solution)/shard_map/ppermute | solution.py:573
  56.5 8.3 %collective-permute-start.17 = (bf16[4,48,640]{2,1,0:T(8,128)(2,1)}, bf16[4,48,640]{2,1,0:T(8,128)(2,1)S(1)}, u32[]{:S(2)}, u32[]{:S(2)}) collective-permute-start(bf16[4,48,640]{2,1,0:T(8,128)(2,1)} %collective-permute-done.14.refs_3_), channel_id=1, source_target_pairs={{0,16},{16,0},{1,17},{17,1},{2,18},{18,2},{3,19},{19,3},{4,20},{20... | collective-permute-start | bytes 737288 | tf_op jit(solution)/shard_map/ppermute | solution.py:573
  57.2 230.2 %reduce-scatter.4.cloned.1.call-start = ((), (), s32[]{:S(2)}) async-start(), calls=%async_computation.4 | async-start | bytes 3932160 | tf_op jit(solution)/shard_map/reduce_scatter | solution.py:1033
  64.8 26.4 %collective-permute-start.21 = (bf16[2,256,768]{2,1,0:T(8,128)(2,1)S(1)}, bf16[2,256,768]{2,1,0:T(8,128)(2,1)}, u32[]{:S(2)}, u32[]{:S(2)}) collective-permute-start(bf16[2,256,768]{2,1,0:T(8,128)(2,1)S(1)} %pad_maximum_fusion.1.refs_8_), channel_id=1, source_target_pairs={{0,16},{4,12},{8,24},{12,4},{16,0},{20,28},{24,8},{28,20},{1,17},{... | collective-permute-start | bytes 2359304 | tf_op jit(solution)/shard_map/ppermute | solution.py:653
  65.6 25.6 %collective-permute-start.22 = (bf16[2,256,768]{2,1,0:T(8,128)(2,1)}, bf16[2,256,768]{2,1,0:T(8,128)(2,1)}, u32[]{:S(2)}, u32[]{:S(2)}) collective-permute-start(bf16[2,256,768]{2,1,0:T(8,128)(2,1)} %collective-permute-done.16.refs_9_), channel_id=1, source_target_pairs={{0,16},{4,12},{8,24},{12,4},{16,0},{20,28},{24,8},{28,20},{1,17},{... | collective-permute-start | bytes 2359304 | tf_op jit(solution)/shard_map/ppermute | solution.py:653
  96.0 4.0 %collective-permute-start.23 = (bf16[256,1536]{1,0:T(8,128)(2,1)S(1)}, bf16[256,1536]{1,0:T(8,128)(2,1)S(1)}, u32[]{:S(2)}, u32[]{:S(2)}) collective-permute-start(bf16[256,1536]{1,0:T(8,128)(2,1)S(1)} %slice.203), channel_id=1, source_target_pairs={{0,4},{4,0},{8,12},{12,8},{1,5},{5,1},{9,13},{13,9},{2,6},{6,2},{1... | collective-permute-start | bytes 2359304 | tf_op jit(solution)/shard_map/ppermute | solution.py:573
  97.4 20.4 %collective-permute-start.25 = (bf16[256,1536]{1,0:T(8,128)(2,1)}, bf16[256,1536]{1,0:T(8,128)(2,1)}, u32[]{:S(2)}, u32[]{:S(2)}) collective-permute-start(bf16[256,1536]{1,0:T(8,128)(2,1)} %add_convert_fusion.4), channel_id=1, source_target_pairs={{0,8},{4,12},{8,0},{12,4},{1,9},{5,13},{9,1},{13,5},{2,10},{6,14},... | collective-permute-start | bytes 2359304 | tf_op jit(solution)/shard_map/ppermute | solution.py:573
  99.3 20.2 %collective-permute-start.26 = (bf16[2,256,768]{2,1,0:T(8,128)(2,1)S(1)}, bf16[2,256,768]{2,1,0:T(8,128)(2,1)}, u32[]{:S(2)}, u32[]{:S(2)}) collective-permute-start(bf16[2,256,768]{2,1,0:T(8,128)(2,1)S(1)} %copy-done.19), channel_id=1, source_target_pairs={{0,4},{4,0},{8,12},{12,8},{1,5},{5,1},{9,13},{13,9},{2,6},{6,2},{1... | collective-permute-start | bytes 2359304 | tf_op jit(solution)/shard_map/ppermute | solution.py:573
  99.5 20.0 %collective-permute-start.27 = (bf16[2,256,768]{2,1,0:T(8,128)(2,1)}, bf16[2,256,768]{2,1,0:T(8,128)(2,1)}, u32[]{:S(2)}, u32[]{:S(2)}) collective-permute-start(bf16[2,256,768]{2,1,0:T(8,128)(2,1)} %collective-permute-done.16.refs_9_), channel_id=1, source_target_pairs={{0,4},{4,0},{8,12},{12,8},{1,5},{5,1},{9,13},{13,9},{2,6},{6,2},{1... | collective-permute-start | bytes 2359304 | tf_op jit(solution)/shard_map/ppermute | solution.py:573
  99.8 19.7 %collective-permute-start.28 = (bf16[2,256,768]{2,1,0:T(8,128)(2,1)}, bf16[2,256,768]{2,1,0:T(8,128)(2,1)}, u32[]{:S(2)}, u32[]{:S(2)}) collective-permute-start(bf16[2,256,768]{2,1,0:T(8,128)(2,1)} %collective-permute-done.21.refs_10_), channel_id=1, source_target_pairs={{0,4},{4,0},{8,12},{12,8},{1,5},{5,1},{9,13},{13,9},{2,6},{6,2},{1... | collective-permute-start | bytes 2359304 | tf_op jit(solution)/shard_map/ppermute | solution.py:573
  100.9 18.6 %collective-permute-start.29 = (bf16[2,256,768]{2,1,0:T(8,128)(2,1)}, bf16[2,256,768]{2,1,0:T(8,128)(2,1)}, u32[]{:S(2)}, u32[]{:S(2)}) collective-permute-start(bf16[2,256,768]{2,1,0:T(8,128)(2,1)} %collective-permute-done.22.refs_11_), channel_id=1, source_target_pairs={{0,4},{4,0},{8,12},{12,8},{1,5},{5,1},{9,13},{13,9},{2,6},{6,2},{1... | collective-permute-start | bytes 2359304 | tf_op jit(solution)/shard_map/ppermute | solution.py:573
  122.0 20.2 %collective-permute-start.31 = (bf16[2,256,768]{2,1,0:T(8,128)(2,1)S(1)}, bf16[2,256,768]{2,1,0:T(8,128)(2,1)S(1)}, u32[]{:S(2)}, u32[]{:S(2)}) collective-permute-start(bf16[2,256,768]{2,1,0:T(8,128)(2,1)S(1)} %pad_maximum_fusion.2.refs_0_), channel_id=1, source_target_pairs={{0,8},{4,20},{8,0},{12,28},{16,24},{20,4},{24,16},{28,12},{1,9},{5... | collective-permute-start | bytes 2359304 | tf_op jit(solution)/shard_map/ppermute | solution.py:653
  123.8 20.0 %collective-permute-start.32 = (bf16[2,256,768]{2,1,0:T(8,128)(2,1)S(1)}, bf16[2,256,768]{2,1,0:T(8,128)(2,1)}, u32[]{:S(2)}, u32[]{:S(2)}) collective-permute-start(bf16[2,256,768]{2,1,0:T(8,128)(2,1)S(1)} %pad_maximum_fusion.2.refs_0_), channel_id=1, source_target_pairs={{0,16},{4,12},{8,24},{12,4},{16,0},{20,28},{24,8},{28,20},{1,17},{... | collective-permute-start | bytes 2359304 | tf_op jit(solution)/shard_map/ppermute | solution.py:653
  142.2 12.1 %collective-permute-start.33 = (bf16[2,256,768]{2,1,0:T(8,128)(2,1)S(1)}, bf16[2,256,768]{2,1,0:T(8,128)(2,1)}, u32[]{:S(2)}, u32[]{:S(2)}) collective-permute-start(bf16[2,256,768]{2,1,0:T(8,128)(2,1)S(1)} %collective-permute-done.31.refs_1_), channel_id=1, source_target_pairs={{0,16},{4,12},{8,24},{12,4},{16,0},{20,28},{24,8},{28,20},{1,17},{... | collective-permute-start | bytes 2359304 | tf_op jit(solution)/shard_map/ppermute | solution.py:653
  143.2 11.7 %collective-permute-start.34 = (bf16[2,256,768]{2,1,0:T(8,128)(2,1)S(1)}, bf16[2,256,768]{2,1,0:T(8,128)(2,1)}, u32[]{:S(2)}, u32[]{:S(2)}) collective-permute-start(bf16[2,256,768]{2,1,0:T(8,128)(2,1)S(1)} %pad_maximum_fusion.2.refs_0_), channel_id=1, source_target_pairs={{0,4},{4,0},{8,12},{12,8},{1,5},{5,1},{9,13},{13,9},{2,6},{6,2},{1... | collective-permute-start | bytes 2359304 | tf_op jit(solution)/shard_map/ppermute | solution.py:573
  143.2 11.7 %collective-permute-start.35 = (bf16[2,256,768]{2,1,0:T(8,128)(2,1)S(1)}, bf16[2,256,768]{2,1,0:T(8,128)(2,1)}, u32[]{:S(2)}, u32[]{:S(2)}) collective-permute-start(bf16[2,256,768]{2,1,0:T(8,128)(2,1)S(1)} %collective-permute-done.31.refs_1_), channel_id=1, source_target_pairs={{0,4},{4,0},{8,12},{12,8},{1,5},{5,1},{9,13},{13,9},{2,6},{6,2},{1... | collective-permute-start | bytes 2359304 | tf_op jit(solution)/shard_map/ppermute | solution.py:573
  143.7 11.2 %collective-permute-start.36 = (bf16[2,256,768]{2,1,0:T(8,128)(2,1)}, bf16[2,256,768]{2,1,0:T(8,128)(2,1)}, u32[]{:S(2)}, u32[]{:S(2)}) collective-permute-start(bf16[2,256,768]{2,1,0:T(8,128)(2,1)} %collective-permute-done.32.refs_2_), channel_id=1, source_target_pairs={{0,4},{4,0},{8,12},{12,8},{1,5},{5,1},{9,13},{13,9},{2,6},{6,2},{1... | collective-permute-start | bytes 2359304 | tf_op jit(solution)/shard_map/ppermute | solution.py:573
  187.7 5.9 %collective-permute-start.38 = (bf16[4,2,256,768]{3,2,1,0:T(8,128)(2,1)}, bf16[4,2,256,768]{3,2,1,0:T(8,128)(2,1)S(1)}, u32[]{:S(2)}, u32[]{:S(2)}) collective-permute-start(bf16[4,2,256,768]{3,2,1,0:T(8,128)(2,1)} %get-tuple-element.160), channel_id=1, source_target_pairs={{0,4},{4,0},{8,12},{12,8},{1,5},{5,1},{9,13},{13,9},{2,6},{6,2},{1... | collective-permute-start | bytes 9437192 | tf_op jit(solution)/shard_map/ppermute | solution.py:573
  196.7 16.3 %collective-permute-start.39 = (bf16[4,2,256,768]{3,2,1,0:T(8,128)(2,1)}, bf16[4,2,256,768]{3,2,1,0:T(8,128)(2,1)}, u32[]{:S(2)}, u32[]{:S(2)}) collective-permute-start(bf16[4,2,256,768]{3,2,1,0:T(8,128)(2,1)} %get-tuple-element.161), channel_id=1, source_target_pairs={{0,4},{4,0},{8,12},{12,8},{1,5},{5,1},{9,13},{13,9},{2,6},{6,2},{1... | collective-permute-start | bytes 9437192 | tf_op jit(solution)/shard_map/ppermute | solution.py:573
  196.9 20.5 %collective-permute-start.40 = (bf16[2,2,256,768]{3,2,1,0:T(8,128)(2,1)S(1)}, bf16[2,2,256,768]{3,2,1,0:T(8,128)(2,1)}, u32[]{:S(2)}, u32[]{:S(2)}) collective-permute-start(bf16[2,2,256,768]{3,2,1,0:T(8,128)(2,1)S(1)} %add_convert_fusion.1), channel_id=1, source_target_pairs={{0,16},{4,12},{8,24},{12,4},{16,0},{20,28},{24,8},{28,20},{1,17},{... | collective-permute-start | bytes 4718600 | tf_op jit(solution)/shard_map/ppermute | solution.py:653
  205.3 99.7 %reduce-scatter.6.cloned.1.call-start = ((), (), s32[]{:S(2)}) async-start(), calls=%async_computation.5 | async-start | bytes 1966080 | tf_op jit(solution)/shard_map/reduce_scatter | solution.py:1033
  219.9 12.1 %collective-permute-start.41 = (bf16[2,256,768]{2,1,0:T(8,128)(2,1)S(1)}, bf16[2,256,768]{2,1,0:T(8,128)(2,1)S(1)}, u32[]{:S(2)}, u32[]{:S(2)}) collective-permute-start(bf16[2,256,768]{2,1,0:T(8,128)(2,1)S(1)} %fusion.15), channel_id=1, source_target_pairs={{0,8},{4,20},{8,0},{12,28},{16,24},{20,4},{24,16},{28,12},{1,9},{5... | collective-permute-start | bytes 2359304 | tf_op jit(solution)/shard_map/ppermute | solution.py:653
  237.0 19.7 %collective-permute-start.43 = (bf16[256,1536]{1,0:T(8,128)(2,1)S(1)}, bf16[256,1536]{1,0:T(8,128)(2,1)}, u32[]{:S(2)}, u32[]{:S(2)}) collective-permute-start(bf16[256,1536]{1,0:T(8,128)(2,1)S(1)} %get-tuple-element.212.refs_0_), channel_id=1, source_target_pairs={{0,8},{4,12},{8,0},{12,4},{1,9},{5,13},{9,1},{13,5},{2,10},{6,14},... | collective-permute-start | bytes 2359304 | tf_op jit(solution)/shard_map/ppermute | solution.py:573
  238.6 18.2 %collective-permute-start.44 = (bf16[256,1536]{1,0:T(8,128)(2,1)S(1)}, bf16[256,1536]{1,0:T(8,128)(2,1)}, u32[]{:S(2)}, u32[]{:S(2)}) collective-permute-start(bf16[256,1536]{1,0:T(8,128)(2,1)S(1)} %get-tuple-element.212.refs_0_), channel_id=1, source_target_pairs={{0,4},{4,0},{8,12},{12,8},{1,5},{5,1},{9,13},{13,9},{2,6},{6,2},{1... | collective-permute-start | bytes 2359304 | tf_op jit(solution)/shard_map/ppermute | solution.py:573
  238.8 6.2 %collective-permute-start.45 = (f32[2,2,9,96]{3,1,2,0:T(2,128)S(1)}, f32[2,2,9,96]{3,1,2,0:T(2,128)S(1)}, u32[]{:S(2)}, u32[]{:S(2)}) collective-permute-start(f32[2,2,9,96]{3,1,2,0:T(2,128)S(1)} %bitcast.210), channel_id=1, source_target_pairs={{0,1},{1,2},{2,3},{3,0},{4,5},{5,6},{6,7},{7,4},{8,9},{9,10},{10,1... | collective-permute-start | bytes 41480 | tf_op jit(solution)/shard_map/ppermute | solution.py:1057
  239.2 6.5 %collective-permute-start.46 = (f32[2,2,9,96]{3,1,2,0:T(2,128)S(1)}, f32[2,2,9,96]{3,1,2,0:T(2,128)S(1)}, u32[]{:S(2)}, u32[]{:S(2)}) collective-permute-start(f32[2,2,9,96]{3,1,2,0:T(2,128)S(1)} %bitcast.211), channel_id=1, source_target_pairs={{0,2},{1,3},{2,0},{3,1},{4,6},{5,7},{6,4},{7,5},{8,10},{9,11},{10,... | collective-permute-start | bytes 41480 | tf_op jit(solution)/shard_map/ppermute | solution.py:1057
  242.9 6.4 %collective-permute-start.47 = (f32[2,2,9,96]{3,1,2,0:T(2,128)S(1)}, f32[2,2,9,96]{3,1,2,0:T(2,128)S(1)}, u32[]{:S(2)}, u32[]{:S(2)}) collective-permute-start(f32[2,2,9,96]{3,1,2,0:T(2,128)S(1)} %bitcast.212), channel_id=1, source_target_pairs={{0,3},{1,0},{2,1},{3,2},{4,7},{5,4},{6,5},{7,6},{8,11},{9,8},{10,9... | collective-permute-start | bytes 41480 | tf_op jit(solution)/shard_map/ppermute | solution.py:1057
  256.7 83.9 %reduce-scatter.8.cloned.1.call-start = ((), (), s32[]{:S(2)}) async-start(), calls=%async_computation.6 | async-start | bytes 1474560 | tf_op jit(solution)/shard_map/reduce_scatter | solution.py:1099
  256.8 30.6 %collective-permute-start.50 = (f32[2,2,9,96]{3,1,2,0:T(2,128)S(1)}, f32[2,2,9,96]{3,1,2,0:T(2,128)}, u32[]{:S(2)}, u32[]{:S(2)}) collective-permute-start(f32[2,2,9,96]{3,1,2,0:T(2,128)S(1)} %fusion.31), channel_id=1, source_target_pairs={{0,16},{16,0},{1,17},{17,1},{2,18},{18,2},{3,19},{19,3},{4,20},{20... | collective-permute-start | bytes 41480 | tf_op jit(solution)/shard_map/ppermute | solution.py:573
  257.9 50.1 %collective-permute-start.48 = (bf16[2,2,256,768]{3,2,1,0:T(8,128)(2,1)}, bf16[2,2,256,768]{3,2,1,0:T(8,128)(2,1)}, u32[]{:S(2)}, u32[]{:S(2)}) collective-permute-start(bf16[2,2,256,768]{3,2,1,0:T(8,128)(2,1)} %add_convert_fusion), channel_id=1, source_target_pairs={{0,16},{4,12},{8,24},{12,4},{16,0},{20,28},{24,8},{28,20},{1,17},{... | collective-permute-start | bytes 4718600 | tf_op jit(solution)/shard_map/ppermute | solution.py:653
  299.4 8.6 %collective-permute-start.62 = (bf16[256,1536]{1,0:T(8,128)(2,1)}, bf16[256,1536]{1,0:T(8,128)(2,1)}, u32[]{:S(2)}, u32[]{:S(2)}) collective-permute-start(bf16[256,1536]{1,0:T(8,128)(2,1)} %get-tuple-element.219), channel_id=1, source_target_pairs={{0,4},{4,0},{8,12},{12,8},{1,5},{5,1},{9,13},{13,9},{2,6},{6,2},{1... | collective-permute-start | bytes 2359304 | tf_op jit(solution)/shard_map/ppermute | solution.py:573
  299.6 8.5 %collective-permute-start.65 = (bf16[256,1536]{1,0:T(8,128)(2,1)}, bf16[256,1536]{1,0:T(8,128)(2,1)}, u32[]{:S(2)}, u32[]{:S(2)}) collective-permute-start(bf16[256,1536]{1,0:T(8,128)(2,1)} %get-tuple-element.218), channel_id=1, source_target_pairs={{0,4},{4,0},{8,12},{12,8},{1,5},{5,1},{9,13},{13,9},{2,6},{6,2},{1... | collective-permute-start | bytes 2359304 | tf_op jit(solution)/shard_map/ppermute | solution.py:573
  305.0 23.6 %collective-permute-start.51 = (bf16[16,48,640]{2,1,0:T(8,128)(2,1)S(1)}, bf16[16,48,640]{2,1,0:T(8,128)(2,1)}, u32[]{:S(2)}, u32[]{:S(2)}) collective-permute-start(bf16[16,48,640]{2,1,0:T(8,128)(2,1)S(1)} %get-tuple-element.223), channel_id=1, source_target_pairs={{0,16},{16,0},{1,17},{17,1},{2,18},{18,2},{3,19},{19,3},{4,20},{20... | collective-permute-start | bytes 2949128 | tf_op jit(solution)/shard_map/ppermute | solution.py:573
  308.0 22.1 %collective-permute-start.56 = (f32[2,9,96]{2,0,1:T(2,128)S(1)}, f32[2,9,96]{2,0,1:T(2,128)S(1)}, u32[]{:S(2)}, u32[]{:S(2)}) collective-permute-start(f32[2,9,96]{2,0,1:T(2,128)S(1)} %bitcast.214), channel_id=1, source_target_pairs={{0,4},{4,0},{8,12},{12,8},{1,5},{5,1},{9,13},{13,9},{2,6},{6,2},{1... | collective-permute-start | bytes 20744 | tf_op jit(solution)/shard_map/ppermute | solution.py:573
  311.7 42.1 %collective-permute-start.63 = (bf16[256,1536]{1,0:T(8,128)(2,1)}, bf16[256,1536]{1,0:T(8,128)(2,1)}, u32[]{:S(2)}, u32[]{:S(2)}) collective-permute-start(bf16[256,1536]{1,0:T(8,128)(2,1)} %get-tuple-element.217), channel_id=1, source_target_pairs={{0,8},{4,12},{8,0},{12,4},{1,9},{5,13},{9,1},{13,5},{2,10},{6,14},... | collective-permute-start | bytes 2359304 | tf_op jit(solution)/shard_map/ppermute | solution.py:573
  331.0 13.6 %collective-permute-start.52 = (bf16[4,48,640]{2,1,0:T(8,128)(2,1)}, bf16[4,48,640]{2,1,0:T(8,128)(2,1)}, u32[]{:S(2)}, u32[]{:S(2)}) collective-permute-start(bf16[4,48,640]{2,1,0:T(8,128)(2,1)} %get-tuple-element.226), channel_id=1, source_target_pairs={{0,1},{1,2},{2,3},{3,0},{4,5},{5,6},{6,7},{7,4},{8,9},{9,10},{10,1... | collective-permute-start | bytes 737288 | tf_op jit(solution)/shard_map/ppermute | solution.py:630
  332.4 18.6 %collective-permute-start.53 = (bf16[4,48,640]{2,1,0:T(8,128)(2,1)}, bf16[4,48,640]{2,1,0:T(8,128)(2,1)}, u32[]{:S(2)}, u32[]{:S(2)}) collective-permute-start(bf16[4,48,640]{2,1,0:T(8,128)(2,1)} %get-tuple-element.228), channel_id=1, source_target_pairs={{0,2},{1,3},{2,0},{3,1},{4,6},{5,7},{6,4},{7,5},{8,10},{9,11},{10,... | collective-permute-start | bytes 737288 | tf_op jit(solution)/shard_map/ppermute | solution.py:630
  335.2 17.3 %collective-permute-start.54 = (bf16[4,48,640]{2,1,0:T(8,128)(2,1)}, bf16[4,48,640]{2,1,0:T(8,128)(2,1)}, u32[]{:S(2)}, u32[]{:S(2)}) collective-permute-start(bf16[4,48,640]{2,1,0:T(8,128)(2,1)} %get-tuple-element.227), channel_id=1, source_target_pairs={{0,3},{1,0},{2,1},{3,2},{4,7},{5,4},{6,5},{7,6},{8,11},{9,8},{10,9... | collective-permute-start | bytes 737288 | tf_op jit(solution)/shard_map/ppermute | solution.py:630
  340.6 17.7 %collective-permute-start.55 = (bf16[96,1536]{1,0:T(8,128)(2,1)}, bf16[96,1536]{1,0:T(8,128)(2,1)S(1)}, u32[]{:S(2)}, u32[]{:S(2)}) collective-permute-start(bf16[96,1536]{1,0:T(8,128)(2,1)} %reduce-scatter.8.cloned.1.call-done), channel_id=1, source_target_pairs={{0,16},{16,0},{1,17},{17,1},{2,18},{18,2},{3,19},{19,3},{4,20},{20... | collective-permute-start | bytes 884744 | tf_op jit(solution)/shard_map/ppermute | solution.py:573
  344.7 13.7 %collective-permute-start.57 = (f32[9,96]{1,0:T(8,128)S(1)}, f32[9,96]{1,0:T(8,128)S(1)}, u32[]{:S(2)}, u32[]{:S(2)}) collective-permute-start(f32[9,96]{1,0:T(8,128)S(1)} %bitcast.215), channel_id=1, source_target_pairs={{0,8},{4,12},{8,0},{12,4},{1,9},{5,13},{9,1},{13,5},{2,10},{6,14},... | collective-permute-start | bytes 10376 | tf_op jit(solution)/shard_map/ppermute | solution.py:573
  351.0 14.0 %collective-permute-start.61 = (bf16[2,256,768]{2,1,0:T(8,128)(2,1)S(1)}, bf16[2,256,768]{2,1,0:T(8,128)(2,1)S(1)}, u32[]{:S(2)}, u32[]{:S(2)}) collective-permute-start(bf16[2,256,768]{2,1,0:T(8,128)(2,1)S(1)} %fusion.16), channel_id=1, source_target_pairs={{0,8},{4,20},{8,0},{12,28},{16,24},{20,4},{24,16},{28,12},{1,9},{5... | collective-permute-start | bytes 2359304 | tf_op jit(solution)/shard_map/ppermute | solution.py:653
  358.5 6.5 %collective-permute-start.59 = (bf16[48,640]{1,0:T(8,128)(2,1)S(1)}, bf16[48,640]{1,0:T(8,128)(2,1)S(1)}, u32[]{:S(2)}, u32[]{:S(2)}) collective-permute-start(bf16[48,640]{1,0:T(8,128)(2,1)S(1)} %get-tuple-element.238), channel_id=1, source_target_pairs={{0,8},{4,12},{8,0},{12,4},{1,9},{5,13},{9,1},{13,5},{2,10},{6,14},... | collective-permute-start | bytes 184328 | tf_op jit(solution)/shard_map/ppermute | solution.py:573
  359.1 5.9 %collective-permute-start.60 = (bf16[48,640]{1,0:T(8,128)(2,1)S(1)}, bf16[48,640]{1,0:T(8,128)(2,1)S(1)}, u32[]{:S(2)}, u32[]{:S(2)}) collective-permute-start(bf16[48,640]{1,0:T(8,128)(2,1)S(1)} %get-tuple-element.240), channel_id=1, source_target_pairs={{0,12},{4,8},{8,4},{12,0},{1,13},{5,9},{9,5},{13,1},{2,14},{6,10},... | collective-permute-start | bytes 184328 | tf_op jit(solution)/shard_map/ppermute | solution.py:573
  365.1 8.5 %collective-permute-start.66 = (bf16[4,48,640]{2,1,0:T(8,128)(2,1)S(1)}, bf16[4,48,640]{2,1,0:T(8,128)(2,1)}, u32[]{:S(2)}, u32[]{:S(2)}) collective-permute-start(bf16[4,48,640]{2,1,0:T(8,128)(2,1)S(1)} %pad_maximum_fusion.5.near_ref), channel_id=1, source_target_pairs={{0,16},{16,0},{1,17},{17,1},{2,18},{18,2},{3,19},{19,3},{4,20},{20... | collective-permute-start | bytes 737288 | tf_op jit(solution)/shard_map/ppermute | solution.py:573
  367.4 9.9 %collective-permute-start.64 = (bf16[256,768]{1,0:T(8,128)(2,1)}, bf16[256,768]{1,0:T(8,128)(2,1)}, u32[]{:S(2)}, u32[]{:S(2)}) collective-permute-start(bf16[256,768]{1,0:T(8,128)(2,1)} %fusion.20), channel_id=1, source_target_pairs={{0,4},{4,0},{8,12},{12,8},{1,5},{5,1},{9,13},{13,9},{2,6},{6,2},{1... | collective-permute-start | bytes 1179656 | tf_op jit(solution)/shard_map/ppermute | solution.py:573
  (54 other events, 487.5 us)
Sparse Core Ops, SparseCore 0:
  57.4 31.6 all-gather.1
  205.4 61.8 reduce-scatter.3
  269.7 35.3 reduce-scatter.5
  307.2 28.1 reduce-scatter.7
